TPU v7x, 32 devices: a whole 2x2x4 slice. The times are simulated.
32 devices in a mesh: tm: 16 (over z, y, x), blk: 2 (over core).
Axes of the slice: x: 2, y: 2, z: 4, core: 2. Of those that a mesh axis runs over, the one named last changes fastest.
Arguments:
- initial_state: float32 [2, 1024], P(None, 'blk'), may hold values from -6 to 6
- decay_rate: float32 [1024], P('blk'), may hold values from 3.90625e-05 to 0.05
- step_sizes: float32 [2, 256], P(None, 'tm'), may hold values from 0.5 to 130
- increments: float32 [2, 256, 16], P(None, 'tm'), may hold values from -6 to 6
- coupling: float32 [16, 8, 128, 128], P(None, 'blk'), may hold values from -0.013671875 to 0.013671875
- input_weight: float32 [16, 1024], P(None, 'blk'), may hold values from -0.25 to 0.25
- gain: float32 [1024], P('blk'), may hold values from 0.1 to 1.9
- value_weight: bfloat16 [1024, 1024], P(None, 'blk'), may hold values from -0.1875 to 0.1875
- gate_weight: bfloat16 [1024, 1024], P(None, 'blk'), may hold values from -0.1875 to 0.1875
Outputs:
- states: float32 [2, 256, 1024], P(None, 'tm', 'blk')
- readout: bfloat16 [2, 256, 1024], P(None, 'tm', 'blk')
All inputs are finite; a program needn't handle non-finite values.
Results may differ from a plain program's by a relative error of at most 0.0051.
Values may be sent and summed in bfloat16 or wider, within the bound.
No kernel may reach another device: no remote copies, remote signals or barrier semaphores. Data moves between devices by JAX's collectives and lax.ppermute only.
A program may use at most 128 MiB of HBM per device.

v0:
```python
import jax
import jax.numpy as jnp
from jax import lax
from jax.experimental import pallas as pl
from jax.experimental.pallas import tpu as pltpu
from jax.sharding import PartitionSpec as P

QUAD = 4
PAD = 16
EPS = 1e-06
CONTRACT_LAST = (((1,), (1,)), ((), ()))
f32 = jnp.float32
bf16 = jnp.bfloat16
VMEM_SPEC = pl.BlockSpec(memory_space=pltpu.VMEM)
SMEM_SPEC = pl.BlockSpec(memory_space=pltpu.SMEM)
ANY_SPEC = pl.BlockSpec(memory_space=pl.ANY)


def params(mib):
    return pltpu.CompilerParams(vmem_limit_bytes=mib << 20)


def partner(array, axis, flip):
    return lax.ppermute(array, axis, [(i, i ^ flip) for i in range(lax.axis_size(axis))])


def pieces(value):
    high = value.astype(bf16).astype(f32)
    middle = (value - high).astype(bf16).astype(f32)
    low = (value - high - middle).astype(bf16).astype(f32)
    return high, middle, low


def row_of(shape):
    return lax.broadcasted_iota(jnp.int32, shape, 0)


def apply_linear(state, weights):
    high = state.astype(bf16).astype(f32)
    low = state - high
    row = row_of((PAD, state.shape[1]))
    stacked = jnp.where(row == 0, high, jnp.where(row == 1, low, 0.0)).astype(bf16)
    out = jnp.dot(stacked, weights, preferred_element_type=f32)
    return out[0:1] + out[1:2]


def unpack_map(ref, chain, size):
    extra = ref[chain, size : size + PAD, :].astype(f32)
    decay = extra[0:1] + extra[1:2] + extra[2:3]
    offset = extra[3:4] + extra[4:5] + extra[5:6]
    return decay, offset


def apply_map(ref, chain, size, state):
    decay, offset = unpack_map(ref, chain, size)
    return state * decay + apply_linear(state, ref[chain, 0:size, :]) + offset


def store_map(ref, chain, size, panel, decay):
    eye = row_of((size, size)) == lax.broadcasted_iota(jnp.int32, (size, size), 1)
    ref[chain, 0:size, :] = (panel[0:size] - jnp.where(eye, decay, 0.0)).astype(bf16)
    row = row_of((PAD, size))
    extra = jnp.zeros((PAD, size), f32)
    for at, value in enumerate(pieces(decay) + pieces(panel[size : size + 1])):
        extra = jnp.where(row == at, value, extra)
    ref[chain, size : size + PAD, :] = extra.astype(bf16)


def build_maps(
    place_ref,
    near_ref,
    far_ref,
    decay_ref,
    input_ref,
    coupling_ref,
    linear_ref,
    offset_ref,
    fade_ref,
    whole_ref,
    coupling_vmem,
    step_maps,
    panels,
    fades,
    drives,
    running,
    sems,
):
    quarter = place_ref[0]
    channels, _, size, _ = coupling_ref.shape
    chains = coupling_vmem.shape[0]
    steps = near_ref.shape[1]
    total = QUAD * steps
    first_block = (quarter // 2) * chains

    def fetch(chain):
        return pltpu.make_async_copy(
            coupling_ref.at[:, first_block + chain], coupling_vmem.at[chain], sems.at[chain]
        )

    for chain in range(chains):
        fetch(chain).start()
    path = jnp.concatenate([near_ref[0], near_ref[1], far_ref[0], far_ref[1]], axis=0)
    moves = path[:, 0:channels]
    gaps = path[:, channels : channels + 1]
    for chain in range(chains):
        fades[chain] = jnp.exp(-gaps * decay_ref[first_block + chain])
        drives[chain] = jnp.dot(
            moves,
            input_ref[first_block + chain],
            precision=lax.Precision.HIGHEST,
            preferred_element_type=f32,
        )
    rows = total * 8
    lanes = channels * 8
    spread = jnp.broadcast_to(moves[:, None, :], (total, 8, channels)).reshape(rows, channels)
    high = spread.astype(bf16)
    low = (spread - high.astype(f32)).astype(bf16)
    widen = (
        lax.broadcasted_iota(jnp.int32, (channels, lanes), 1) // 8
        == lax.broadcasted_iota(jnp.int32, (channels, lanes), 0)
    )
    widen = jnp.where(widen, 1.0, 0.0).astype(bf16)
    same = row_of((rows, lanes)) % 8 == lax.broadcasted_iota(jnp.int32, (rows, lanes), 1) % 8
    left = jnp.concatenate(
        [
            jnp.where(same, jnp.dot(part, widen, preferred_element_type=f32), 0.0).astype(bf16)
            for part in (high, low)
        ],
        axis=1,
    )
    eye = row_of((size, size)) == lax.broadcasted_iota(jnp.int32, (size, size), 1)
    for chain in range(chains):
        fetch(chain).wait()

        @pl.loop(0, size // PAD)
        def _(tile):
            at = pl.multiple_of(tile * PAD, PAD)
            tiles = [
                coupling_vmem[chain, :, pl.ds(at + half, 8), :].reshape(lanes, size).astype(bf16)
                for half in (0, 8)
            ]
            right = jnp.concatenate(tiles, axis=1)
            right = jnp.concatenate([right, right], axis=0)
            made = jnp.dot(left, right, preferred_element_type=f32)
            halves = [made[:, 0:size].reshape(total, 8, size), made[:, size:].reshape(total, 8, size)]
            step_maps[chain, :, pl.ds(at, PAD), :] = jnp.concatenate(halves, axis=1).astype(bf16)

        for slot in range(QUAD):
            panels[chain, slot, 0:size, :] = jnp.where(eye, 1.0, 0.0)
            panels[chain, slot, size : size + PAD, :] = jnp.zeros((PAD, size), f32)
            running[chain, slot] = jnp.ones((1, size), f32)

    @pl.loop(0, steps)
    def _(step):
        for chain in range(chains):
            for slot in range(QUAD):
                at = slot * steps + step
                panel = panels[chain, slot]
                fade = fades[chain, pl.ds(at, 1), :]
                drive = drives[chain, pl.ds(at, 1), :]
                pushed = lax.dot_general(
                    panel.astype(bf16),
                    step_maps[chain, at],
                    CONTRACT_LAST,
                    preferred_element_type=f32,
                )
                moved = panel * fade + pushed
                matrix = moved[0:size]
                offset = moved[size:] + drive
                panels[chain, slot, 0:size, :] = matrix
                panels[chain, slot, size : size + PAD, :] = offset
                decay = running[chain, slot] * fade
                running[chain, slot] = decay
                linear_ref[chain, slot, step] = (matrix - jnp.where(eye, decay, 0.0)).astype(bf16)
                offset_ref[chain, slot, pl.ds(step, 1), :] = offset[0:1]
                fade_ref[chain, slot, pl.ds(step, 1), :] = decay

    for chain in range(chains):
        panel = panels[chain, quarter]
        decay = running[chain, quarter]
        for order in range(1, QUAD):
            slot = order ^ quarter
            late = running[chain, slot]
            pushed = jnp.dot(
                panel.astype(bf16), linear_ref[chain, slot, steps - 1], preferred_element_type=f32
            )
            moved = panel * late + pushed
            panel = jnp.concatenate(
                [moved[0:size], moved[size:] + panels[chain, slot, size : size + 1, :]], axis=0
            )
            decay = decay * late
        store_map(whole_ref, chain, size, panel, decay)


def join_maps(place_ref, own_ref, other_ref, out_ref):
    size = own_ref.shape[2]

    def join(early, late):
        for chain in range(own_ref.shape[0]):
            decay, offset = unpack_map(early, chain, size)
            eye = row_of((size, size)) == lax.broadcasted_iota(jnp.int32, (size, size), 1)
            matrix = early[chain, 0:size, :].astype(f32) + jnp.where(eye, decay, 0.0)
            panel = jnp.concatenate([matrix, jnp.broadcast_to(offset, (PAD, size))], axis=0)
            late_decay, late_offset = unpack_map(late, chain, size)
            moved = panel * late_decay + jnp.dot(
                panel.astype(bf16), late[chain, 0:size, :], preferred_element_type=f32
            )
            panel = jnp.concatenate([moved[0:size], moved[size:] + late_offset], axis=0)
            store_map(out_ref, chain, size, panel, decay * late_decay)

    @pl.when(place_ref[0] == 0)
    def _():
        join(own_ref, other_ref)

    @pl.when(place_ref[0] != 0)
    def _():
        join(other_ref, own_ref)


def cross_pair(place_ref, own_ref, other_ref, start_ref, out_ref):
    size = own_ref.shape[2]
    chains = own_ref.shape[0]

    def cross(early, late):
        for chain in range(chains):
            state = start_ref[place_ref[1] + chain]
            state = apply_map(early, chain, size, state)
            out_ref[chain] = apply_map(late, chain, size, state)

    @pl.when(place_ref[0] == 0)
    def _():
        cross(own_ref, other_ref)

    @pl.when(place_ref[0] != 0)
    def _():
        cross(other_ref, own_ref)


def run_steps(place_ref, start_ref, base_ref, *refs):
    level_refs = refs[:-7]
    linear_ref, offset_ref, fade_ref, keep_ref, across_ref, later_ref, entries = refs[-7:]
    chains, _, steps, size, _ = linear_ref.shape
    quarter = place_ref[0]
    for chain in range(chains):
        entries[chain, 0] = start_ref[place_ref[1] + chain]

    @pl.when(place_ref[2] != 0)
    def _():
        for chain in range(chains):
            entries[chain, 0] = base_ref[chain]

    for level, ref in reversed(list(enumerate(level_refs))):

        @pl.when(place_ref[3 + level] != 0)
        def _():
            for chain in range(chains):
                entries[chain, 0] = apply_map(ref, chain, size, entries[chain, 0])

    states = [entries[chain, 0] for chain in range(chains)]
    for order in range(QUAD):
        slot = order ^ quarter
        for chain in range(chains):
            entries[chain, slot] = states[chain]
            if order + 1 < QUAD:
                states[chain] = (
                    states[chain] * fade_ref[chain, slot, steps - 1 : steps, :]
                    + apply_linear(states[chain], linear_ref[chain, slot, steps - 1])
                    + offset_ref[chain, slot, steps - 1 : steps, :]
                )
    targets = {0: (keep_ref, 0), 1: (across_ref, 0), 2: (later_ref, 0), 3: (across_ref, 1)}
    row = row_of((steps, size))
    for slot in range(QUAD):
        target, place = targets[slot]
        for chain in range(chains):
            entry = entries[chain, slot]
            same = jnp.broadcast_to(entry, (PAD, size)).astype(bf16)
            gathered = entry * fade_ref[chain, slot] + offset_ref[chain, slot]
            for step in range(0, steps, 2):
                pair = jnp.concatenate(
                    [linear_ref[chain, slot, step], linear_ref[chain, slot, step + 1]], axis=1
                )
                out = jnp.dot(same, pair, preferred_element_type=f32)
                for half in range(2):
                    part = jnp.broadcast_to(out[0:1, half * size : (half + 1) * size], (steps, size))
                    gathered = gathered + jnp.where(row == step + half, part, 0.0)
            target[place, chain] = gathered


def scale_states(
    place_ref, keep_ref, across_ref, later_ref, gain_ref, states_ref, packed_ref, table
):
    records, steps, units = states_ref.shape
    chains = keep_ref.shape[1]
    size = keep_ref.shape[3]
    record = place_ref[0] % 2
    half = place_ref[0] // 2
    for chain in range(chains):
        here = half * chains + chain
        there = (1 - half) * chains + chain
        table[record, here] = keep_ref[0, chain]
        table[1 - record, here] = across_ref[0, chain]
        table[record, there] = later_ref[0, chain]
        table[1 - record, there] = later_ref[1, chain]
    for index in range(records):
        squares = jnp.zeros((steps, 1), f32)
        for block in range(units // size):
            at = block * size
            value = table[index, block]
            states_ref[index, :, at : at + size] = value
            packed_ref[index * steps : (index + 1) * steps, at : at + size] = (
                value * gain_ref[:, at : at + size]
            ).astype(bf16)
            squares = squares + jnp.sum(value * value, axis=1, keepdims=True)
        lane = lax.broadcasted_iota(jnp.int32, (steps, size), 1)
        extra = jnp.zeros((steps, size), f32)
        for at, value in enumerate(pieces(squares)):
            extra = jnp.where(lane == at, value, extra)
        packed_ref[index * steps : (index + 1) * steps, units : units + size] = extra.astype(bf16)


def read_out(place_ref, own_ref, other_ref, value_ref, gate_ref, out_ref):
    units = value_ref.shape[0] // 2
    own_at = pl.multiple_of(place_ref[0] * units, units)
    other_at = pl.multiple_of((1 - place_ref[0]) * units, units)
    own = own_ref[:, 0:units]
    other = other_ref[:, 0:units]
    squares = jnp.sum(
        own_ref[:, units:].astype(f32) + other_ref[:, units:].astype(f32), axis=1, keepdims=True
    )
    inverse = lax.rsqrt(squares / value_ref.shape[0] + EPS)

    def project(ref):
        return jnp.dot(own, ref[pl.ds(own_at, units), :], preferred_element_type=f32) + jnp.dot(
            other, ref[pl.ds(other_at, units), :], preferred_element_type=f32
        )

    value = project(value_ref) * inverse
    gate = project(gate_ref) * inverse
    out_ref[...] = (value * jax.nn.sigmoid(gate)).astype(bf16)


def body(
    initial_state,
    decay_rate,
    step_sizes,
    increments,
    coupling,
    input_weight,
    gain,
    value_weight,
    gate_weight,
):
    records, local_units = initial_state.shape
    channels, local_blocks, size, _ = coupling.shape
    steps = step_sizes.shape[1]
    devices = lax.axis_size("tm")
    bits = devices.bit_length() - 1
    chains = records * local_blocks // QUAD
    assert devices == 1 << bits and bits >= 4 and records == 2
    place = lax.axis_index("tm")
    quarter = place % QUAD
    record = quarter % 2
    first_chain = record * local_blocks + (quarter // 2) * chains

    path = jnp.concatenate([increments, step_sizes[:, :, None]], axis=2)
    mine = lax.dynamic_index_in_dim(path, record, 0, keepdims=False)
    theirs = lax.dynamic_index_in_dim(path, 1 - record, 0, keepdims=False)
    near = jnp.stack([mine, partner(theirs, "tm", 1)])
    far = partner(near, "tm", 2)

    total = QUAD * steps
    linear, offset, fade, whole = pl.pallas_call(
        build_maps,
        out_shape=(
            jax.ShapeDtypeStruct((chains, QUAD, steps, size, size), bf16),
            jax.ShapeDtypeStruct((chains, QUAD, steps, size), f32),
            jax.ShapeDtypeStruct((chains, QUAD, steps, size), f32),
            jax.ShapeDtypeStruct((chains, size + PAD, size), bf16),
        ),
        in_specs=[SMEM_SPEC] + [VMEM_SPEC] * 4 + [ANY_SPEC],
        out_specs=(VMEM_SPEC,) * 4,
        scratch_shapes=[
            pltpu.VMEM((chains, channels, size, size), f32),
            pltpu.VMEM((chains, total, size, size), bf16),
            pltpu.VMEM((chains, QUAD, size + PAD, size), f32),
            pltpu.VMEM((chains, total, size), f32),
            pltpu.VMEM((chains, total, size), f32),
            pltpu.VMEM((chains, QUAD, 1, size), f32),
            pltpu.SemaphoreType.DMA((chains,)),
        ],
        compiler_params=params(32),
        name="build_maps",
    )(
        jnp.stack([quarter]),
        near,
        far,
        decay_rate.reshape(local_blocks, 1, size),
        jnp.transpose(input_weight.reshape(channels, local_blocks, size), (1, 0, 2)),
        coupling,
    )

    start = initial_state.reshape(records * local_blocks, 1, size)
    earlier = []
    sides = []
    for level in range(2, bits - 1):
        other = partner(whole, "tm", 1 << level)
        side = (place >> level) % 2
        sides.append(side)
        earlier.append(other)
        if level + 1 < bits - 1:
            whole = pl.pallas_call(
                join_maps,
                out_shape=jax.ShapeDtypeStruct(whole.shape, bf16),
                in_specs=[SMEM_SPEC] + [VMEM_SPEC] * 2,
                out_specs=VMEM_SPEC,
                compiler_params=params(16),
                name="join_maps",
            )(jnp.stack([side]), whole, other)
    crossed = pl.pallas_call(
        cross_pair,
        out_shape=jax.ShapeDtypeStruct((chains, 1, size), f32),
        in_specs=[SMEM_SPEC] + [VMEM_SPEC] * 3,
        out_specs=VMEM_SPEC,
        compiler_params=params(16),
        name="cross_pair",
    )(jnp.stack([sides[-1], first_chain]), whole, earlier[-1], start)
    base = partner(crossed, "tm", 1 << (bits - 1))

    piece = (chains, steps, size)
    keep, across, later = pl.pallas_call(
        run_steps,
        out_shape=(
            jax.ShapeDtypeStruct((1,) + piece, f32),
            jax.ShapeDtypeStruct((2,) + piece, f32),
            jax.ShapeDtypeStruct((1,) + piece, f32),
        ),
        in_specs=[SMEM_SPEC] + [VMEM_SPEC] * (5 + len(earlier)),
        out_specs=(VMEM_SPEC,) * 3,
        scratch_shapes=[pltpu.VMEM((chains, QUAD, 1, size), f32)],
        compiler_params=params(16),
        name="run_steps",
    )(
        jnp.stack([quarter, first_chain, place >> (bits - 1)] + sides),
        start,
        base,
        *earlier,
        linear,
        offset,
        fade,
    )
    across = partner(across, "tm", 1)
    later = partner(jnp.concatenate([later, across[1:2]], axis=0), "tm", 2)

    rows = records * steps
    states, packed = pl.pallas_call(
        scale_states,
        out_shape=(
            jax.ShapeDtypeStruct((records, steps, local_units), f32),
            jax.ShapeDtypeStruct((rows, local_units + size), bf16),
        ),
        in_specs=[SMEM_SPEC] + [VMEM_SPEC] * 4,
        out_specs=(VMEM_SPEC,) * 2,
        scratch_shapes=[pltpu.VMEM((records, local_blocks, steps, size), f32)],
        compiler_params=params(16),
        name="scale_states",
    )(jnp.stack([quarter]), keep, across, later, gain.reshape(1, local_units))
    packed_other = partner(packed, "blk", 1)
    features = value_weight.shape[1]
    readout = pl.pallas_call(
        read_out,
        out_shape=jax.ShapeDtypeStruct((rows, features), bf16),
        in_specs=[SMEM_SPEC] + [VMEM_SPEC] * 4,
        out_specs=VMEM_SPEC,
        compiler_params=params(16),
        name="read_out",
    )(jnp.stack([lax.axis_index("blk")]), packed, packed_other, value_weight, gate_weight)
    return (states, readout.reshape(records, steps, features))


def solution(mesh):
    placed = (
        P(None, "blk"),
        P("blk"),
        P(None, "tm"),
        P(None, "tm", None),
        P(None, "blk", None, None),
        P(None, "blk"),
        P("blk"),
        P(None, "blk"),
        P(None, "blk"),
    )
    return jax.shard_map(
        body,
        mesh=mesh,
        in_specs=placed,
        out_specs=(P(None, "tm", "blk"), P(None, "tm", "blk")),
        check_vma=False,
    )
```

profile of v0, /device:TPU:0, one launch (start us, length us, event | category | flops | bytes accessed | tf_op | source)
XLA Modules:
  0.0 45.8 jit_solution(11219067367180670763)
XLA Ops:
  0.6 0.0 copy-start
  0.7 0.8 %copy.12 = f32[2,16,1]{2,1,0:T(8,128)S(1)} copy(f32[2,16,1]{1,0,2:T(2,128)} %bitcast.23) | data formatting | bytes 256 | tf_op jit(solution)/shard_map/broadcast_in_dim | solution.py:365
  1.4 0.8 %fusion.2 = (f32[1,16,17]{2,1,0:T(8,128)S(1)}, f32[16,17]{1,0:T(8,128)S(1)}) fusion(s32[]{:T(128)S(6)} %select_n.30, f32[2,16,16]{2,1,0:T(8,128)} %param.12, f32[2,16,1]{2,1,0:T(8,128)S(1)} %copy.12, s32[]{:T(128)S(6)} %select_n.31), kind=kLoop, calls=%fused_computation.9 | loop fusion | flops 544 | bytes 4360 | tf_op jit(solution)/shard_map/concatenate | solution.py:365
  2.2 3.0 %collective-permute-start = (f32[16,17]{1,0:T(8,128)S(1)}, f32[16,17]{1,0:T(8,128)S(1)}, u32[]{:S(2)}, u32[]{:S(2)}) collective-permute-start(f32[16,17]{1,0:T(8,128)S(1)} %get-tuple-element.21), channel_id=1, source_target_pairs={{0,2},{2,0},{4,6},{6,4},{8,10},{10,8},{12,14},{14,12},{16,18},{18,... | collective-permute-start | bytes 3272 | tf_op jit(solution)/shard_map/ppermute | solution.py:24
  5.2 1.6 %collective-permute-done = f32[16,17]{1,0:T(8,128)S(1)} collective-permute-done((f32[16,17]{1,0:T(8,128)S(1)}, f32[16,17]{1,0:T(8,128)S(1)}, u32[]{:S(2)}, u32[]{:S(2)}) %collective-permute-start) | collective-permute-done | bytes 1120 | tf_op jit(solution)/shard_map/ppermute | solution.py:24
  6.8 2.0 %collective-permute-start.1 = (f32[2,16,17]{2,1,0:T(8,128)S(1)}, f32[2,16,17]{2,1,0:T(8,128)S(1)}, u32[]{:S(2)}, u32[]{:S(2)}) collective-permute-start(f32[2,16,17]{2,1,0:T(8,128)S(1)} %pad_maximum_fusion.1.near_ref), channel_id=1, source_target_pairs={{0,4},{2,6},{4,0},{6,2},{8,12},{10,14},{12,8},{14,10},{16,20},{18,... | collective-permute-start | bytes 6536 | tf_op jit(solution)/shard_map/ppermute | solution.py:24
  8.9 0.0 copy-done
  8.9 0.7 %reshape.19.start_ref = f32[8,1,128]{2,1,0:T(1,128)S(1)} reshape(f32[2,512]{1,0:T(2,128)} %param.9) | data formatting | bytes 8192 | tf_op jit(solution)/shard_map/reshape | solution.py:402
  9.6 1.0 %collective-permute-done.1.far_ref = f32[2,16,17]{2,1,0:T(8,128)S(1)} collective-permute-done((f32[2,16,17]{2,1,0:T(8,128)S(1)}, f32[2,16,17]{2,1,0:T(8,128)S(1)}, u32[]{:S(2)}, u32[]{:S(2)}) %collective-permute-start.1) | collective-permute-done | bytes 2208 | tf_op jit(solution)/shard_map/ppermute | solution.py:24
  10.6 0.0 copy-start.1
  10.6 2.2 %copy-done.1 = f32[16,4,128,128]{3,2,1,0:T(8,128)S(1)} copy-done((f32[16,4,128,128]{3,2,1,0:T(8,128)S(1)}, f32[16,4,128,128]{3,2,1,0:T(8,128)}, u32[]{:S(2)}) %copy-start.1) | copy-done | bytes 4194328
  12.8 0.0 copy-start.4
  12.8 0.7 %copy-done.4 = f32[512]{0:T(512)S(1)} copy-done((f32[512]{0:T(512)S(1)}, f32[512]{0:T(512)}, u32[]{:S(2)}) %copy-start.4) | copy-done | bytes 2072
  13.5 0.0 copy-start.5
  13.5 0.0 copy-start.2
  13.5 0.0 copy-start.3
  13.5 10.0 %build_maps.1 = (bf16[2,4,16,128,128]{4,3,2,1,0:T(8,128)(2,1)S(1)}, f32[2,4,16,128]{3,2,1,0:T(8,128)S(1)}, f32[2,4,16,128]{3,2,1,0:T(8,128)S(1)}, bf16[2,144,128]{2,1,0:T(8,128)(2,1)S(1)}) custom-call(s32[1]{0:T(128)} %bitcast.place_ref, f32[2,16,17]{2,1,0:T(8,128)S(1)} %pad_maximum_fusion.1.near_ref, f32[2,16,17]{2,1,0:T(8,128)S(1)} %collective-permute-done.1.far_ref, ...), custom_call_target="tpu_custom_call" | custom-call | tf_op jit(solution)/shard_map/build_maps/pallas_call | solution.py:372
  23.5 2.1 %collective-permute-start.2 = (bf16[2,144,128]{2,1,0:T(8,128)(2,1)S(1)}, bf16[2,144,128]{2,1,0:T(8,128)(2,1)S(1)}, u32[]{:S(2)}, u32[]{:S(2)}) collective-permute-start(bf16[2,144,128]{2,1,0:T(8,128)(2,1)S(1)} %get-tuple-element.11.own_ref), channel_id=1, source_target_pairs={{0,8},{2,10},{4,12},{6,14},{8,0},{10,2},{12,4},{14,6},{16,24},{18,... | collective-permute-start | bytes 221192 | tf_op jit(solution)/shard_map/ppermute | solution.py:24
  25.6 0.1 pad_add_fusion.1.place_ref
  25.7 2.3 %collective-permute-done.2.other_ref.refs_0_ = bf16[2,144,128]{2,1,0:T(8,128)(2,1)S(1)} collective-permute-done((bf16[2,144,128]{2,1,0:T(8,128)(2,1)S(1)}, bf16[2,144,128]{2,1,0:T(8,128)(2,1)S(1)}, u32[]{:S(2)}, u32[]{:S(2)}) %collective-permute-start.2) | collective-permute-done | bytes 73760 | tf_op jit(solution)/shard_map/ppermute | solution.py:24
  27.9 0.8 %cross_pair.1 = f32[2,1,128]{2,1,0:T(1,128)S(1)} custom-call(s32[2]{0:T(128)S(1)} %pad_add_fusion.1.place_ref, bf16[2,144,128]{2,1,0:T(8,128)(2,1)S(1)} %get-tuple-element.11.own_ref, bf16[2,144,128]{2,1,0:T(8,128)(2,1)S(1)} %collective-permute-done.2.other_ref.refs_0_, f32[8,1,128]{2,1,0:T(1,128)S(1)} %reshape.19.start_ref), custom_call_target="tpu_custom_call" | custom-call | tf_op jit(solution)/shard_map/cross_pair/pallas_call | solution.py:419
  28.7 3.0 %collective-permute-start.3 = (f32[2,1,128]{2,1,0:T(1,128)S(1)}, f32[2,1,128]{2,1,0:T(1,128)S(1)}, u32[]{:S(2)}, u32[]{:S(2)}) collective-permute-start(f32[2,1,128]{2,1,0:T(1,128)S(1)} %cross_pair.1), channel_id=1, source_target_pairs={{0,16},{2,18},{4,20},{6,22},{8,24},{10,26},{12,28},{14,30},{16,0},... | collective-permute-start | bytes 3080 | tf_op jit(solution)/shard_map/ppermute | solution.py:24
  31.8 0.1 pad_add_fusion.place_ref
  31.9 1.5 %collective-permute-done.3.base_ref = f32[2,1,128]{2,1,0:T(1,128)S(1)} collective-permute-done((f32[2,1,128]{2,1,0:T(1,128)S(1)}, f32[2,1,128]{2,1,0:T(1,128)S(1)}, u32[]{:S(2)}, u32[]{:S(2)}) %collective-permute-start.3) | collective-permute-done | bytes 1056 | tf_op jit(solution)/shard_map/ppermute | solution.py:24
  33.3 1.6 %run_steps.1 = (f32[1,2,16,128]{3,2,1,0:T(8,128)S(1)}, f32[2,2,16,128]{3,2,1,0:T(8,128)S(1)}, f32[1,2,16,128]{3,2,1,0:T(8,128)S(1)}) custom-call(s32[4]{0:T(128)S(1)} %pad_add_fusion.place_ref, f32[8,1,128]{2,1,0:T(1,128)S(1)} %reshape.19.start_ref, f32[2,1,128]{2,1,0:T(1,128)S(1)} %collective-permute-done.3.base_ref, ...), custom_call_target="tpu_custom_call" | custom-call | tf_op jit(solution)/shard_map/run_steps/pallas_call | solution.py:430
  34.9 1.9 %collective-permute-start.4 = (f32[2,2,16,128]{3,2,1,0:T(8,128)S(1)}, f32[2,2,16,128]{3,2,1,0:T(8,128)S(1)}, u32[]{:S(2)}, u32[]{:S(2)}) collective-permute-start(f32[2,2,16,128]{3,2,1,0:T(8,128)S(1)} %get-tuple-element.16), channel_id=1, source_target_pairs={{0,2},{2,0},{4,6},{6,4},{8,10},{10,8},{12,14},{14,12},{16,18},{18,... | collective-permute-start | bytes 98312 | tf_op jit(solution)/shard_map/ppermute | solution.py:24
  36.8 2.1 %collective-permute-done.4.across_ref = f32[2,2,16,128]{3,2,1,0:T(8,128)S(1)} collective-permute-done((f32[2,2,16,128]{3,2,1,0:T(8,128)S(1)}, f32[2,2,16,128]{3,2,1,0:T(8,128)S(1)}, u32[]{:S(2)}, u32[]{:S(2)}) %collective-permute-start.4) | collective-permute-done | bytes 32800 | tf_op jit(solution)/shard_map/ppermute | solution.py:24
  38.9 1.9 %collective-permute-start.5 = (f32[2,2,16,128]{3,2,1,0:T(8,128)S(1)}, f32[2,2,16,128]{3,2,1,0:T(8,128)S(1)}, u32[]{:S(2)}, u32[]{:S(2)}) collective-permute-start(f32[2,2,16,128]{3,2,1,0:T(8,128)S(1)} %pad_maximum_fusion), channel_id=1, source_target_pairs={{0,4},{2,6},{4,0},{6,2},{8,12},{10,14},{12,8},{14,10},{16,20},{18,... | collective-permute-start | bytes 98312 | tf_op jit(solution)/shard_map/ppermute | solution.py:24
  40.8 2.1 %collective-permute-done.5.later_ref = f32[2,2,16,128]{3,2,1,0:T(8,128)S(1)} collective-permute-done((f32[2,2,16,128]{3,2,1,0:T(8,128)S(1)}, f32[2,2,16,128]{3,2,1,0:T(8,128)S(1)}, u32[]{:S(2)}, u32[]{:S(2)}) %collective-permute-start.5) | collective-permute-done | bytes 32800 | tf_op jit(solution)/shard_map/ppermute | solution.py:24
  42.8 0.0 copy-done.5
  42.8 0.7 %scale_states.1 = (f32[2,16,512]{2,1,0:T(8,128)}, bf16[32,640]{1,0:T(8,128)(2,1)S(1)}) custom-call(s32[1]{0:T(128)} %bitcast.place_ref, f32[1,2,16,128]{3,2,1,0:T(8,128)S(1)} %get-tuple-element.15.keep_ref, f32[2,2,16,128]{3,2,1,0:T(8,128)S(1)} %collective-permute-done.4.across_ref, f32[2,2,16,128]{3,2,1,0:T(8,128)S(1)} %collective-permute-done.5.later_ref, ...), custom_call_target="tpu_custom_call" | custom-call | tf_op jit(solution)/shard_map/scale_states/pallas_call | solution.py:455
  43.5 0.0 collective-permute-start.6
  43.5 1.2 %collective-permute-done.6.other_ref = bf16[32,640]{1,0:T(8,128)(2,1)S(1)} collective-permute-done((bf16[32,640]{1,0:T(8,128)(2,1)S(1)}, bf16[32,640]{1,0:T(8,128)(2,1)S(1)}, u32[]{:S(2)}, u32[]{:S(2)}) %collective-permute-start.6) | collective-permute-done | bytes 40992 | tf_op jit(solution)/shard_map/ppermute | solution.py:24
  44.7 0.0 copy-done.2
  44.7 0.0 copy-done.3
  44.7 1.1 %read_out.1 = bf16[32,512]{1,0:T(8,128)(2,1)} custom-call(s32[1]{0:T(128)} %bitcast.10.place_ref, bf16[32,640]{1,0:T(8,128)(2,1)S(1)} %get-tuple-element.19.own_ref, bf16[32,640]{1,0:T(8,128)(2,1)S(1)} %collective-permute-done.6.other_ref, bf16[1024,512]{1,0:T(8,128)(2,1)S(1)} %copy-done.2, bf16[1024,512]{1,0:T(8,128)(2,1)S(1)} %copy-done.3), custom_call_target="tpu_custom_call" | custom-call | tf_op jit(solution)/shard_map/read_out/pallas_call | solution.py:469
  (4 shorter events, 0.0 us)
Async XLA Ops:
  0.6 8.3 %copy-start = (f32[16,512]{1,0:T(8,128)S(1)}, f32[16,512]{1,0:T(8,128)}, u32[]{:S(2)}) copy-start(f32[16,512]{1,0:T(8,128)} %param.14) | copy-start | bytes 98308
  2.2 4.6 %collective-permute-start = (f32[16,17]{1,0:T(8,128)S(1)}, f32[16,17]{1,0:T(8,128)S(1)}, u32[]{:S(2)}, u32[]{:S(2)}) collective-permute-start(f32[16,17]{1,0:T(8,128)S(1)} %get-tuple-element.21), channel_id=1, source_target_pairs={{0,2},{2,0},{4,6},{6,4},{8,10},{10,8},{12,14},{14,12},{16,18},{18,... | collective-permute-start | bytes 3272 | tf_op jit(solution)/shard_map/ppermute | solution.py:24
  6.8 3.8 %collective-permute-start.1 = (f32[2,16,17]{2,1,0:T(8,128)S(1)}, f32[2,16,17]{2,1,0:T(8,128)S(1)}, u32[]{:S(2)}, u32[]{:S(2)}) collective-permute-start(f32[2,16,17]{2,1,0:T(8,128)S(1)} %pad_maximum_fusion.1.near_ref), channel_id=1, source_target_pairs={{0,4},{2,6},{4,0},{6,2},{8,12},{10,14},{12,8},{14,10},{16,20},{18,... | collective-permute-start | bytes 6536 | tf_op jit(solution)/shard_map/ppermute | solution.py:24
  10.6 2.2 %copy-start.1 = (f32[16,4,128,128]{3,2,1,0:T(8,128)S(1)}, f32[16,4,128,128]{3,2,1,0:T(8,128)}, u32[]{:S(2)}) copy-start(f32[16,4,128,128]{3,2,1,0:T(8,128)} %coupling_ref.1) | copy-start | bytes 12582916
  12.8 0.7 %copy-start.4 = (f32[512]{0:T(512)S(1)}, f32[512]{0:T(512)}, u32[]{:S(2)}) copy-start(f32[512]{0:T(512)} %param.10) | copy-start | bytes 6148
  13.5 29.3 %copy-start.5 = (f32[512]{0:T(512)S(1)}, f32[512]{0:T(512)}, u32[]{:S(2)}) copy-start(f32[512]{0:T(512)} %param.15) | copy-start | bytes 6148
  13.5 31.2 %copy-start.2 = (bf16[1024,512]{1,0:T(8,128)(2,1)S(1)}, bf16[1024,512]{1,0:T(8,128)(2,1)}, u32[]{:S(2)}) copy-start(bf16[1024,512]{1,0:T(8,128)(2,1)} %value_ref.1) | copy-start | bytes 3145732
  13.5 31.2 %copy-start.3 = (bf16[1024,512]{1,0:T(8,128)(2,1)S(1)}, bf16[1024,512]{1,0:T(8,128)(2,1)}, u32[]{:S(2)}) copy-start(bf16[1024,512]{1,0:T(8,128)(2,1)} %gate_ref.1) | copy-start | bytes 3145732
  23.5 4.5 %collective-permute-start.2 = (bf16[2,144,128]{2,1,0:T(8,128)(2,1)S(1)}, bf16[2,144,128]{2,1,0:T(8,128)(2,1)S(1)}, u32[]{:S(2)}, u32[]{:S(2)}) collective-permute-start(bf16[2,144,128]{2,1,0:T(8,128)(2,1)S(1)} %get-tuple-element.11.own_ref), channel_id=1, source_target_pairs={{0,8},{2,10},{4,12},{6,14},{8,0},{10,2},{12,4},{14,6},{16,24},{18,... | collective-permute-start | bytes 221192 | tf_op jit(solution)/shard_map/ppermute | solution.py:24
  28.7 4.6 %collective-permute-start.3 = (f32[2,1,128]{2,1,0:T(1,128)S(1)}, f32[2,1,128]{2,1,0:T(1,128)S(1)}, u32[]{:S(2)}, u32[]{:S(2)}) collective-permute-start(f32[2,1,128]{2,1,0:T(1,128)S(1)} %cross_pair.1), channel_id=1, source_target_pairs={{0,16},{2,18},{4,20},{6,22},{8,24},{10,26},{12,28},{14,30},{16,0},... | collective-permute-start | bytes 3080 | tf_op jit(solution)/shard_map/ppermute | solution.py:24
  34.9 4.0 %collective-permute-start.4 = (f32[2,2,16,128]{3,2,1,0:T(8,128)S(1)}, f32[2,2,16,128]{3,2,1,0:T(8,128)S(1)}, u32[]{:S(2)}, u32[]{:S(2)}) collective-permute-start(f32[2,2,16,128]{3,2,1,0:T(8,128)S(1)} %get-tuple-element.16), channel_id=1, source_target_pairs={{0,2},{2,0},{4,6},{6,4},{8,10},{10,8},{12,14},{14,12},{16,18},{18,... | collective-permute-start | bytes 98312 | tf_op jit(solution)/shard_map/ppermute | solution.py:24
  38.9 3.9 %collective-permute-start.5 = (f32[2,2,16,128]{3,2,1,0:T(8,128)S(1)}, f32[2,2,16,128]{3,2,1,0:T(8,128)S(1)}, u32[]{:S(2)}, u32[]{:S(2)}) collective-permute-start(f32[2,2,16,128]{3,2,1,0:T(8,128)S(1)} %pad_maximum_fusion), channel_id=1, source_target_pairs={{0,4},{2,6},{4,0},{6,2},{8,12},{10,14},{12,8},{14,10},{16,20},{18,... | collective-permute-start | bytes 98312 | tf_op jit(solution)/shard_map/ppermute | solution.py:24
  43.5 1.2 %collective-permute-start.6 = (bf16[32,640]{1,0:T(8,128)(2,1)S(1)}, bf16[32,640]{1,0:T(8,128)(2,1)S(1)}, u32[]{:S(2)}, u32[]{:S(2)}) collective-permute-start(bf16[32,640]{1,0:T(8,128)(2,1)S(1)} %get-tuple-element.19.own_ref), channel_id=1, source_target_pairs={{0,1},{1,0},{2,3},{3,2},{4,5},{5,4},{6,7},{7,6},{8,9},{9,8},{10,11... | collective-permute-start | bytes 122888 | tf_op jit(solution)/shard_map/ppermute | solution.py:24
where the time goes:
time: 46.1 us; the launch traced here: 45.8 us
  Pallas kernels  14.1 us (31%)
  starting transfers between devices  13.9 us (30%)
  waiting for transfers between devices  11.7 us (25%)
  local copies, waits for them, and re-layouts  4.36 us (9%)
  other arithmetic  0.95 us (2%)
  between operations  0.71 us (2%)
    ppermute x7, starting transfers between devices, partner(): lax.ppermute(array, axis, [(i, i ^ flip) for i in range(lax.axis_size(axi...  13.9 us
    ppermute x7, waiting for transfers between devices, partner(): lax.ppermute(array, axis, [(i, i ^ flip) for i in range(lax.axis_size(axi...  11.7 us
    pallas_call x1, Pallas kernels, body(): pl.pallas_call(build_maps, out_shape=(jax.ShapeDtypeStruct((chains, QUAD,...  9.97 us
    unnamed x12, local copies, waits for them, and re-layouts  2.89 us
    pallas_call x1, Pallas kernels, body(): pl.pallas_call(run_steps, out_shape=(jax.ShapeDtypeStruct((1,) + piece, f...  1.58 us
    pallas_call x1, Pallas kernels, body(): pl.pallas_call(read_out, out_shape=jax.ShapeDtypeStruct((rows, features),...  1.1 us
  transfers between devices with their start and end apart: 7, of which 7 were waited for; matrix products, arithmetic and copies ran while one was open for 2% of the time, Pallas kernels for 0%

commit v1 on v0

--- a/solution.py
+++ b/solution.py
@@ -1,3 +1,5 @@
+import functools
+
 import jax
 import jax.numpy as jnp
 from jax import lax
@@ -8,12 +10,13 @@
 QUAD = 4
 PAD = 16
 EPS = 1e-06
+FORM_UNROLL = 4
+STEP_UNROLL = 4
 CONTRACT_LAST = (((1,), (1,)), ((), ()))
 f32 = jnp.float32
 bf16 = jnp.bfloat16
 VMEM_SPEC = pl.BlockSpec(memory_space=pltpu.VMEM)
-SMEM_SPEC = pl.BlockSpec(memory_space=pltpu.SMEM)
-ANY_SPEC = pl.BlockSpec(memory_space=pl.ANY)
+HBM_SPEC = pl.BlockSpec(memory_space=pltpu.HBM)
 
 
 def params(mib):
@@ -29,6 +32,14 @@
     middle = (value - high).astype(bf16).astype(f32)
     low = (value - high - middle).astype(bf16).astype(f32)
     return high, middle, low
+
+
+def corner_of_quad():
+    return lax.axis_index("tm") & (QUAD - 1)
+
+
+def bit_of(level):
+    return (lax.axis_index("tm") >> level) & 1
 
 
 def row_of(shape):
@@ -66,52 +77,63 @@
     ref[chain, size : size + PAD, :] = extra.astype(bf16)
 
 
-def build_maps(
-    place_ref,
-    near_ref,
-    far_ref,
+def stage_inputs(
     decay_ref,
     input_ref,
+    initial_ref,
     coupling_ref,
-    linear_ref,
-    offset_ref,
-    fade_ref,
-    whole_ref,
+    tiles_ref,
+    decays_ref,
+    inputs_ref,
+    starts_ref,
     coupling_vmem,
-    step_maps,
-    panels,
-    fades,
-    drives,
-    running,
+    decay_vmem,
+    input_vmem,
+    initial_vmem,
     sems,
 ):
-    quarter = place_ref[0]
-    channels, _, size, _ = coupling_ref.shape
-    chains = coupling_vmem.shape[0]
-    steps = near_ref.shape[1]
-    total = QUAD * steps
-    first_block = (quarter // 2) * chains
-
-    def fetch(chain):
-        return pltpu.make_async_copy(
+    chains, channels, size, _ = coupling_vmem.shape
+    record = corner_of_quad() & 1
+    first_block = (corner_of_quad() >> 1) * chains
+    copies = [
+        pltpu.make_async_copy(
             coupling_ref.at[:, first_block + chain], coupling_vmem.at[chain], sems.at[chain]
         )
-
-    for chain in range(chains):
-        fetch(chain).start()
-    path = jnp.concatenate([near_ref[0], near_ref[1], far_ref[0], far_ref[1]], axis=0)
-    moves = path[:, 0:channels]
-    gaps = path[:, channels : channels + 1]
-    for chain in range(chains):
-        fades[chain] = jnp.exp(-gaps * decay_ref[first_block + chain])
-        drives[chain] = jnp.dot(
-            moves,
-            input_ref[first_block + chain],
-            precision=lax.Precision.HIGHEST,
-            preferred_element_type=f32,
-        )
+        for chain in range(chains)
+    ]
+    copies.append(pltpu.make_async_copy(decay_ref, decay_vmem, sems.at[chains]))
+    copies.append(pltpu.make_async_copy(input_ref, input_vmem, sems.at[chains + 1]))
+    copies.append(pltpu.make_async_copy(initial_ref, initial_vmem, sems.at[chains + 2]))
+    for copy in copies:
+        copy.start()
+    for copy in copies[chains:]:
+        copy.wait()
+    for chain in range(chains):
+        lanes = pl.ds(pl.multiple_of((first_block + chain) * size, size), size)
+        decays_ref[chain] = decay_vmem[:, lanes]
+        inputs_ref[chain] = input_vmem[:, lanes]
+        initial = initial_vmem[:, lanes]
+        starts_ref[chain] = jnp.where(record == 0, initial[0:1], initial[1:2])
+    for chain in range(chains):
+        copies[chain].wait()
+        for tile in range(size // PAD):
+            halves = [
+                coupling_vmem[chain, :, tile * PAD + half : tile * PAD + half + 8, :]
+                .reshape(channels * 8, size)
+                .astype(bf16)
+                for half in (0, 8)
+            ]
+            tiles_ref[chain, tile] = jnp.concatenate(halves, axis=1)
+
+
+def form_steps(slots, decay_ref, input_ref, tiles_ref, maps_ref, fades_ref, drives_ref):
+    chains, tile_count, lanes, _ = tiles_ref.shape
+    size = decay_ref.shape[2]
+    channels = lanes // 8
+    steps = slots[0].shape[0] - 1
+    total = len(slots) * steps
+    moves = jnp.concatenate([slot[0:steps] for slot in slots], axis=0)
     rows = total * 8
-    lanes = channels * 8
     spread = jnp.broadcast_to(moves[:, None, :], (total, 8, channels)).reshape(rows, channels)
     high = spread.astype(bf16)
     low = (spread - high.astype(f32)).astype(bf16)
@@ -128,52 +150,108 @@
         ],
         axis=1,
     )
+    for chain in range(chains):
+
+        @pl.loop(0, tile_count, step=FORM_UNROLL)
+        def _(first):
+            for more in range(FORM_UNROLL):
+                tile = first + more
+                right = tiles_ref[chain, tile]
+                right = jnp.concatenate([right, right], axis=0)
+                made = jnp.dot(left, right, preferred_element_type=f32)
+                halves = [
+                    made[:, 0:size].reshape(total, 8, size),
+                    made[:, size:].reshape(total, 8, size),
+                ]
+                at = pl.multiple_of(tile * PAD, PAD)
+                maps_ref[chain, :, pl.ds(at, PAD), :] = jnp.concatenate(halves, axis=1).astype(bf16)
+
+    corner = row_of((steps, steps)) == lax.broadcasted_iota(jnp.int32, (steps, steps), 1)
+    gaps = jnp.concatenate(
+        [
+            jnp.sum(jnp.where(corner, slot[steps : steps + 1, 0:steps], 0.0), axis=1, keepdims=True)
+            for slot in slots
+        ],
+        axis=0,
+    )
+    for chain in range(chains):
+        fades_ref[chain] = jnp.exp(-gaps * decay_ref[chain])
+        drives_ref[chain] = jnp.dot(
+            moves, input_ref[chain], precision=lax.Precision.HIGHEST, preferred_element_type=f32
+        )
+
+
+def form_near(near_ref, decay_ref, input_ref, tiles_ref, maps_ref, fades_ref, drives_ref):
+    slots = [near_ref[0], near_ref[1]]
+    form_steps(slots, decay_ref, input_ref, tiles_ref, maps_ref, fades_ref, drives_ref)
+
+
+def build_maps(
+    far_ref,
+    decay_ref,
+    input_ref,
+    tiles_ref,
+    near_maps,
+    near_fades,
+    near_drives,
+    linear_ref,
+    offset_ref,
+    fade_ref,
+    whole_ref,
+    far_maps,
+    far_fades,
+    far_drives,
+    panels,
+    running,
+):
+    quarter = corner_of_quad()
+    chains, _, steps, size, _ = linear_ref.shape
+    slots = [far_ref[0], far_ref[1]]
+    form_steps(slots, decay_ref, input_ref, tiles_ref, far_maps, far_fades, far_drives)
     eye = row_of((size, size)) == lax.broadcasted_iota(jnp.int32, (size, size), 1)
-    for chain in range(chains):
-        fetch(chain).wait()
-
-        @pl.loop(0, size // PAD)
-        def _(tile):
-            at = pl.multiple_of(tile * PAD, PAD)
-            tiles = [
-                coupling_vmem[chain, :, pl.ds(at + half, 8), :].reshape(lanes, size).astype(bf16)
-                for half in (0, 8)
-            ]
-            right = jnp.concatenate(tiles, axis=1)
-            right = jnp.concatenate([right, right], axis=0)
-            made = jnp.dot(left, right, preferred_element_type=f32)
-            halves = [made[:, 0:size].reshape(total, 8, size), made[:, size:].reshape(total, 8, size)]
-            step_maps[chain, :, pl.ds(at, PAD), :] = jnp.concatenate(halves, axis=1).astype(bf16)
-
+    zero = jnp.zeros((size + PAD, size), bf16)
+    for chain in range(chains):
         for slot in range(QUAD):
             panels[chain, slot, 0:size, :] = jnp.where(eye, 1.0, 0.0)
             panels[chain, slot, size : size + PAD, :] = jnp.zeros((PAD, size), f32)
             running[chain, slot] = jnp.ones((1, size), f32)
 
-    @pl.loop(0, steps)
-    def _(step):
-        for chain in range(chains):
-            for slot in range(QUAD):
-                at = slot * steps + step
-                panel = panels[chain, slot]
-                fade = fades[chain, pl.ds(at, 1), :]
-                drive = drives[chain, pl.ds(at, 1), :]
-                pushed = lax.dot_general(
-                    panel.astype(bf16),
-                    step_maps[chain, at],
-                    CONTRACT_LAST,
-                    preferred_element_type=f32,
-                )
-                moved = panel * fade + pushed
-                matrix = moved[0:size]
-                offset = moved[size:] + drive
-                panels[chain, slot, 0:size, :] = matrix
-                panels[chain, slot, size : size + PAD, :] = offset
-                decay = running[chain, slot] * fade
-                running[chain, slot] = decay
-                linear_ref[chain, slot, step] = (matrix - jnp.where(eye, decay, 0.0)).astype(bf16)
-                offset_ref[chain, slot, pl.ds(step, 1), :] = offset[0:1]
-                fade_ref[chain, slot, pl.ds(step, 1), :] = decay
+    @pl.loop(0, steps, step=STEP_UNROLL)
+    def _(first):
+        for more in range(STEP_UNROLL):
+            step = first + more
+            for chain in range(chains):
+                for maps, fades, drives, base in (
+                    (near_maps, near_fades, near_drives, 0),
+                    (far_maps, far_fades, far_drives, 2),
+                ):
+                    pair = [panels[chain, base + half] for half in range(2)]
+                    upper = jnp.concatenate([pair[0].astype(bf16), zero], axis=1)
+                    lower = jnp.concatenate([zero, pair[1].astype(bf16)], axis=1)
+                    late = jnp.concatenate([maps[chain, step], maps[chain, steps + step]], axis=1)
+                    pushed = lax.dot_general(
+                        jnp.concatenate([upper, lower], axis=0),
+                        late,
+                        CONTRACT_LAST,
+                        preferred_element_type=f32,
+                    )
+                    for half in range(2):
+                        slot = base + half
+                        at = half * steps + step
+                        fade = fades[chain, pl.ds(at, 1), :]
+                        first_row = half * (size + PAD)
+                        moved = pair[half] * fade + pushed[first_row : first_row + size + PAD]
+                        matrix = moved[0:size]
+                        offset = moved[size:] + drives[chain, pl.ds(at, 1), :]
+                        panels[chain, slot, 0:size, :] = matrix
+                        panels[chain, slot, size : size + PAD, :] = offset
+                        decay = running[chain, slot] * fade
+                        running[chain, slot] = decay
+                        linear_ref[chain, slot, step] = (
+                            matrix - jnp.where(eye, decay, 0.0)
+                        ).astype(bf16)
+                        offset_ref[chain, slot, pl.ds(step, 1), :] = offset[0:1]
+                        fade_ref[chain, slot, pl.ds(step, 1), :] = decay
 
     for chain in range(chains):
         panel = panels[chain, quarter]
@@ -192,7 +270,7 @@
         store_map(whole_ref, chain, size, panel, decay)
 
 
-def join_maps(place_ref, own_ref, other_ref, out_ref):
+def join_maps(level, own_ref, other_ref, out_ref):
     size = own_ref.shape[2]
 
     def join(early, late):
@@ -208,50 +286,50 @@
             panel = jnp.concatenate([moved[0:size], moved[size:] + late_offset], axis=0)
             store_map(out_ref, chain, size, panel, decay * late_decay)
 
-    @pl.when(place_ref[0] == 0)
+    @pl.when(bit_of(level) == 0)
     def _():
         join(own_ref, other_ref)
 
-    @pl.when(place_ref[0] != 0)
+    @pl.when(bit_of(level) != 0)
     def _():
         join(other_ref, own_ref)
 
 
-def cross_pair(place_ref, own_ref, other_ref, start_ref, out_ref):
+def cross_pair(level, own_ref, other_ref, start_ref, out_ref):
     size = own_ref.shape[2]
     chains = own_ref.shape[0]
 
     def cross(early, late):
         for chain in range(chains):
-            state = start_ref[place_ref[1] + chain]
+            state = start_ref[chain]
             state = apply_map(early, chain, size, state)
             out_ref[chain] = apply_map(late, chain, size, state)
 
-    @pl.when(place_ref[0] == 0)
+    @pl.when(bit_of(level) == 0)
     def _():
         cross(own_ref, other_ref)
 
-    @pl.when(place_ref[0] != 0)
+    @pl.when(bit_of(level) != 0)
     def _():
         cross(other_ref, own_ref)
 
 
-def run_steps(place_ref, start_ref, base_ref, *refs):
+def run_steps(start_ref, base_ref, *refs):
     level_refs = refs[:-7]
     linear_ref, offset_ref, fade_ref, keep_ref, across_ref, later_ref, entries = refs[-7:]
     chains, _, steps, size, _ = linear_ref.shape
-    quarter = place_ref[0]
-    for chain in range(chains):
-        entries[chain, 0] = start_ref[place_ref[1] + chain]
-
-    @pl.when(place_ref[2] != 0)
+    quarter = corner_of_quad()
+    for chain in range(chains):
+        entries[chain, 0] = start_ref[chain]
+
+    @pl.when(bit_of(2 + len(level_refs)) != 0)
     def _():
         for chain in range(chains):
             entries[chain, 0] = base_ref[chain]
 
     for level, ref in reversed(list(enumerate(level_refs))):
 
-        @pl.when(place_ref[3 + level] != 0)
+        @pl.when(bit_of(2 + level) != 0)
         def _():
             for chain in range(chains):
                 entries[chain, 0] = apply_map(ref, chain, size, entries[chain, 0])
@@ -286,14 +364,12 @@
             target[place, chain] = gathered
 
 
-def scale_states(
-    place_ref, keep_ref, across_ref, later_ref, gain_ref, states_ref, packed_ref, table
-):
+def scale_states(keep_ref, across_ref, later_ref, gain_ref, states_ref, packed_ref, table):
     records, steps, units = states_ref.shape
     chains = keep_ref.shape[1]
     size = keep_ref.shape[3]
-    record = place_ref[0] % 2
-    half = place_ref[0] // 2
+    record = corner_of_quad() & 1
+    half = corner_of_quad() >> 1
     for chain in range(chains):
         here = half * chains + chain
         there = (1 - half) * chains + chain
@@ -318,10 +394,13 @@
         packed_ref[index * steps : (index + 1) * steps, units : units + size] = extra.astype(bf16)
 
 
-def read_out(place_ref, own_ref, other_ref, value_ref, gate_ref, out_ref):
+def read_out(states_vmem, own_ref, other_ref, value_ref, gate_ref, states_ref, out_ref, sem):
+    copy = pltpu.make_async_copy(states_vmem, states_ref, sem)
+    copy.start()
     units = value_ref.shape[0] // 2
-    own_at = pl.multiple_of(place_ref[0] * units, units)
-    other_at = pl.multiple_of((1 - place_ref[0]) * units, units)
+    core = lax.axis_index("blk")
+    own_at = pl.multiple_of(core * units, units)
+    other_at = pl.multiple_of((1 - core) * units, units)
     own = own_ref[:, 0:units]
     other = other_ref[:, 0:units]
     squares = jnp.sum(
@@ -337,6 +416,7 @@
     value = project(value_ref) * inverse
     gate = project(gate_ref) * inverse
     out_ref[...] = (value * jax.nn.sigmoid(gate)).astype(bf16)
+    copy.wait()
 
 
 def body(
@@ -360,15 +440,54 @@
     place = lax.axis_index("tm")
     quarter = place % QUAD
     record = quarter % 2
-    first_chain = record * local_blocks + (quarter // 2) * chains
-
-    path = jnp.concatenate([increments, step_sizes[:, :, None]], axis=2)
+
+    levels = range(2, bits - 1)
+    path = jnp.concatenate([increments, step_sizes[:, None, :]], axis=1)
     mine = lax.dynamic_index_in_dim(path, record, 0, keepdims=False)
     theirs = lax.dynamic_index_in_dim(path, 1 - record, 0, keepdims=False)
     near = jnp.stack([mine, partner(theirs, "tm", 1)])
+
+    total = QUAD // 2 * steps
+    tiles, decays, inputs, start = pl.pallas_call(
+        stage_inputs,
+        out_shape=(
+            jax.ShapeDtypeStruct((chains, size // PAD, channels * 8, 2 * size), bf16),
+            jax.ShapeDtypeStruct((chains, 1, size), f32),
+            jax.ShapeDtypeStruct((chains, channels, size), f32),
+            jax.ShapeDtypeStruct((chains, 1, size), f32),
+        ),
+        in_specs=[HBM_SPEC] * 4,
+        out_specs=(VMEM_SPEC,) * 4,
+        scratch_shapes=[
+            pltpu.VMEM((chains, channels, size, size), f32),
+            pltpu.VMEM((1, local_units), f32),
+            pltpu.VMEM((channels, local_units), f32),
+            pltpu.VMEM((records, local_units), f32),
+            pltpu.SemaphoreType.DMA((chains + 3,)),
+        ],
+        compiler_params=params(16),
+        name="stage_inputs",
+    )(
+        *(
+            pltpu.with_memory_space_constraint(array, pltpu.HBM)
+            for array in (decay_rate.reshape(1, local_units), input_weight, initial_state, coupling)
+        ),
+    )
+    near, tiles = lax.optimization_barrier((near, tiles))
     far = partner(near, "tm", 2)
-
-    total = QUAD * steps
+    formed = (
+        pltpu.VMEM((chains, total, size, size), bf16),
+        pltpu.VMEM((chains, total, size), f32),
+        pltpu.VMEM((chains, total, size), f32),
+    )
+    near_formed = pl.pallas_call(
+        form_near,
+        out_shape=tuple(jax.ShapeDtypeStruct(item.shape, item.dtype) for item in formed),
+        in_specs=[VMEM_SPEC] * 4,
+        out_specs=(VMEM_SPEC,) * 3,
+        compiler_params=params(16),
+        name="form_near",
+    )(near, decays, inputs, tiles)
     linear, offset, fade, whole = pl.pallas_call(
         build_maps,
         out_shape=(
@@ -377,53 +496,38 @@
             jax.ShapeDtypeStruct((chains, QUAD, steps, size), f32),
             jax.ShapeDtypeStruct((chains, size + PAD, size), bf16),
         ),
-        in_specs=[SMEM_SPEC] + [VMEM_SPEC] * 4 + [ANY_SPEC],
+        in_specs=[VMEM_SPEC] * 7,
         out_specs=(VMEM_SPEC,) * 4,
         scratch_shapes=[
-            pltpu.VMEM((chains, channels, size, size), f32),
-            pltpu.VMEM((chains, total, size, size), bf16),
+            *formed,
             pltpu.VMEM((chains, QUAD, size + PAD, size), f32),
-            pltpu.VMEM((chains, total, size), f32),
-            pltpu.VMEM((chains, total, size), f32),
             pltpu.VMEM((chains, QUAD, 1, size), f32),
-            pltpu.SemaphoreType.DMA((chains,)),
         ],
-        compiler_params=params(32),
+        compiler_params=params(24),
         name="build_maps",
-    )(
-        jnp.stack([quarter]),
-        near,
-        far,
-        decay_rate.reshape(local_blocks, 1, size),
-        jnp.transpose(input_weight.reshape(channels, local_blocks, size), (1, 0, 2)),
-        coupling,
-    )
-
-    start = initial_state.reshape(records * local_blocks, 1, size)
+    )(far, decays, inputs, tiles, *near_formed)
+
     earlier = []
-    sides = []
     for level in range(2, bits - 1):
         other = partner(whole, "tm", 1 << level)
-        side = (place >> level) % 2
-        sides.append(side)
         earlier.append(other)
         if level + 1 < bits - 1:
             whole = pl.pallas_call(
-                join_maps,
+                functools.partial(join_maps, level),
                 out_shape=jax.ShapeDtypeStruct(whole.shape, bf16),
-                in_specs=[SMEM_SPEC] + [VMEM_SPEC] * 2,
+                in_specs=[VMEM_SPEC] * 2,
                 out_specs=VMEM_SPEC,
                 compiler_params=params(16),
                 name="join_maps",
-            )(jnp.stack([side]), whole, other)
+            )(whole, other)
     crossed = pl.pallas_call(
-        cross_pair,
+        functools.partial(cross_pair, bits - 2),
         out_shape=jax.ShapeDtypeStruct((chains, 1, size), f32),
-        in_specs=[SMEM_SPEC] + [VMEM_SPEC] * 3,
+        in_specs=[VMEM_SPEC] * 3,
         out_specs=VMEM_SPEC,
         compiler_params=params(16),
         name="cross_pair",
-    )(jnp.stack([sides[-1], first_chain]), whole, earlier[-1], start)
+    )(whole, earlier[-1], start)
     base = partner(crossed, "tm", 1 << (bits - 1))
 
     piece = (chains, steps, size)
@@ -434,13 +538,12 @@
             jax.ShapeDtypeStruct((2,) + piece, f32),
             jax.ShapeDtypeStruct((1,) + piece, f32),
         ),
-        in_specs=[SMEM_SPEC] + [VMEM_SPEC] * (5 + len(earlier)),
+        in_specs=[VMEM_SPEC] * (5 + len(earlier)),
         out_specs=(VMEM_SPEC,) * 3,
         scratch_shapes=[pltpu.VMEM((chains, QUAD, 1, size), f32)],
         compiler_params=params(16),
         name="run_steps",
     )(
-        jnp.stack([quarter, first_chain, place >> (bits - 1)] + sides),
         start,
         base,
         *earlier,
@@ -455,25 +558,29 @@
     states, packed = pl.pallas_call(
         scale_states,
         out_shape=(
-            jax.ShapeDtypeStruct((records, steps, local_units), f32),
+            pltpu.VMEM((records, steps, local_units), f32),
             jax.ShapeDtypeStruct((rows, local_units + size), bf16),
         ),
-        in_specs=[SMEM_SPEC] + [VMEM_SPEC] * 4,
+        in_specs=[VMEM_SPEC] * 4,
         out_specs=(VMEM_SPEC,) * 2,
         scratch_shapes=[pltpu.VMEM((records, local_blocks, steps, size), f32)],
         compiler_params=params(16),
         name="scale_states",
-    )(jnp.stack([quarter]), keep, across, later, gain.reshape(1, local_units))
+    )(keep, across, later, gain.reshape(1, local_units))
     packed_other = partner(packed, "blk", 1)
     features = value_weight.shape[1]
-    readout = pl.pallas_call(
+    states, readout = pl.pallas_call(
         read_out,
-        out_shape=jax.ShapeDtypeStruct((rows, features), bf16),
-        in_specs=[SMEM_SPEC] + [VMEM_SPEC] * 4,
-        out_specs=VMEM_SPEC,
+        out_shape=(
+            jax.ShapeDtypeStruct((records, steps, local_units), f32),
+            jax.ShapeDtypeStruct((rows, features), bf16),
+        ),
+        in_specs=[VMEM_SPEC] * 5,
+        out_specs=(HBM_SPEC, VMEM_SPEC),
+        scratch_shapes=[pltpu.SemaphoreType.DMA(())],
         compiler_params=params(16),
         name="read_out",
-    )(jnp.stack([lax.axis_index("blk")]), packed, packed_other, value_weight, gate_weight)
+    )(states, packed, packed_other, value_weight, gate_weight)
     return (states, readout.reshape(records, steps, features))
 
 

time: 46.1 us -> 36.6 us (0.79)
  local copies, waits for them, and re-layouts: 4.36 us -> 0.02 us
  Pallas kernels: 14.1 us -> 11.4 us
  waiting for transfers between devices: 11.7 us -> 9.45 us
    pallas_call x1, Pallas kernels: 9.97 us -> 5.45 us  [body(): pl.pallas_call(build_maps, out_shape=(jax.ShapeDtypeStruct((chains, QUAD,...]
    unnamed x12 -> x6, local copies, waits for them, and re-layouts: 2.89 us -> 0.02 us
    pallas_call x3 -> x5, Pallas kernels: 2.56 us -> 4.92 us  [the longest x1 1.64 us: body(): pl.pallas_call(stage_inputs, out_shape=(jax.ShapeDtypeStruct((chains, siz...]
    ppermute x7, waiting for transfers between devices: 11.7 us -> 9.45 us  [partner(): lax.ppermute(array, axis, [(i, i ^ flip) for i in range(lax.axis_size(axi...]
    broadcast_in_dim x1 -> x0, local copies, waits for them, and re-layouts: 0.76 us -> none  [body(): path = jnp.concatenate([increments, step_sizes[:, :, None]], axis=2)]
    reshape x1 -> x0, local copies, waits for them, and re-layouts: 0.7 us -> none  [body(): start = initial_state.reshape(records * local_blocks, 1, size)]
    pallas_call x1, Pallas kernels: 1.58 us -> 1.03 us  [body(): pl.pallas_call(run_steps, out_shape=(jax.ShapeDtypeStruct((1,) + piece, f...]
  transfers between devices with their start and end apart: 7 -> 7, of which waited for: 7 -> 6; matrix products, arithmetic and copies ran while one was open for 2% -> 0% of each run, Pallas kernels for 0% -> 9%
where the time goes in v1:
time: 36.6 us; the launch traced here: 36.3 us
  starting transfers between devices  14 us (38%)
  Pallas kernels  11.4 us (31%)
  waiting for transfers between devices  9.45 us (26%)
  other arithmetic  0.74 us (2%)
  between operations  0.73 us (2%)
    ppermute x7, starting transfers between devices, partner(): lax.ppermute(array, axis, [(i, i ^ flip) for i in range(lax.axis_size(axi...  14 us
    ppermute x7, waiting for transfers between devices, partner(): lax.ppermute(array, axis, [(i, i ^ flip) for i in range(lax.axis_size(axi...  9.45 us
    pallas_call x1, Pallas kernels, body(): pl.pallas_call(build_maps, out_shape=(jax.ShapeDtypeStruct((chains, QUAD,...  5.45 us
    pallas_call x1, Pallas kernels, body(): pl.pallas_call(stage_inputs, out_shape=(jax.ShapeDtypeStruct((chains, siz...  1.64 us
    pallas_call x1, Pallas kernels, body(): pl.pallas_call(form_near, out_shape=tuple((jax.ShapeDtypeStruct(item.shap...  1.63 us
    pallas_call x1, Pallas kernels, body(): pl.pallas_call(read_out, out_shape=(jax.ShapeDtypeStruct((records, steps,...  1.27 us
    pallas_call x1, Pallas kernels, body(): pl.pallas_call(run_steps, out_shape=(jax.ShapeDtypeStruct((1,) + piece, f...  1.03 us
  transfers between devices with their start and end apart: 7, of which 6 were waited for; matrix products, arithmetic and copies ran while one was open for 0% of the time, Pallas kernels for 9%

profile of v1, /device:TPU:0, one launch (start us, length us, event | category | flops | bytes accessed | tf_op | source)
XLA Modules:
  0.0 36.3 jit_solution(4610964248219430194)
XLA Ops:
  0.7 0.7 %fusion.2 = (f32[1,17,16]{2,1,0:T(8,128)S(1)}, f32[17,16]{1,0:T(8,128)S(1)}) fusion(s32[]{:T(128)S(6)} %select_n.20, f32[2,16,16]{2,1,0:T(8,128)} %param.12, f32[2,1,16]{2,1,0:T(1,128)} %bitcast.12, s32[]{:T(128)S(6)} %select_n.21), kind=kLoop, calls=%fused_computation.8 | loop fusion | flops 544 | bytes 4360 | tf_op jit(solution)/shard_map/concatenate | solution.py:445
  1.4 3.0 %collective-permute-start = (f32[17,16]{1,0:T(8,128)S(1)}, f32[17,16]{1,0:T(8,128)S(1)}, u32[]{:S(2)}, u32[]{:S(2)}) collective-permute-start(f32[17,16]{1,0:T(8,128)S(1)} %get-tuple-element.43), channel_id=1, source_target_pairs={{0,2},{2,0},{4,6},{6,4},{8,10},{10,8},{12,14},{14,12},{16,18},{18,... | collective-permute-start | bytes 3272 | tf_op jit(solution)/shard_map/ppermute | solution.py:27
  4.4 1.6 %stage_inputs.1 = (bf16[2,8,128,256]{3,2,1,0:T(8,128)(2,1)S(1)}, f32[2,1,128]{2,1,0:T(1,128)S(1)}, f32[2,16,128]{2,1,0:T(8,128)S(1)}, f32[2,1,128]{2,1,0:T(1,128)S(1)}) custom-call(f32[1,512]{1,0:T(1,128)} %bitcast.11, f32[16,512]{1,0:T(8,128)} %input_ref.1, f32[2,512]{1,0:T(2,128)} %initial_ref.1, f32[16,4,128,128]{3,2,1,0:T(8,128)} %coupling_ref.1), custom_call_target="tpu_custom_call" | custom-call | tf_op jit(solution)/shard_map/stage_inputs/pallas_call | solution.py:451
  6.0 0.0 collective-permute-done
  6.0 2.1 %collective-permute-start.1 = (f32[2,17,16]{2,1,0:T(8,128)S(1)}, f32[2,17,16]{2,1,0:T(8,128)S(1)}, u32[]{:S(2)}, u32[]{:S(2)}) collective-permute-start(f32[2,17,16]{2,1,0:T(8,128)S(1)} %pad_maximum_fusion.1.near_ref), channel_id=1, source_target_pairs={{0,4},{2,6},{4,0},{6,2},{8,12},{10,14},{12,8},{14,10},{16,20},{18,... | collective-permute-start | bytes 6536 | tf_op jit(solution)/shard_map/ppermute | solution.py:27
  8.1 1.6 %form_near.1 = (bf16[2,32,128,128]{3,2,1,0:T(8,128)(2,1)S(1)}, f32[2,32,128]{2,1,0:T(8,128)S(1)}, f32[2,32,128]{2,1,0:T(8,128)S(1)}) custom-call(f32[2,17,16]{2,1,0:T(8,128)S(1)} %pad_maximum_fusion.1.near_ref, f32[2,1,128]{2,1,0:T(1,128)S(1)} %get-tuple-element.25.decay_ref, f32[2,16,128]{2,1,0:T(8,128)S(1)} %get-tuple-element.26.input_ref, ...), custom_call_target="tpu_custom_call" | custom-call | tf_op jit(solution)/shard_map/form_near/pallas_call | solution.py:483
  9.7 0.0 copy-start.2
  9.7 0.0 copy-start
  9.8 0.0 copy-start.1
  9.8 0.2 collective-permute-done.1.far_ref
  9.9 5.5 %build_maps.1 = (bf16[2,4,16,128,128]{4,3,2,1,0:T(8,128)(2,1)S(1)}, f32[2,4,16,128]{3,2,1,0:T(8,128)S(1)}, f32[2,4,16,128]{3,2,1,0:T(8,128)S(1)}, bf16[2,144,128]{2,1,0:T(8,128)(2,1)S(1)}) custom-call(f32[2,17,16]{2,1,0:T(8,128)S(1)} %collective-permute-done.1.far_ref, f32[2,1,128]{2,1,0:T(1,128)S(1)} %get-tuple-element.25.decay_ref, ...), custom_call_target="tpu_custom_call" | custom-call | tf_op jit(solution)/shard_map/build_maps/pallas_call | solution.py:491
  15.4 2.1 %collective-permute-start.2 = (bf16[2,144,128]{2,1,0:T(8,128)(2,1)S(1)}, bf16[2,144,128]{2,1,0:T(8,128)(2,1)S(1)}, u32[]{:S(2)}, u32[]{:S(2)}) collective-permute-start(bf16[2,144,128]{2,1,0:T(8,128)(2,1)S(1)} %get-tuple-element.31.own_ref), channel_id=1, source_target_pairs={{0,8},{2,10},{4,12},{6,14},{8,0},{10,2},{12,4},{14,6},{16,24},{18,... | collective-permute-start | bytes 221192 | tf_op jit(solution)/shard_map/ppermute | solution.py:27
  17.5 2.3 %collective-permute-done.2.other_ref.refs_0_ = bf16[2,144,128]{2,1,0:T(8,128)(2,1)S(1)} collective-permute-done((bf16[2,144,128]{2,1,0:T(8,128)(2,1)S(1)}, bf16[2,144,128]{2,1,0:T(8,128)(2,1)S(1)}, u32[]{:S(2)}, u32[]{:S(2)}) %collective-permute-start.2) | collective-permute-done | bytes 73760 | tf_op jit(solution)/shard_map/ppermute | solution.py:27
  19.8 0.3 cross_pair.1
  20.1 3.1 %collective-permute-start.3 = (f32[2,1,128]{2,1,0:T(1,128)S(1)}, f32[2,1,128]{2,1,0:T(1,128)S(1)}, u32[]{:S(2)}, u32[]{:S(2)}) collective-permute-start(f32[2,1,128]{2,1,0:T(1,128)S(1)} %cross_pair.1), channel_id=1, source_target_pairs={{0,16},{2,18},{4,20},{6,22},{8,24},{10,26},{12,28},{14,30},{16,0},... | collective-permute-start | bytes 3080 | tf_op jit(solution)/shard_map/ppermute | solution.py:27
  23.2 1.6 %collective-permute-done.3.base_ref = f32[2,1,128]{2,1,0:T(1,128)S(1)} collective-permute-done((f32[2,1,128]{2,1,0:T(1,128)S(1)}, f32[2,1,128]{2,1,0:T(1,128)S(1)}, u32[]{:S(2)}, u32[]{:S(2)}) %collective-permute-start.3) | collective-permute-done | bytes 1056 | tf_op jit(solution)/shard_map/ppermute | solution.py:27
  24.7 1.0 %run_steps.1 = (f32[1,2,16,128]{3,2,1,0:T(8,128)S(1)}, f32[2,2,16,128]{3,2,1,0:T(8,128)S(1)}, f32[1,2,16,128]{3,2,1,0:T(8,128)S(1)}) custom-call(f32[2,1,128]{2,1,0:T(1,128)S(1)} %get-tuple-element.22.start_ref, f32[2,1,128]{2,1,0:T(1,128)S(1)} %collective-permute-done.3.base_ref, bf16[2,144,128]{2,1,0:T(8,128)(2,1)S(1)} %collective-permute-done.2.other_ref.refs_0_, ...), custom_call_target="tpu_custom_call" | custom-call | tf_op jit(solution)/shard_map/run_steps/pallas_call | solution.py:534
  25.7 1.9 %collective-permute-start.4 = (f32[2,2,16,128]{3,2,1,0:T(8,128)S(1)}, f32[2,2,16,128]{3,2,1,0:T(8,128)S(1)}, u32[]{:S(2)}, u32[]{:S(2)}) collective-permute-start(f32[2,2,16,128]{3,2,1,0:T(8,128)S(1)} %get-tuple-element.36), channel_id=1, source_target_pairs={{0,2},{2,0},{4,6},{6,4},{8,10},{10,8},{12,14},{14,12},{16,18},{18,... | collective-permute-start | bytes 98312 | tf_op jit(solution)/shard_map/ppermute | solution.py:27
  27.6 2.1 %collective-permute-done.4.across_ref = f32[2,2,16,128]{3,2,1,0:T(8,128)S(1)} collective-permute-done((f32[2,2,16,128]{3,2,1,0:T(8,128)S(1)}, f32[2,2,16,128]{3,2,1,0:T(8,128)S(1)}, u32[]{:S(2)}, u32[]{:S(2)}) %collective-permute-start.4) | collective-permute-done | bytes 32800 | tf_op jit(solution)/shard_map/ppermute | solution.py:27
  29.7 1.8 %collective-permute-start.5 = (f32[2,2,16,128]{3,2,1,0:T(8,128)S(1)}, f32[2,2,16,128]{3,2,1,0:T(8,128)S(1)}, u32[]{:S(2)}, u32[]{:S(2)}) collective-permute-start(f32[2,2,16,128]{3,2,1,0:T(8,128)S(1)} %pad_maximum_fusion), channel_id=1, source_target_pairs={{0,4},{2,6},{4,0},{6,2},{8,12},{10,14},{12,8},{14,10},{16,20},{18,... | collective-permute-start | bytes 98312 | tf_op jit(solution)/shard_map/ppermute | solution.py:27
  31.6 2.1 %collective-permute-done.5.later_ref = f32[2,2,16,128]{3,2,1,0:T(8,128)S(1)} collective-permute-done((f32[2,2,16,128]{3,2,1,0:T(8,128)S(1)}, f32[2,2,16,128]{3,2,1,0:T(8,128)S(1)}, u32[]{:S(2)}, u32[]{:S(2)}) %collective-permute-start.5) | collective-permute-done | bytes 32800 | tf_op jit(solution)/shard_map/ppermute | solution.py:27
  33.6 0.0 copy-done.2
  33.6 0.1 scale_states.1
  33.8 0.1 collective-permute-start.6
  33.8 1.2 %collective-permute-done.6.other_ref = bf16[32,640]{1,0:T(8,128)(2,1)S(1)} collective-permute-done((bf16[32,640]{1,0:T(8,128)(2,1)S(1)}, bf16[32,640]{1,0:T(8,128)(2,1)S(1)}, u32[]{:S(2)}, u32[]{:S(2)}) %collective-permute-start.6) | collective-permute-done | bytes 40992 | tf_op jit(solution)/shard_map/ppermute | solution.py:27
  35.0 0.0 copy-done
  35.0 0.0 copy-done.1
  35.1 1.3 %read_out.1 = (f32[2,16,512]{2,1,0:T(8,128)}, bf16[32,512]{1,0:T(8,128)(2,1)}) custom-call(f32[2,16,512]{2,1,0:T(8,128)S(1)} %get-tuple-element.38.states_vmem, bf16[32,640]{1,0:T(8,128)(2,1)S(1)} %get-tuple-element.39.own_ref, bf16[32,640]{1,0:T(8,128)(2,1)S(1)} %collective-permute-done.6.other_ref, bf16[1024,512]{1,0:T(8,128)(2,1)S(1)} %copy-done, ...), custom_call_target="tpu_custom_call" | custom-call | tf_op jit(solution)/shard_map/read_out/pallas_call | solution.py:572
  (3 shorter events, 0.0 us)
Async XLA Ops:
  1.4 4.6 %collective-permute-start = (f32[17,16]{1,0:T(8,128)S(1)}, f32[17,16]{1,0:T(8,128)S(1)}, u32[]{:S(2)}, u32[]{:S(2)}) collective-permute-start(f32[17,16]{1,0:T(8,128)S(1)} %get-tuple-element.43), channel_id=1, source_target_pairs={{0,2},{2,0},{4,6},{6,4},{8,10},{10,8},{12,14},{14,12},{16,18},{18,... | collective-permute-start | bytes 3272 | tf_op jit(solution)/shard_map/ppermute | solution.py:27
  6.0 3.9 %collective-permute-start.1 = (f32[2,17,16]{2,1,0:T(8,128)S(1)}, f32[2,17,16]{2,1,0:T(8,128)S(1)}, u32[]{:S(2)}, u32[]{:S(2)}) collective-permute-start(f32[2,17,16]{2,1,0:T(8,128)S(1)} %pad_maximum_fusion.1.near_ref), channel_id=1, source_target_pairs={{0,4},{2,6},{4,0},{6,2},{8,12},{10,14},{12,8},{14,10},{16,20},{18,... | collective-permute-start | bytes 6536 | tf_op jit(solution)/shard_map/ppermute | solution.py:27
  9.7 23.9 %copy-start.2 = (f32[512]{0:T(512)S(1)}, f32[512]{0:T(512)}, u32[]{:S(2)}) copy-start(f32[512]{0:T(512)} %param.15) | copy-start | bytes 6148
  9.7 25.3 %copy-start = (bf16[1024,512]{1,0:T(8,128)(2,1)S(1)}, bf16[1024,512]{1,0:T(8,128)(2,1)}, u32[]{:S(2)}) copy-start(bf16[1024,512]{1,0:T(8,128)(2,1)} %value_ref.1) | copy-start | bytes 3145732
  9.8 25.3 %copy-start.1 = (bf16[1024,512]{1,0:T(8,128)(2,1)S(1)}, bf16[1024,512]{1,0:T(8,128)(2,1)}, u32[]{:S(2)}) copy-start(bf16[1024,512]{1,0:T(8,128)(2,1)} %gate_ref.1) | copy-start | bytes 3145732
  15.4 4.5 %collective-permute-start.2 = (bf16[2,144,128]{2,1,0:T(8,128)(2,1)S(1)}, bf16[2,144,128]{2,1,0:T(8,128)(2,1)S(1)}, u32[]{:S(2)}, u32[]{:S(2)}) collective-permute-start(bf16[2,144,128]{2,1,0:T(8,128)(2,1)S(1)} %get-tuple-element.31.own_ref), channel_id=1, source_target_pairs={{0,8},{2,10},{4,12},{6,14},{8,0},{10,2},{12,4},{14,6},{16,24},{18,... | collective-permute-start | bytes 221192 | tf_op jit(solution)/shard_map/ppermute | solution.py:27
  20.1 4.6 %collective-permute-start.3 = (f32[2,1,128]{2,1,0:T(1,128)S(1)}, f32[2,1,128]{2,1,0:T(1,128)S(1)}, u32[]{:S(2)}, u32[]{:S(2)}) collective-permute-start(f32[2,1,128]{2,1,0:T(1,128)S(1)} %cross_pair.1), channel_id=1, source_target_pairs={{0,16},{2,18},{4,20},{6,22},{8,24},{10,26},{12,28},{14,30},{16,0},... | collective-permute-start | bytes 3080 | tf_op jit(solution)/shard_map/ppermute | solution.py:27
  25.7 4.0 %collective-permute-start.4 = (f32[2,2,16,128]{3,2,1,0:T(8,128)S(1)}, f32[2,2,16,128]{3,2,1,0:T(8,128)S(1)}, u32[]{:S(2)}, u32[]{:S(2)}) collective-permute-start(f32[2,2,16,128]{3,2,1,0:T(8,128)S(1)} %get-tuple-element.36), channel_id=1, source_target_pairs={{0,2},{2,0},{4,6},{6,4},{8,10},{10,8},{12,14},{14,12},{16,18},{18,... | collective-permute-start | bytes 98312 | tf_op jit(solution)/shard_map/ppermute | solution.py:27
  29.7 3.9 %collective-permute-start.5 = (f32[2,2,16,128]{3,2,1,0:T(8,128)S(1)}, f32[2,2,16,128]{3,2,1,0:T(8,128)S(1)}, u32[]{:S(2)}, u32[]{:S(2)}) collective-permute-start(f32[2,2,16,128]{3,2,1,0:T(8,128)S(1)} %pad_maximum_fusion), channel_id=1, source_target_pairs={{0,4},{2,6},{4,0},{6,2},{8,12},{10,14},{12,8},{14,10},{16,20},{18,... | collective-permute-start | bytes 98312 | tf_op jit(solution)/shard_map/ppermute | solution.py:27
  33.8 1.3 %collective-permute-start.6 = (bf16[32,640]{1,0:T(8,128)(2,1)S(1)}, bf16[32,640]{1,0:T(8,128)(2,1)S(1)}, u32[]{:S(2)}, u32[]{:S(2)}) collective-permute-start(bf16[32,640]{1,0:T(8,128)(2,1)S(1)} %get-tuple-element.39.own_ref), channel_id=1, source_target_pairs={{0,1},{1,0},{2,3},{3,2},{4,5},{5,4},{6,7},{7,6},{8,9},{9,8},{10,11... | collective-permute-start | bytes 122888 | tf_op jit(solution)/shard_map/ppermute | solution.py:27

commit v2 on v1

--- a/solution.py
+++ b/solution.py
@@ -10,8 +10,7 @@
 QUAD = 4
 PAD = 16
 EPS = 1e-06
-FORM_UNROLL = 4
-STEP_UNROLL = 4
+PARTS = 2
 CONTRACT_LAST = (((1,), (1,)), ((), ()))
 f32 = jnp.float32
 bf16 = jnp.bfloat16
@@ -116,14 +115,14 @@
         starts_ref[chain] = jnp.where(record == 0, initial[0:1], initial[1:2])
     for chain in range(chains):
         copies[chain].wait()
-        for tile in range(size // PAD):
-            halves = [
-                coupling_vmem[chain, :, tile * PAD + half : tile * PAD + half + 8, :]
-                .reshape(channels * 8, size)
-                .astype(bf16)
-                for half in (0, 8)
-            ]
-            tiles_ref[chain, tile] = jnp.concatenate(halves, axis=1)
+        for channel in range(0, channels, 2):
+            pair = [coupling_vmem[chain, channel + more].T for more in range(2)]
+            for tile in range(size // 8):
+                rows = jnp.concatenate([part[tile * 8 : tile * 8 + 8] for part in pair], axis=0)
+                at = (tile % 2) * size
+                tiles_ref[chain, tile // 2, channel * 8 : channel * 8 + PAD, at : at + size] = rows.astype(
+                    bf16
+                )
 
 
 def form_steps(slots, decay_ref, input_ref, tiles_ref, maps_ref, fades_ref, drives_ref):
@@ -151,20 +150,15 @@
         axis=1,
     )
     for chain in range(chains):
-
-        @pl.loop(0, tile_count, step=FORM_UNROLL)
-        def _(first):
-            for more in range(FORM_UNROLL):
-                tile = first + more
-                right = tiles_ref[chain, tile]
-                right = jnp.concatenate([right, right], axis=0)
-                made = jnp.dot(left, right, preferred_element_type=f32)
-                halves = [
-                    made[:, 0:size].reshape(total, 8, size),
-                    made[:, size:].reshape(total, 8, size),
-                ]
-                at = pl.multiple_of(tile * PAD, PAD)
-                maps_ref[chain, :, pl.ds(at, PAD), :] = jnp.concatenate(halves, axis=1).astype(bf16)
+        for tile in range(tile_count):
+            right = tiles_ref[chain, tile]
+            right = jnp.concatenate([right, right], axis=0)
+            made = jnp.dot(left, right, preferred_element_type=f32)
+            halves = [
+                made[:, 0:size].reshape(total, 8, size),
+                made[:, size:].reshape(total, 8, size),
+            ]
+            maps_ref[chain, :, tile * PAD : tile * PAD + PAD, :] = jnp.concatenate(halves, axis=1).astype(bf16)
 
     corner = row_of((steps, steps)) == lax.broadcasted_iota(jnp.int32, (steps, steps), 1)
     gaps = jnp.concatenate(
@@ -181,93 +175,115 @@
         )
 
 
-def form_near(near_ref, decay_ref, input_ref, tiles_ref, maps_ref, fades_ref, drives_ref):
-    slots = [near_ref[0], near_ref[1]]
-    form_steps(slots, decay_ref, input_ref, tiles_ref, maps_ref, fades_ref, drives_ref)
-
-
-def build_maps(
-    far_ref,
+def build_pair(
+    slots,
     decay_ref,
     input_ref,
     tiles_ref,
-    near_maps,
-    near_fades,
-    near_drives,
     linear_ref,
     offset_ref,
     fade_ref,
+    early_ref,
+    panel_ref,
     whole_ref,
-    far_maps,
-    far_fades,
-    far_drives,
+    maps,
+    fades,
+    drives,
     panels,
     running,
 ):
-    quarter = corner_of_quad()
+    form_steps(slots, decay_ref, input_ref, tiles_ref, maps, fades, drives)
     chains, _, steps, size, _ = linear_ref.shape
-    slots = [far_ref[0], far_ref[1]]
-    form_steps(slots, decay_ref, input_ref, tiles_ref, far_maps, far_fades, far_drives)
+    part_steps = steps // PARTS
     eye = row_of((size, size)) == lax.broadcasted_iota(jnp.int32, (size, size), 1)
-    zero = jnp.zeros((size + PAD, size), bf16)
+    parts = [(chain, slot, part) for chain in range(chains) for slot in range(2) for part in range(PARTS)]
+
+    def keep(chain, slot, part, step, linear, offset, decay):
+        linear_ref[chain, slot, part * part_steps + step] = linear
+        at = part * part_steps + step
+        offset_ref[chain, slot, at : at + 1, :] = offset
+        fade_ref[chain, slot, at : at + 1, :] = decay
+        running[chain, slot, part] = decay
+
+    for chain, slot, part in parts:
+        at = slot * steps + part * part_steps
+        fade = fades[chain, at : at + 1, :]
+        drive = drives[chain, at : at + 1, :]
+        panels[chain, slot, part, 0:size, :] = maps[chain, at].astype(f32) + jnp.where(eye, fade, 0.0)
+        panels[chain, slot, part, size : size + PAD, :] = jnp.broadcast_to(drive, (PAD, size))
+        keep(chain, slot, part, 0, maps[chain, at], drive, fade)
+    for step in range(1, part_steps):
+        for chain, slot, part in parts:
+            at = slot * steps + part * part_steps + step
+            panel = panels[chain, slot, part]
+            fade = fades[chain, at : at + 1, :]
+            pushed = jnp.dot(panel.astype(bf16), maps[chain, at], preferred_element_type=f32)
+            moved = panel * fade + pushed
+            matrix = moved[0:size]
+            offset = moved[size:] + drives[chain, at : at + 1, :]
+            panels[chain, slot, part, 0:size, :] = matrix
+            panels[chain, slot, part, size : size + PAD, :] = offset
+            decay = running[chain, slot, part] * fade
+            linear = (matrix - jnp.where(eye, decay, 0.0)).astype(bf16)
+            keep(chain, slot, part, step, linear, offset[0:1], decay)
+
+    early = corner_of_quad() & 1
     for chain in range(chains):
-        for slot in range(QUAD):
-            panels[chain, slot, 0:size, :] = jnp.where(eye, 1.0, 0.0)
-            panels[chain, slot, size : size + PAD, :] = jnp.zeros((PAD, size), f32)
-            running[chain, slot] = jnp.ones((1, size), f32)
-
-    @pl.loop(0, steps, step=STEP_UNROLL)
-    def _(first):
-        for more in range(STEP_UNROLL):
-            step = first + more
-            for chain in range(chains):
-                for maps, fades, drives, base in (
-                    (near_maps, near_fades, near_drives, 0),
-                    (far_maps, far_fades, far_drives, 2),
-                ):
-                    pair = [panels[chain, base + half] for half in range(2)]
-                    upper = jnp.concatenate([pair[0].astype(bf16), zero], axis=1)
-                    lower = jnp.concatenate([zero, pair[1].astype(bf16)], axis=1)
-                    late = jnp.concatenate([maps[chain, step], maps[chain, steps + step]], axis=1)
-                    pushed = lax.dot_general(
-                        jnp.concatenate([upper, lower], axis=0),
-                        late,
-                        CONTRACT_LAST,
-                        preferred_element_type=f32,
-                    )
-                    for half in range(2):
-                        slot = base + half
-                        at = half * steps + step
-                        fade = fades[chain, pl.ds(at, 1), :]
-                        first_row = half * (size + PAD)
-                        moved = pair[half] * fade + pushed[first_row : first_row + size + PAD]
-                        matrix = moved[0:size]
-                        offset = moved[size:] + drives[chain, pl.ds(at, 1), :]
-                        panels[chain, slot, 0:size, :] = matrix
-                        panels[chain, slot, size : size + PAD, :] = offset
-                        decay = running[chain, slot] * fade
-                        running[chain, slot] = decay
-                        linear_ref[chain, slot, step] = (
-                            matrix - jnp.where(eye, decay, 0.0)
-                        ).astype(bf16)
-                        offset_ref[chain, slot, pl.ds(step, 1), :] = offset[0:1]
-                        fade_ref[chain, slot, pl.ds(step, 1), :] = decay
-
-    for chain in range(chains):
-        panel = panels[chain, quarter]
-        decay = running[chain, quarter]
-        for order in range(1, QUAD):
-            slot = order ^ quarter
-            late = running[chain, slot]
-            pushed = jnp.dot(
-                panel.astype(bf16), linear_ref[chain, slot, steps - 1], preferred_element_type=f32
+        for slot in range(2):
+            panel = panels[chain, slot, 0]
+            decay = running[chain, slot, 0]
+            for part in range(1, PARTS):
+                panel, decay = join_panels(
+                    panel,
+                    decay,
+                    linear_ref[chain, slot, (part + 1) * part_steps - 1],
+                    running[chain, slot, part],
+                    panels[chain, slot, part, size : size + 1, :],
+                )
+            panels[chain, slot, 0] = panel
+            running[chain, slot, 0] = decay
+        first = panels[chain, early, 0], running[chain, early, 0]
+        last_panel, last_decay = panels[chain, 1 - early, 0], running[chain, 1 - early, 0]
+        linear = (last_panel[0:size] - jnp.where(eye, last_decay, 0.0)).astype(bf16)
+        panel, decay = join_panels(*first, linear, last_decay, last_panel[size : size + 1])
+        store_map(early_ref, chain, size, *first)
+        panel_ref[chain] = panel
+        store_map(whole_ref, chain, size, panel, decay)
+
+
+def build_near(near_ref, *refs):
+    build_pair([near_ref[0], near_ref[1]], *refs)
+
+
+def build_far(far_ref, decay_ref, input_ref, tiles_ref, near_panel, near_whole, *refs):
+    *outs, far_whole, quad_ref, far_panel = refs[:7]
+    build_pair(
+        [far_ref[0], far_ref[1]], decay_ref, input_ref, tiles_ref, *outs, far_panel, far_whole, *refs[7:]
+    )
+    size = far_whole.shape[2]
+
+    def join(panel_ref, early_ref, late_ref):
+        for chain in range(far_whole.shape[0]):
+            decay, _ = unpack_map(early_ref, chain, size)
+            late_decay, late_offset = unpack_map(late_ref, chain, size)
+            joined = join_panels(
+                panel_ref[chain], decay, late_ref[chain, 0:size, :], late_decay, late_offset
             )
-            moved = panel * late + pushed
-            panel = jnp.concatenate(
-                [moved[0:size], moved[size:] + panels[chain, slot, size : size + 1, :]], axis=0
-            )
-            decay = decay * late
-        store_map(whole_ref, chain, size, panel, decay)
+            store_map(quad_ref, chain, size, *joined)
+
+    @pl.when(bit_of(1) == 0)
+    def _():
+        join(near_panel, near_whole, far_whole)
+
+    @pl.when(bit_of(1) != 0)
+    def _():
+        join(far_panel, far_whole, near_whole)
+
+
+def join_panels(panel, decay, linear, late_decay, late_offset):
+    size = linear.shape[0]
+    moved = panel * late_decay + jnp.dot(panel.astype(bf16), linear, preferred_element_type=f32)
+    return jnp.concatenate([moved[0:size], moved[size:] + late_offset], axis=0), decay * late_decay
 
 
 def join_maps(level, own_ref, other_ref, out_ref):
@@ -280,11 +296,8 @@
             matrix = early[chain, 0:size, :].astype(f32) + jnp.where(eye, decay, 0.0)
             panel = jnp.concatenate([matrix, jnp.broadcast_to(offset, (PAD, size))], axis=0)
             late_decay, late_offset = unpack_map(late, chain, size)
-            moved = panel * late_decay + jnp.dot(
-                panel.astype(bf16), late[chain, 0:size, :], preferred_element_type=f32
-            )
-            panel = jnp.concatenate([moved[0:size], moved[size:] + late_offset], axis=0)
-            store_map(out_ref, chain, size, panel, decay * late_decay)
+            joined = join_panels(panel, decay, late[chain, 0:size, :], late_decay, late_offset)
+            store_map(out_ref, chain, size, *joined)
 
     @pl.when(bit_of(level) == 0)
     def _():
@@ -315,53 +328,77 @@
 
 
 def run_steps(start_ref, base_ref, *refs):
-    level_refs = refs[:-7]
-    linear_ref, offset_ref, fade_ref, keep_ref, across_ref, later_ref, entries = refs[-7:]
-    chains, _, steps, size, _ = linear_ref.shape
-    quarter = corner_of_quad()
+    keep_ref, across_ref, later_ref, entries = refs[-4:]
+    near, far = refs[-14:-9], refs[-9:-4]
+    level_refs = refs[:-14]
+    chains, _, steps, size, _ = near[0].shape
+    part_steps = steps // PARTS
+    early = corner_of_quad() & 1
     for chain in range(chains):
-        entries[chain, 0] = start_ref[chain]
+        entries[chain, 0, 0, 0] = start_ref[chain]
 
     @pl.when(bit_of(2 + len(level_refs)) != 0)
     def _():
         for chain in range(chains):
-            entries[chain, 0] = base_ref[chain]
+            entries[chain, 0, 0, 0] = base_ref[chain]
 
     for level, ref in reversed(list(enumerate(level_refs))):
 
         @pl.when(bit_of(2 + level) != 0)
         def _():
             for chain in range(chains):
-                entries[chain, 0] = apply_map(ref, chain, size, entries[chain, 0])
-
-    states = [entries[chain, 0] for chain in range(chains)]
-    for order in range(QUAD):
-        slot = order ^ quarter
+                entries[chain, 0, 0, 0] = apply_map(ref, chain, size, entries[chain, 0, 0, 0])
+
+    states = [entries[chain, 0, 0, 0] for chain in range(chains)]
+
+    def enter(pairs):
         for chain in range(chains):
-            entries[chain, slot] = states[chain]
-            if order + 1 < QUAD:
-                states[chain] = (
-                    states[chain] * fade_ref[chain, slot, steps - 1 : steps, :]
-                    + apply_linear(states[chain], linear_ref[chain, slot, steps - 1])
-                    + offset_ref[chain, slot, steps - 1 : steps, :]
+            state = states[chain]
+            following = apply_map(pairs[0][1][4], chain, size, state)
+            for (side, pair), state in zip(pairs, (state, following)):
+                linear_ref, offset_ref, fade_ref, early_ref, _ = pair
+                slots = [(early, state), (1 - early, apply_map(early_ref, chain, size, state))]
+                for slot, state in slots:
+                    entries[chain, side, slot, 0] = state
+                    for part in range(1, PARTS):
+                        at = part * part_steps - 1
+                        state = (
+                            state * fade_ref[chain, slot, at : at + 1, :]
+                            + apply_linear(state, linear_ref[chain, slot, at])
+                            + offset_ref[chain, slot, at : at + 1, :]
+                        )
+                        entries[chain, side, slot, part] = state
+
+    @pl.when(bit_of(1) == 0)
+    def _():
+        enter([(0, near), (1, far)])
+
+    @pl.when(bit_of(1) != 0)
+    def _():
+        enter([(1, far), (0, near)])
+
+    targets = {(0, 0): (keep_ref, 0), (0, 1): (across_ref, 0), (1, 0): (later_ref, 0), (1, 1): (across_ref, 1)}
+    row = row_of((part_steps, size))
+    for (side, slot), (target, place) in targets.items():
+        linear_ref, offset_ref, fade_ref, _, _ = (near, far)[side]
+        for chain in range(chains):
+            for part in range(PARTS):
+                entry = entries[chain, side, slot, part]
+                same = jnp.broadcast_to(entry, (PAD, size)).astype(bf16)
+                at = part * part_steps
+                gathered = (
+                    entry * fade_ref[chain, slot, at : at + part_steps, :]
+                    + offset_ref[chain, slot, at : at + part_steps, :]
                 )
-    targets = {0: (keep_ref, 0), 1: (across_ref, 0), 2: (later_ref, 0), 3: (across_ref, 1)}
-    row = row_of((steps, size))
-    for slot in range(QUAD):
-        target, place = targets[slot]
-        for chain in range(chains):
-            entry = entries[chain, slot]
-            same = jnp.broadcast_to(entry, (PAD, size)).astype(bf16)
-            gathered = entry * fade_ref[chain, slot] + offset_ref[chain, slot]
-            for step in range(0, steps, 2):
-                pair = jnp.concatenate(
-                    [linear_ref[chain, slot, step], linear_ref[chain, slot, step + 1]], axis=1
-                )
-                out = jnp.dot(same, pair, preferred_element_type=f32)
-                for half in range(2):
-                    part = jnp.broadcast_to(out[0:1, half * size : (half + 1) * size], (steps, size))
-                    gathered = gathered + jnp.where(row == step + half, part, 0.0)
-            target[place, chain] = gathered
+                for step in range(0, part_steps, 2):
+                    pair = jnp.concatenate(
+                        [linear_ref[chain, slot, at + step + half] for half in range(2)], axis=1
+                    )
+                    out = jnp.dot(same, pair, preferred_element_type=f32)
+                    for half in range(2):
+                        spread = out[0:part_steps, half * size : (half + 1) * size]
+                        gathered = gathered + jnp.where(row == step + half, spread, 0.0)
+                target[place, chain, at : at + part_steps, :] = gathered
 
 
 def scale_states(keep_ref, across_ref, later_ref, gain_ref, states_ref, packed_ref, table):
@@ -394,29 +431,32 @@
         packed_ref[index * steps : (index + 1) * steps, units : units + size] = extra.astype(bf16)
 
 
-def read_out(states_vmem, own_ref, other_ref, value_ref, gate_ref, states_ref, out_ref, sem):
+def project(packed_ref, core, value_ref, gate_ref):
+    units = value_ref.shape[0] // 2
+    at = pl.ds(pl.multiple_of(core * units, units), units)
+    scaled = packed_ref[:, 0:units]
+    return [
+        jnp.dot(scaled, ref[at, :], preferred_element_type=f32) for ref in (value_ref, gate_ref)
+    ]
+
+
+def read_own(states_vmem, own_ref, value_ref, gate_ref, states_ref, sums_ref, sem):
     copy = pltpu.make_async_copy(states_vmem, states_ref, sem)
     copy.start()
+    for index, total in enumerate(project(own_ref, lax.axis_index("blk"), value_ref, gate_ref)):
+        sums_ref[index] = total
+    copy.wait()
+
+
+def read_out(own_ref, other_ref, sums_ref, value_ref, gate_ref, out_ref):
     units = value_ref.shape[0] // 2
-    core = lax.axis_index("blk")
-    own_at = pl.multiple_of(core * units, units)
-    other_at = pl.multiple_of((1 - core) * units, units)
-    own = own_ref[:, 0:units]
-    other = other_ref[:, 0:units]
     squares = jnp.sum(
         own_ref[:, units:].astype(f32) + other_ref[:, units:].astype(f32), axis=1, keepdims=True
     )
     inverse = lax.rsqrt(squares / value_ref.shape[0] + EPS)
-
-    def project(ref):
-        return jnp.dot(own, ref[pl.ds(own_at, units), :], preferred_element_type=f32) + jnp.dot(
-            other, ref[pl.ds(other_at, units), :], preferred_element_type=f32
-        )
-
-    value = project(value_ref) * inverse
-    gate = project(gate_ref) * inverse
+    other = project(other_ref, 1 - lax.axis_index("blk"), value_ref, gate_ref)
+    value, gate = ((sums_ref[index] + other[index]) * inverse for index in range(2))
     out_ref[...] = (value * jax.nn.sigmoid(gate)).astype(bf16)
-    copy.wait()
 
 
 def body(
@@ -475,37 +515,39 @@
     )
     near, tiles = lax.optimization_barrier((near, tiles))
     far = partner(near, "tm", 2)
-    formed = (
+    pair_shapes = (
+        jax.ShapeDtypeStruct((chains, 2, steps, size, size), bf16),
+        jax.ShapeDtypeStruct((chains, 2, steps, size), f32),
+        jax.ShapeDtypeStruct((chains, 2, steps, size), f32),
+        jax.ShapeDtypeStruct((chains, size + PAD, size), bf16),
+        jax.ShapeDtypeStruct((chains, size + PAD, size), f32),
+        jax.ShapeDtypeStruct((chains, size + PAD, size), bf16),
+    )
+    pair_scratch = [
         pltpu.VMEM((chains, total, size, size), bf16),
         pltpu.VMEM((chains, total, size), f32),
         pltpu.VMEM((chains, total, size), f32),
-    )
-    near_formed = pl.pallas_call(
-        form_near,
-        out_shape=tuple(jax.ShapeDtypeStruct(item.shape, item.dtype) for item in formed),
+        pltpu.VMEM((chains, 2, PARTS, size + PAD, size), f32),
+        pltpu.VMEM((chains, 2, PARTS, 1, size), f32),
+    ]
+    *near_maps, near_panel, near_whole = pl.pallas_call(
+        build_near,
+        out_shape=pair_shapes,
         in_specs=[VMEM_SPEC] * 4,
-        out_specs=(VMEM_SPEC,) * 3,
-        compiler_params=params(16),
-        name="form_near",
+        out_specs=(VMEM_SPEC,) * 6,
+        scratch_shapes=pair_scratch,
+        compiler_params=params(20),
+        name="build_near",
     )(near, decays, inputs, tiles)
-    linear, offset, fade, whole = pl.pallas_call(
-        build_maps,
-        out_shape=(
-            jax.ShapeDtypeStruct((chains, QUAD, steps, size, size), bf16),
-            jax.ShapeDtypeStruct((chains, QUAD, steps, size), f32),
-            jax.ShapeDtypeStruct((chains, QUAD, steps, size), f32),
-            jax.ShapeDtypeStruct((chains, size + PAD, size), bf16),
-        ),
-        in_specs=[VMEM_SPEC] * 7,
-        out_specs=(VMEM_SPEC,) * 4,
-        scratch_shapes=[
-            *formed,
-            pltpu.VMEM((chains, QUAD, size + PAD, size), f32),
-            pltpu.VMEM((chains, QUAD, 1, size), f32),
-        ],
-        compiler_params=params(24),
-        name="build_maps",
-    )(far, decays, inputs, tiles, *near_formed)
+    *far_maps, far_whole, whole = pl.pallas_call(
+        build_far,
+        out_shape=pair_shapes[:4] + pair_shapes[5:] * 2,
+        in_specs=[VMEM_SPEC] * 6,
+        out_specs=(VMEM_SPEC,) * 6,
+        scratch_shapes=[pltpu.VMEM(pair_shapes[4].shape, f32)] + pair_scratch,
+        compiler_params=params(20),
+        name="build_far",
+    )(far, decays, inputs, tiles, near_panel, near_whole)
 
     earlier = []
     for level in range(2, bits - 1):
@@ -538,18 +580,19 @@
             jax.ShapeDtypeStruct((2,) + piece, f32),
             jax.ShapeDtypeStruct((1,) + piece, f32),
         ),
-        in_specs=[VMEM_SPEC] * (5 + len(earlier)),
+        in_specs=[VMEM_SPEC] * (12 + len(earlier)),
         out_specs=(VMEM_SPEC,) * 3,
-        scratch_shapes=[pltpu.VMEM((chains, QUAD, 1, size), f32)],
+        scratch_shapes=[pltpu.VMEM((chains, 2, 2, PARTS, 1, size), f32)],
         compiler_params=params(16),
         name="run_steps",
     )(
         start,
         base,
         *earlier,
-        linear,
-        offset,
-        fade,
+        *near_maps,
+        near_whole,
+        *far_maps,
+        far_whole,
     )
     across = partner(across, "tm", 1)
     later = partner(jnp.concatenate([later, across[1:2]], axis=0), "tm", 2)
@@ -569,18 +612,26 @@
     )(keep, across, later, gain.reshape(1, local_units))
     packed_other = partner(packed, "blk", 1)
     features = value_weight.shape[1]
-    states, readout = pl.pallas_call(
-        read_out,
+    states, sums = pl.pallas_call(
+        read_own,
         out_shape=(
             jax.ShapeDtypeStruct((records, steps, local_units), f32),
-            jax.ShapeDtypeStruct((rows, features), bf16),
+            jax.ShapeDtypeStruct((2, rows, features), f32),
         ),
-        in_specs=[VMEM_SPEC] * 5,
+        in_specs=[VMEM_SPEC] * 4,
         out_specs=(HBM_SPEC, VMEM_SPEC),
         scratch_shapes=[pltpu.SemaphoreType.DMA(())],
         compiler_params=params(16),
+        name="read_own",
+    )(states, packed, value_weight, gate_weight)
+    readout = pl.pallas_call(
+        read_out,
+        out_shape=jax.ShapeDtypeStruct((rows, features), bf16),
+        in_specs=[VMEM_SPEC] * 5,
+        out_specs=VMEM_SPEC,
+        compiler_params=params(16),
         name="read_out",
-    )(states, packed, packed_other, value_weight, gate_weight)
+    )(packed, packed_other, sums, value_weight, gate_weight)
     return (states, readout.reshape(records, steps, features))
 
 

time: 36.6 us -> 34.4 us (0.940)
  starting transfers between devices: 14 us -> 11.8 us
  Pallas kernels: 11.4 us -> 10.5 us
  waiting for transfers between devices: 9.45 us -> 10.3 us
    ppermute x7, starting transfers between devices: 14 us -> 11.8 us  [partner(): lax.ppermute(array, axis, [(i, i ^ flip) for i in range(lax.axis_size(axi...]
    pallas_call x3 -> x4, Pallas kernels: 8.36 us -> 7.02 us  [the longest x1 2.81 us: body(): pl.pallas_call(build_far, out_shape=pair_shapes[:4] + pair_shapes[5:] * 2...]
    ppermute x7, waiting for transfers between devices: 9.45 us -> 10.3 us  [partner(): lax.ppermute(array, axis, [(i, i ^ flip) for i in range(lax.axis_size(axi...]
  transfers between devices with their start and end apart: 7 -> 7, of which waited for: 6 -> 5; matrix products, arithmetic and copies ran while one was open for 0% -> 0% of each run, Pallas kernels for 9% -> 15%
where the time goes in v2:
time: 34.4 us; the launch traced here: 34.2 us
  starting transfers between devices  11.8 us (34%)
  Pallas kernels  10.5 us (31%)
  waiting for transfers between devices  10.3 us (30%)
  between operations  0.76 us (2%)
  other arithmetic  0.74 us (2%)
    ppermute x7, starting transfers between devices, partner(): lax.ppermute(array, axis, [(i, i ^ flip) for i in range(lax.axis_size(axi...  11.8 us
    ppermute x7, waiting for transfers between devices, partner(): lax.ppermute(array, axis, [(i, i ^ flip) for i in range(lax.axis_size(axi...  10.3 us
    pallas_call x1, Pallas kernels, body(): pl.pallas_call(build_far, out_shape=pair_shapes[:4] + pair_shapes[5:] * 2...  2.81 us
    pallas_call x1, Pallas kernels, body(): pl.pallas_call(build_near, out_shape=pair_shapes, in_specs=[VMEM_SPEC] *...  2.62 us
    pallas_call x1, Pallas kernels, body(): pl.pallas_call(stage_inputs, out_shape=(jax.ShapeDtypeStruct((chains, siz...  1.87 us
    pallas_call x1, Pallas kernels, body(): pl.pallas_call(run_steps, out_shape=(jax.ShapeDtypeStruct((1,) + piece, f...  1.23 us
    pallas_call x1, Pallas kernels, body(): pl.pallas_call(read_out, out_shape=jax.ShapeDtypeStruct((rows, features),...  0.92 us
    concatenate x1, other arithmetic, body(): path = jnp.concatenate([increments, step_sizes[:, None, :]], axis=1)  0.73 us
  transfers between devices with their start and end apart: 7, of which 5 were waited for; matrix products, arithmetic and copies ran while one was open for 0% of the time, Pallas kernels for 15%

profile of v2, /device:TPU:0, one launch (start us, length us, event | category | flops | bytes accessed | tf_op | source)
XLA Modules:
  0.0 34.2 jit_solution(12260386210060069636)
XLA Ops:
  0.7 0.7 %fusion.2 = (f32[1,17,16]{2,1,0:T(8,128)S(1)}, f32[17,16]{1,0:T(8,128)S(1)}) fusion(s32[]{:T(128)S(6)} %select_n.20, f32[2,16,16]{2,1,0:T(8,128)} %param.12, f32[2,1,16]{2,1,0:T(1,128)} %bitcast.13, s32[]{:T(128)S(6)} %select_n.21), kind=kLoop, calls=%fused_computation.8 | loop fusion | flops 544 | bytes 4360 | tf_op jit(solution)/shard_map/concatenate | solution.py:485
  1.4 3.0 %collective-permute-start = (f32[17,16]{1,0:T(8,128)S(1)}, f32[17,16]{1,0:T(8,128)S(1)}, u32[]{:S(2)}, u32[]{:S(2)}) collective-permute-start(f32[17,16]{1,0:T(8,128)S(1)} %get-tuple-element.53), channel_id=1, source_target_pairs={{0,2},{2,0},{4,6},{6,4},{8,10},{10,8},{12,14},{14,12},{16,18},{18,... | collective-permute-start | bytes 3272 | tf_op jit(solution)/shard_map/ppermute | solution.py:26
  4.4 1.9 %stage_inputs.1 = (bf16[2,8,128,256]{3,2,1,0:T(8,128)(2,1)S(1)}, f32[2,1,128]{2,1,0:T(1,128)S(1)}, f32[2,16,128]{2,1,0:T(8,128)S(1)}, f32[2,1,128]{2,1,0:T(1,128)S(1)}) custom-call(f32[1,512]{1,0:T(1,128)} %bitcast.12, f32[16,512]{1,0:T(8,128)} %input_ref.1, f32[2,512]{1,0:T(2,128)} %initial_ref.1, f32[16,4,128,128]{3,2,1,0:T(8,128)} %coupling_ref.1), custom_call_target="tpu_custom_call" | custom-call | tf_op jit(solution)/shard_map/stage_inputs/pallas_call | solution.py:491
  6.2 0.0 collective-permute-done
  6.3 1.8 %collective-permute-start.1 = (f32[2,17,16]{2,1,0:T(8,128)S(1)}, f32[2,17,16]{2,1,0:T(8,128)S(1)}, u32[]{:S(2)}, u32[]{:S(2)}) collective-permute-start(f32[2,17,16]{2,1,0:T(8,128)S(1)} %pad_maximum_fusion.1.near_ref), channel_id=1, source_target_pairs={{0,4},{2,6},{4,0},{6,2},{8,12},{10,14},{12,8},{14,10},{16,20},{18,... | collective-permute-start | bytes 6536 | tf_op jit(solution)/shard_map/ppermute | solution.py:26
  8.1 2.6 %build_near.1 = (bf16[2,2,16,128,128]{4,3,2,1,0:T(8,128)(2,1)S(1)}, f32[2,2,16,128]{3,2,1,0:T(8,128)S(1)}, f32[2,2,16,128]{3,2,1,0:T(8,128)S(1)}, bf16[2,144,128...) custom-call(f32[2,17,16]{2,1,0:T(8,128)S(1)} %pad_maximum_fusion.1.near_ref, ...), custom_call_target="tpu_custom_call" | custom-call | tf_op jit(solution)/shard_map/build_near/pallas_call | solution.py:533
  10.7 0.0 collective-permute-done.1.far_ref
  10.7 2.8 %build_far.1 = (bf16[2,2,16,128,128]{4,3,2,1,0:T(8,128)(2,1)S(1)}, f32[2,2,16,128]{3,2,1,0:T(8,128)S(1)}, f32[2,2,16,128]{3,2,1,0:T(8,128)S(1)}, bf16[2,144,128]...) custom-call(f32[2,17,16]{2,1,0:T(8,128)S(1)} %collective-permute-done.1.far_ref, ...), custom_call_target="tpu_custom_call" | custom-call | tf_op jit(solution)/shard_map/build_far/pallas_call | solution.py:542
  13.5 1.6 %collective-permute-start.2 = (bf16[2,144,128]{2,1,0:T(8,128)(2,1)S(1)}, bf16[2,144,128]{2,1,0:T(8,128)(2,1)S(1)}, u32[]{:S(2)}, u32[]{:S(2)}) collective-permute-start(bf16[2,144,128]{2,1,0:T(8,128)(2,1)S(1)} %get-tuple-element.35.own_ref), channel_id=1, source_target_pairs={{0,8},{2,10},{4,12},{6,14},{8,0},{10,2},{12,4},{14,6},{16,24},{18,... | collective-permute-start | bytes 221192 | tf_op jit(solution)/shard_map/ppermute | solution.py:26
  15.2 2.8 %collective-permute-done.2.other_ref.refs_0_ = bf16[2,144,128]{2,1,0:T(8,128)(2,1)S(1)} collective-permute-done((bf16[2,144,128]{2,1,0:T(8,128)(2,1)S(1)}, bf16[2,144,128]{2,1,0:T(8,128)(2,1)S(1)}, u32[]{:S(2)}, u32[]{:S(2)}) %collective-permute-start.2) | collective-permute-done | bytes 73760 | tf_op jit(solution)/shard_map/ppermute | solution.py:26
  18.0 0.3 cross_pair.1
  18.2 2.6 %collective-permute-start.3 = (f32[2,1,128]{2,1,0:T(1,128)S(1)}, f32[2,1,128]{2,1,0:T(1,128)S(1)}, u32[]{:S(2)}, u32[]{:S(2)}) collective-permute-start(f32[2,1,128]{2,1,0:T(1,128)S(1)} %cross_pair.1), channel_id=1, source_target_pairs={{0,16},{2,18},{4,20},{6,22},{8,24},{10,26},{12,28},{14,30},{16,0},... | collective-permute-start | bytes 3080 | tf_op jit(solution)/shard_map/ppermute | solution.py:26
  20.8 1.9 %collective-permute-done.3.base_ref = f32[2,1,128]{2,1,0:T(1,128)S(1)} collective-permute-done((f32[2,1,128]{2,1,0:T(1,128)S(1)}, f32[2,1,128]{2,1,0:T(1,128)S(1)}, u32[]{:S(2)}, u32[]{:S(2)}) %collective-permute-start.3) | collective-permute-done | bytes 1056 | tf_op jit(solution)/shard_map/ppermute | solution.py:26
  22.7 0.0 copy-start.2
  22.7 0.0 copy-start
  22.7 0.0 copy-start.1
  22.7 1.2 %run_steps.1 = (f32[1,2,16,128]{3,2,1,0:T(8,128)S(1)}, f32[2,2,16,128]{3,2,1,0:T(8,128)S(1)}, f32[1,2,16,128]{3,2,1,0:T(8,128)S(1)}) custom-call(f32[2,1,128]{2,1,0:T(1,128)S(1)} %get-tuple-element.27.start_ref, f32[2,1,128]{2,1,0:T(1,128)S(1)} %collective-permute-done.3.base_ref, bf16[2,144,128]{2,1,0:T(8,128)(2,1)S(1)} %collective-permute-done.2.other_ref.refs_0_, ...), custom_call_target="tpu_custom_call" | custom-call | tf_op jit(solution)/shard_map/run_steps/pallas_call | solution.py:576
  24.0 1.5 %collective-permute-start.4 = (f32[2,2,16,128]{3,2,1,0:T(8,128)S(1)}, f32[2,2,16,128]{3,2,1,0:T(8,128)S(1)}, u32[]{:S(2)}, u32[]{:S(2)}) collective-permute-start(f32[2,2,16,128]{3,2,1,0:T(8,128)S(1)} %get-tuple-element.46), channel_id=1, source_target_pairs={{0,2},{2,0},{4,6},{6,4},{8,10},{10,8},{12,14},{14,12},{16,18},{18,... | collective-permute-start | bytes 98312 | tf_op jit(solution)/shard_map/ppermute | solution.py:26
  25.5 2.4 %collective-permute-done.4.across_ref = f32[2,2,16,128]{3,2,1,0:T(8,128)S(1)} collective-permute-done((f32[2,2,16,128]{3,2,1,0:T(8,128)S(1)}, f32[2,2,16,128]{3,2,1,0:T(8,128)S(1)}, u32[]{:S(2)}, u32[]{:S(2)}) %collective-permute-start.4) | collective-permute-done | bytes 32800 | tf_op jit(solution)/shard_map/ppermute | solution.py:26
  27.9 1.2 %collective-permute-start.5 = (f32[2,2,16,128]{3,2,1,0:T(8,128)S(1)}, f32[2,2,16,128]{3,2,1,0:T(8,128)S(1)}, u32[]{:S(2)}, u32[]{:S(2)}) collective-permute-start(f32[2,2,16,128]{3,2,1,0:T(8,128)S(1)} %pad_maximum_fusion), channel_id=1, source_target_pairs={{0,4},{2,6},{4,0},{6,2},{8,12},{10,14},{12,8},{14,10},{16,20},{18,... | collective-permute-start | bytes 98312 | tf_op jit(solution)/shard_map/ppermute | solution.py:26
  29.1 2.7 %collective-permute-done.5.later_ref = f32[2,2,16,128]{3,2,1,0:T(8,128)S(1)} collective-permute-done((f32[2,2,16,128]{3,2,1,0:T(8,128)S(1)}, f32[2,2,16,128]{3,2,1,0:T(8,128)S(1)}, u32[]{:S(2)}, u32[]{:S(2)}) %collective-permute-start.5) | collective-permute-done | bytes 32800 | tf_op jit(solution)/shard_map/ppermute | solution.py:26
  31.8 0.0 copy-done.2
  31.8 0.1 scale_states.1
  32.0 0.1 collective-permute-start.6
  32.0 0.0 copy-done
  32.0 0.0 copy-done.1
  32.1 0.7 %read_own.1 = (f32[2,16,512]{2,1,0:T(8,128)}, f32[2,32,512]{2,1,0:T(8,128)S(1)}) custom-call(f32[2,16,512]{2,1,0:T(8,128)S(1)} %get-tuple-element.48.states_vmem, bf16[32,640]{1,0:T(8,128)(2,1)S(1)} %get-tuple-element.49.own_ref, bf16[1024,512]{1,0:T(8,128)(2,1)S(1)} %copy-done, bf16[1024,512]{1,0:T(8,128)(2,1)S(1)} %copy-done.1), custom_call_target="tpu_custom_call" | custom-call | tf_op jit(solution)/shard_map/read_own/pallas_call | solution.py:615
  32.7 0.5 %collective-permute-done.6.other_ref = bf16[32,640]{1,0:T(8,128)(2,1)S(1)} collective-permute-done((bf16[32,640]{1,0:T(8,128)(2,1)S(1)}, bf16[32,640]{1,0:T(8,128)(2,1)S(1)}, u32[]{:S(2)}, u32[]{:S(2)}) %collective-permute-start.6) | collective-permute-done | bytes 40992 | tf_op jit(solution)/shard_map/ppermute | solution.py:26
  33.2 0.9 %read_out.1 = bf16[32,512]{1,0:T(8,128)(2,1)} custom-call(bf16[32,640]{1,0:T(8,128)(2,1)S(1)} %get-tuple-element.49.own_ref, bf16[32,640]{1,0:T(8,128)(2,1)S(1)} %collective-permute-done.6.other_ref, f32[2,32,512]{2,1,0:T(8,128)S(1)} %get-tuple-element.51.sums_ref, bf16[1024,512]{1,0:T(8,128)(2,1)S(1)} %copy-done, bf16[1024,512]{1,0:T(8,128)(2,1)S(1)} %copy-done.1), custom_call_target="tpu_custom_call" | custom-call | tf_op jit(solution)/shard_map/read_out/pallas_call | solution.py:627
  (3 shorter events, 0.0 us)
Async XLA Ops:
  1.4 4.8 %collective-permute-start = (f32[17,16]{1,0:T(8,128)S(1)}, f32[17,16]{1,0:T(8,128)S(1)}, u32[]{:S(2)}, u32[]{:S(2)}) collective-permute-start(f32[17,16]{1,0:T(8,128)S(1)} %get-tuple-element.53), channel_id=1, source_target_pairs={{0,2},{2,0},{4,6},{6,4},{8,10},{10,8},{12,14},{14,12},{16,18},{18,... | collective-permute-start | bytes 3272 | tf_op jit(solution)/shard_map/ppermute | solution.py:26
  6.3 4.5 %collective-permute-start.1 = (f32[2,17,16]{2,1,0:T(8,128)S(1)}, f32[2,17,16]{2,1,0:T(8,128)S(1)}, u32[]{:S(2)}, u32[]{:S(2)}) collective-permute-start(f32[2,17,16]{2,1,0:T(8,128)S(1)} %pad_maximum_fusion.1.near_ref), channel_id=1, source_target_pairs={{0,4},{2,6},{4,0},{6,2},{8,12},{10,14},{12,8},{14,10},{16,20},{18,... | collective-permute-start | bytes 6536 | tf_op jit(solution)/shard_map/ppermute | solution.py:26
  13.5 4.4 %collective-permute-start.2 = (bf16[2,144,128]{2,1,0:T(8,128)(2,1)S(1)}, bf16[2,144,128]{2,1,0:T(8,128)(2,1)S(1)}, u32[]{:S(2)}, u32[]{:S(2)}) collective-permute-start(bf16[2,144,128]{2,1,0:T(8,128)(2,1)S(1)} %get-tuple-element.35.own_ref), channel_id=1, source_target_pairs={{0,8},{2,10},{4,12},{6,14},{8,0},{10,2},{12,4},{14,6},{16,24},{18,... | collective-permute-start | bytes 221192 | tf_op jit(solution)/shard_map/ppermute | solution.py:26
  18.2 4.5 %collective-permute-start.3 = (f32[2,1,128]{2,1,0:T(1,128)S(1)}, f32[2,1,128]{2,1,0:T(1,128)S(1)}, u32[]{:S(2)}, u32[]{:S(2)}) collective-permute-start(f32[2,1,128]{2,1,0:T(1,128)S(1)} %cross_pair.1), channel_id=1, source_target_pairs={{0,16},{2,18},{4,20},{6,22},{8,24},{10,26},{12,28},{14,30},{16,0},... | collective-permute-start | bytes 3080 | tf_op jit(solution)/shard_map/ppermute | solution.py:26
  22.7 9.1 %copy-start.2 = (f32[512]{0:T(512)S(1)}, f32[512]{0:T(512)}, u32[]{:S(2)}) copy-start(f32[512]{0:T(512)} %param.15) | copy-start | bytes 6148
  22.7 9.3 %copy-start = (bf16[1024,512]{1,0:T(8,128)(2,1)S(1)}, bf16[1024,512]{1,0:T(8,128)(2,1)}, u32[]{:S(2)}) copy-start(bf16[1024,512]{1,0:T(8,128)(2,1)} %value_ref.3) | copy-start | bytes 3145732
  22.7 9.3 %copy-start.1 = (bf16[1024,512]{1,0:T(8,128)(2,1)S(1)}, bf16[1024,512]{1,0:T(8,128)(2,1)}, u32[]{:S(2)}) copy-start(bf16[1024,512]{1,0:T(8,128)(2,1)} %gate_ref.3) | copy-start | bytes 3145732
  24.0 4.0 %collective-permute-start.4 = (f32[2,2,16,128]{3,2,1,0:T(8,128)S(1)}, f32[2,2,16,128]{3,2,1,0:T(8,128)S(1)}, u32[]{:S(2)}, u32[]{:S(2)}) collective-permute-start(f32[2,2,16,128]{3,2,1,0:T(8,128)S(1)} %get-tuple-element.46), channel_id=1, source_target_pairs={{0,2},{2,0},{4,6},{6,4},{8,10},{10,8},{12,14},{14,12},{16,18},{18,... | collective-permute-start | bytes 98312 | tf_op jit(solution)/shard_map/ppermute | solution.py:26
  27.9 3.9 %collective-permute-start.5 = (f32[2,2,16,128]{3,2,1,0:T(8,128)S(1)}, f32[2,2,16,128]{3,2,1,0:T(8,128)S(1)}, u32[]{:S(2)}, u32[]{:S(2)}) collective-permute-start(f32[2,2,16,128]{3,2,1,0:T(8,128)S(1)} %pad_maximum_fusion), channel_id=1, source_target_pairs={{0,4},{2,6},{4,0},{6,2},{8,12},{10,14},{12,8},{14,10},{16,20},{18,... | collective-permute-start | bytes 98312 | tf_op jit(solution)/shard_map/ppermute | solution.py:26
  32.0 1.3 %collective-permute-start.6 = (bf16[32,640]{1,0:T(8,128)(2,1)S(1)}, bf16[32,640]{1,0:T(8,128)(2,1)S(1)}, u32[]{:S(2)}, u32[]{:S(2)}) collective-permute-start(bf16[32,640]{1,0:T(8,128)(2,1)S(1)} %get-tuple-element.49.own_ref), channel_id=1, source_target_pairs={{0,1},{1,0},{2,3},{3,2},{4,5},{5,4},{6,7},{7,6},{8,9},{9,8},{10,11... | collective-permute-start | bytes 122888 | tf_op jit(solution)/shard_map/ppermute | solution.py:26

commit v3 on v2

--- a/solution.py
+++ b/solution.py
@@ -45,13 +45,10 @@
     return lax.broadcasted_iota(jnp.int32, shape, 0)
 
 
-def apply_linear(state, weights):
+def split_state(state):
     high = state.astype(bf16).astype(f32)
-    low = state - high
     row = row_of((PAD, state.shape[1]))
-    stacked = jnp.where(row == 0, high, jnp.where(row == 1, low, 0.0)).astype(bf16)
-    out = jnp.dot(stacked, weights, preferred_element_type=f32)
-    return out[0:1] + out[1:2]
+    return jnp.where(row == 0, high, jnp.where(row == 1, state - high, 0.0)).astype(bf16)
 
 
 def unpack_map(ref, chain, size):
@@ -63,17 +60,36 @@
 
 def apply_map(ref, chain, size, state):
     decay, offset = unpack_map(ref, chain, size)
-    return state * decay + apply_linear(state, ref[chain, 0:size, :]) + offset
+    out = jnp.dot(split_state(state), ref[chain, 0:size, :], preferred_element_type=f32)
+    return state * decay + out[0:1] + out[1:2] + offset
+
+
+def panel_of(ref, chain, size):
+    decay, offset = unpack_map(ref, chain, size)
+    eye = row_of((size, size)) == lax.broadcasted_iota(jnp.int32, (size, size), 1)
+    matrix = ref[chain, 0:size, :].astype(f32) + jnp.where(eye, decay, 0.0)
+    return jnp.concatenate([matrix, jnp.broadcast_to(offset, (PAD, size))], axis=0), decay
+
+
+def join_packed(panel, decay, ref, chain, size):
+    late_decay, late_offset = unpack_map(ref, chain, size)
+    return join_panels(panel, decay, ref[chain, 0:size, :], late_decay, late_offset)
+
+
+def pack_map(ref, chain, linear, decay, offset):
+    size = linear.shape[0]
+    ref[chain, 0:size, :] = linear
+    row = row_of((PAD, size))
+    extra = jnp.zeros((PAD, size), f32)
+    for at, value in enumerate(pieces(decay) + pieces(offset)):
+        extra = jnp.where(row == at, value, extra)
+    ref[chain, size : size + PAD, :] = extra.astype(bf16)
 
 
 def store_map(ref, chain, size, panel, decay):
     eye = row_of((size, size)) == lax.broadcasted_iota(jnp.int32, (size, size), 1)
-    ref[chain, 0:size, :] = (panel[0:size] - jnp.where(eye, decay, 0.0)).astype(bf16)
-    row = row_of((PAD, size))
-    extra = jnp.zeros((PAD, size), f32)
-    for at, value in enumerate(pieces(decay) + pieces(panel[size : size + 1])):
-        extra = jnp.where(row == at, value, extra)
-    ref[chain, size : size + PAD, :] = extra.astype(bf16)
+    linear = (panel[0:size] - jnp.where(eye, decay, 0.0)).astype(bf16)
+    pack_map(ref, chain, linear, decay, panel[size : size + 1])
 
 
 def stage_inputs(
@@ -183,14 +199,11 @@
     linear_ref,
     offset_ref,
     fade_ref,
-    early_ref,
-    panel_ref,
-    whole_ref,
+    panels,
+    running,
     maps,
     fades,
     drives,
-    panels,
-    running,
 ):
     form_steps(slots, decay_ref, input_ref, tiles_ref, maps, fades, drives)
     chains, _, steps, size, _ = linear_ref.shape
@@ -227,49 +240,79 @@
             linear = (matrix - jnp.where(eye, decay, 0.0)).astype(bf16)
             keep(chain, slot, part, step, linear, offset[0:1], decay)
 
+
+def join_pairs(pairs):
+    chains, _, steps, size, _ = pairs[0][0].shape
+    part_steps = steps // PARTS
+    eye = row_of((size, size)) == lax.broadcasted_iota(jnp.int32, (size, size), 1)
     early = corner_of_quad() & 1
-    for chain in range(chains):
-        for slot in range(2):
-            panel = panels[chain, slot, 0]
-            decay = running[chain, slot, 0]
-            for part in range(1, PARTS):
-                panel, decay = join_panels(
-                    panel,
-                    decay,
-                    linear_ref[chain, slot, (part + 1) * part_steps - 1],
-                    running[chain, slot, part],
-                    panels[chain, slot, part, size : size + 1, :],
-                )
-            panels[chain, slot, 0] = panel
-            running[chain, slot, 0] = decay
-        first = panels[chain, early, 0], running[chain, early, 0]
-        last_panel, last_decay = panels[chain, 1 - early, 0], running[chain, 1 - early, 0]
-        linear = (last_panel[0:size] - jnp.where(eye, last_decay, 0.0)).astype(bf16)
-        panel, decay = join_panels(*first, linear, last_decay, last_panel[size : size + 1])
-        store_map(early_ref, chain, size, *first)
+    places = [(pair, chain, turn) for pair in range(len(pairs)) for chain in range(chains) for turn in range(2)]
+    wholes = {}
+    for place in places:
+        pair, chain, turn = place
+        panels, running = pairs[pair][4:]
+        slot = turn ^ early
+        wholes[place] = panels[chain, slot, 0], running[chain, slot, 0]
+    for part in range(1, PARTS):
+        for place in places:
+            pair, chain, turn = place
+            linear_ref, (panels, running) = pairs[pair][0], pairs[pair][4:]
+            slot = turn ^ early
+            wholes[place] = join_panels(
+                *wholes[place],
+                linear_ref[chain, slot, (part + 1) * part_steps - 1],
+                running[chain, slot, part],
+                panels[chain, slot, part, size : size + 1, :],
+            )
+    joined = {}
+    for pair, chain, turn in places:
+        if turn == 0:
+            panel, decay = wholes[pair, chain, 1]
+            linear = (panel[0:size] - jnp.where(eye, decay, 0.0)).astype(bf16)
+            joined[pair, chain] = join_panels(
+                *wholes[pair, chain, 0], linear, decay, panel[size : size + 1]
+            )
+    for (pair, chain), (panel, decay) in joined.items():
+        _, early_ref, panel_ref, whole_ref, _, _ = pairs[pair]
         panel_ref[chain] = panel
         store_map(whole_ref, chain, size, panel, decay)
+        store_map(early_ref, chain, size, *wholes[pair, chain, 0])
 
 
 def build_near(near_ref, *refs):
     build_pair([near_ref[0], near_ref[1]], *refs)
 
 
-def build_far(far_ref, decay_ref, input_ref, tiles_ref, near_panel, near_whole, *refs):
-    *outs, far_whole, quad_ref, far_panel = refs[:7]
+def build_far(far_ref, decay_ref, input_ref, tiles_ref, near_linear, near_panels, near_running, *refs):
+    linear_ref, offset_ref, fade_ref, near_early, near_whole, far_early, far_whole, quad_ref = refs[:8]
+    near_panel, far_panel, panels, running, *scratch = refs[8:]
     build_pair(
-        [far_ref[0], far_ref[1]], decay_ref, input_ref, tiles_ref, *outs, far_panel, far_whole, *refs[7:]
+        [far_ref[0], far_ref[1]],
+        decay_ref,
+        input_ref,
+        tiles_ref,
+        linear_ref,
+        offset_ref,
+        fade_ref,
+        panels,
+        running,
+        *scratch,
+    )
+    join_pairs(
+        [
+            (near_linear, near_early, near_panel, near_whole, near_panels, near_running),
+            (linear_ref, far_early, far_panel, far_whole, panels, running),
+        ]
     )
     size = far_whole.shape[2]
 
     def join(panel_ref, early_ref, late_ref):
+        joined = []
         for chain in range(far_whole.shape[0]):
             decay, _ = unpack_map(early_ref, chain, size)
-            late_decay, late_offset = unpack_map(late_ref, chain, size)
-            joined = join_panels(
-                panel_ref[chain], decay, late_ref[chain, 0:size, :], late_decay, late_offset
-            )
-            store_map(quad_ref, chain, size, *joined)
+            joined.append(join_packed(panel_ref[chain], decay, late_ref, chain, size))
+        for chain, (panel, decay) in enumerate(joined):
+            store_map(quad_ref, chain, size, panel, decay)
 
     @pl.when(bit_of(1) == 0)
     def _():
@@ -291,13 +334,7 @@
 
     def join(early, late):
         for chain in range(own_ref.shape[0]):
-            decay, offset = unpack_map(early, chain, size)
-            eye = row_of((size, size)) == lax.broadcasted_iota(jnp.int32, (size, size), 1)
-            matrix = early[chain, 0:size, :].astype(f32) + jnp.where(eye, decay, 0.0)
-            panel = jnp.concatenate([matrix, jnp.broadcast_to(offset, (PAD, size))], axis=0)
-            late_decay, late_offset = unpack_map(late, chain, size)
-            joined = join_panels(panel, decay, late[chain, 0:size, :], late_decay, late_offset)
-            store_map(out_ref, chain, size, *joined)
+            store_map(out_ref, chain, size, *join_packed(*panel_of(early, chain, size), late, chain, size))
 
     @pl.when(bit_of(level) == 0)
     def _():
@@ -313,10 +350,11 @@
     chains = own_ref.shape[0]
 
     def cross(early, late):
-        for chain in range(chains):
-            state = start_ref[chain]
-            state = apply_map(early, chain, size, state)
-            out_ref[chain] = apply_map(late, chain, size, state)
+        states = [start_ref[chain] for chain in range(chains)]
+        for ref in (early, late):
+            states = [apply_map(ref, chain, size, state) for chain, state in enumerate(states)]
+        for chain, state in enumerate(states):
+            out_ref[chain] = state
 
     @pl.when(bit_of(level) == 0)
     def _():
@@ -327,60 +365,96 @@
         cross(other_ref, own_ref)
 
 
-def run_steps(start_ref, base_ref, *refs):
-    keep_ref, across_ref, later_ref, entries = refs[-4:]
-    near, far = refs[-14:-9], refs[-9:-4]
-    level_refs = refs[:-14]
+def lay_routes(*refs):
+    near, far, routes_ref = refs[0:5], refs[5:10], refs[10]
+    chains, _, steps, size, _ = near[0].shape
+    last = steps // PARTS - 1
+    early = corner_of_quad() & 1
+    parts = 2 * PARTS
+
+    def lay(pairs):
+        for chain in range(chains):
+            for order, (linear_ref, offset_ref, fade_ref, early_ref, _) in enumerate(pairs):
+                before = pairs[0][4] if order else None
+                if before is not None:
+                    routes_ref[chain, parts - 1] = before[chain]
+                for second in range(2):
+                    slot = 1 - early if second else early
+                    at = order * parts + second * PARTS
+                    maps = []
+                    if order:
+                        maps.append(panel_of(before, chain, size))
+                    if second:
+                        maps = [
+                            join_packed(*maps[0], early_ref, chain, size)
+                            if maps
+                            else panel_of(early_ref, chain, size)
+                        ]
+                        store_map(routes_ref.at[chain], at - 1, size, *maps[0])
+                    for part in range(1, PARTS):
+                        place = part * (last + 1) - 1
+                        linear = linear_ref[chain, slot, place]
+                        fade = fade_ref[chain, slot, place : place + 1, :]
+                        offset = offset_ref[chain, slot, place : place + 1, :]
+                        if maps:
+                            maps = [join_panels(*maps[0], linear, fade, offset)]
+                            store_map(routes_ref.at[chain], at + part - 1, size, *maps[0])
+                        else:
+                            pack_map(routes_ref.at[chain], at + part - 1, linear, fade, offset)
+                            maps = []
+
+    @pl.when(bit_of(1) == 0)
+    def _():
+        lay([near, far])
+
+    @pl.when(bit_of(1) != 0)
+    def _():
+        lay([far, near])
+
+
+def enter_routes(routes_ref, *refs):
+    *level_refs, out_ref, total = refs
+    chains, count, _, size = out_ref.shape
+    ones = jnp.ones((1, size), f32)
+    for chain in range(chains):
+        pack_map(total, chain, jnp.zeros((size, size), bf16), ones, 0.0 * ones)
+    for level, ref in reversed(list(enumerate(level_refs))):
+
+        @pl.when(bit_of(2 + level) != 0)
+        def _():
+            for chain in range(chains):
+                store_map(
+                    total, chain, size, *join_packed(*panel_of(total, chain, size), ref, chain, size)
+                )
+
+    for chain in range(chains):
+        out_ref[chain, 0] = total[chain]
+        panel = panel_of(total, chain, size)
+        for part in range(1, count):
+            joined = join_packed(*panel, routes_ref.at[chain], part - 1, size)
+            store_map(out_ref.at[chain], part, size, *joined)
+
+
+def run_steps(top, start_ref, base_ref, routes_ref, *refs):
+    near, far = refs[0:3], refs[3:6]
+    keep_ref, across_ref, later_ref, entries = refs[6:]
     chains, _, steps, size, _ = near[0].shape
     part_steps = steps // PARTS
     early = corner_of_quad() & 1
     for chain in range(chains):
-        entries[chain, 0, 0, 0] = start_ref[chain]
-
-    @pl.when(bit_of(2 + len(level_refs)) != 0)
-    def _():
-        for chain in range(chains):
-            entries[chain, 0, 0, 0] = base_ref[chain]
-
-    for level, ref in reversed(list(enumerate(level_refs))):
-
-        @pl.when(bit_of(2 + level) != 0)
-        def _():
-            for chain in range(chains):
-                entries[chain, 0, 0, 0] = apply_map(ref, chain, size, entries[chain, 0, 0, 0])
-
-    states = [entries[chain, 0, 0, 0] for chain in range(chains)]
-
-    def enter(pairs):
-        for chain in range(chains):
-            state = states[chain]
-            following = apply_map(pairs[0][1][4], chain, size, state)
-            for (side, pair), state in zip(pairs, (state, following)):
-                linear_ref, offset_ref, fade_ref, early_ref, _ = pair
-                slots = [(early, state), (1 - early, apply_map(early_ref, chain, size, state))]
-                for slot, state in slots:
-                    entries[chain, side, slot, 0] = state
-                    for part in range(1, PARTS):
-                        at = part * part_steps - 1
-                        state = (
-                            state * fade_ref[chain, slot, at : at + 1, :]
-                            + apply_linear(state, linear_ref[chain, slot, at])
-                            + offset_ref[chain, slot, at : at + 1, :]
-                        )
-                        entries[chain, side, slot, part] = state
-
-    @pl.when(bit_of(1) == 0)
-    def _():
-        enter([(0, near), (1, far)])
-
-    @pl.when(bit_of(1) != 0)
-    def _():
-        enter([(1, far), (0, near)])
+        state = jnp.where(bit_of(top) == 0, start_ref[chain], base_ref[chain])
+        stacked = split_state(state)
+        for part in range(4 * PARTS):
+            decay, offset = unpack_map(routes_ref.at[chain], part, size)
+            out = jnp.dot(stacked, routes_ref[chain, part, 0:size, :], preferred_element_type=f32)
+            side = part // (2 * PARTS) ^ bit_of(1)
+            slot = part // PARTS % 2 ^ early
+            entries[chain, side, slot, part % PARTS] = state * decay + out[0:1] + out[1:2] + offset
 
     targets = {(0, 0): (keep_ref, 0), (0, 1): (across_ref, 0), (1, 0): (later_ref, 0), (1, 1): (across_ref, 1)}
     row = row_of((part_steps, size))
     for (side, slot), (target, place) in targets.items():
-        linear_ref, offset_ref, fade_ref, _, _ = (near, far)[side]
+        linear_ref, offset_ref, fade_ref = (near, far)[side]
         for chain in range(chains):
             for part in range(PARTS):
                 entry = entries[chain, side, slot, part]
@@ -519,35 +593,38 @@
         jax.ShapeDtypeStruct((chains, 2, steps, size, size), bf16),
         jax.ShapeDtypeStruct((chains, 2, steps, size), f32),
         jax.ShapeDtypeStruct((chains, 2, steps, size), f32),
-        jax.ShapeDtypeStruct((chains, size + PAD, size), bf16),
-        jax.ShapeDtypeStruct((chains, size + PAD, size), f32),
-        jax.ShapeDtypeStruct((chains, size + PAD, size), bf16),
-    )
-    pair_scratch = [
+    )
+    panel_shapes = (
+        pltpu.VMEM((chains, 2, PARTS, size + PAD, size), f32),
+        pltpu.VMEM((chains, 2, PARTS, 1, size), f32),
+    )
+    formed = [
         pltpu.VMEM((chains, total, size, size), bf16),
         pltpu.VMEM((chains, total, size), f32),
         pltpu.VMEM((chains, total, size), f32),
-        pltpu.VMEM((chains, 2, PARTS, size + PAD, size), f32),
-        pltpu.VMEM((chains, 2, PARTS, 1, size), f32),
     ]
-    *near_maps, near_panel, near_whole = pl.pallas_call(
+    *near_maps, near_panels, near_running = pl.pallas_call(
         build_near,
-        out_shape=pair_shapes,
+        out_shape=pair_shapes + panel_shapes,
         in_specs=[VMEM_SPEC] * 4,
-        out_specs=(VMEM_SPEC,) * 6,
-        scratch_shapes=pair_scratch,
+        out_specs=(VMEM_SPEC,) * 5,
+        scratch_shapes=formed,
         compiler_params=params(20),
         name="build_near",
     )(near, decays, inputs, tiles)
-    *far_maps, far_whole, whole = pl.pallas_call(
+    packed_map = jax.ShapeDtypeStruct((chains, size + PAD, size), bf16)
+    panel = pltpu.VMEM((chains, size + PAD, size), f32)
+    *far_maps, near_early, near_whole, far_early, far_whole, whole = pl.pallas_call(
         build_far,
-        out_shape=pair_shapes[:4] + pair_shapes[5:] * 2,
-        in_specs=[VMEM_SPEC] * 6,
-        out_specs=(VMEM_SPEC,) * 6,
-        scratch_shapes=[pltpu.VMEM(pair_shapes[4].shape, f32)] + pair_scratch,
+        out_shape=pair_shapes + (packed_map,) * 5,
+        in_specs=[VMEM_SPEC] * 7,
+        out_specs=(VMEM_SPEC,) * 8,
+        scratch_shapes=[panel, panel, *panel_shapes, *formed],
         compiler_params=params(20),
         name="build_far",
-    )(far, decays, inputs, tiles, near_panel, near_whole)
+    )(far, decays, inputs, tiles, near_maps[0], near_panels, near_running)
+    near_maps += [near_early, near_whole]
+    far_maps += [far_early, far_whole]
 
     earlier = []
     for level in range(2, bits - 1):
@@ -562,6 +639,14 @@
                 compiler_params=params(16),
                 name="join_maps",
             )(whole, other)
+    routes = pl.pallas_call(
+        lay_routes,
+        out_shape=jax.ShapeDtypeStruct((chains, 4 * PARTS - 1, size + PAD, size), bf16),
+        in_specs=[VMEM_SPEC] * 10,
+        out_specs=VMEM_SPEC,
+        compiler_params=params(16),
+        name="lay_routes",
+    )(*near_maps, *far_maps)
     crossed = pl.pallas_call(
         functools.partial(cross_pair, bits - 2),
         out_shape=jax.ShapeDtypeStruct((chains, 1, size), f32),
@@ -570,17 +655,26 @@
         compiler_params=params(16),
         name="cross_pair",
     )(whole, earlier[-1], start)
+    routes = pl.pallas_call(
+        enter_routes,
+        out_shape=jax.ShapeDtypeStruct((chains, 4 * PARTS, size + PAD, size), bf16),
+        in_specs=[VMEM_SPEC] * (1 + len(earlier)),
+        out_specs=VMEM_SPEC,
+        scratch_shapes=[pltpu.VMEM((chains, size + PAD, size), bf16)],
+        compiler_params=params(16),
+        name="enter_routes",
+    )(routes, *earlier)
     base = partner(crossed, "tm", 1 << (bits - 1))
 
     piece = (chains, steps, size)
     keep, across, later = pl.pallas_call(
-        run_steps,
+        functools.partial(run_steps, bits - 1),
         out_shape=(
             jax.ShapeDtypeStruct((1,) + piece, f32),
             jax.ShapeDtypeStruct((2,) + piece, f32),
             jax.ShapeDtypeStruct((1,) + piece, f32),
         ),
-        in_specs=[VMEM_SPEC] * (12 + len(earlier)),
+        in_specs=[VMEM_SPEC] * 9,
         out_specs=(VMEM_SPEC,) * 3,
         scratch_shapes=[pltpu.VMEM((chains, 2, 2, PARTS, 1, size), f32)],
         compiler_params=params(16),
@@ -588,11 +682,9 @@
     )(
         start,
         base,
-        *earlier,
-        *near_maps,
-        near_whole,
-        *far_maps,
-        far_whole,
+        routes,
+        *near_maps[0:3],
+        *far_maps[0:3],
     )
     across = partner(across, "tm", 1)
     later = partner(jnp.concatenate([later, across[1:2]], axis=0), "tm", 2)

time: 34.4 us -> 33.5 us (0.974)
  waiting for transfers between devices: 10.3 us -> 8.49 us
  starting transfers between devices: 11.8 us -> 12.8 us
    ppermute x7, waiting for transfers between devices: 10.3 us -> 8.49 us  [partner(): lax.ppermute(array, axis, [(i, i ^ flip) for i in range(lax.axis_size(axi...]
    ppermute x7, starting transfers between devices: 11.8 us -> 12.8 us  [partner(): lax.ppermute(array, axis, [(i, i ^ flip) for i in range(lax.axis_size(axi...]
    pallas_call x3 -> x5, Pallas kernels: 6.66 us -> 6.63 us  [the longest x1 2.75 us: body(): pl.pallas_call(build_far, out_shape=pair_shapes + (packed_map,) * 5, in_s...]
  transfers between devices with their start and end apart: 7 -> 7, of which waited for: 5 -> 5; matrix products, arithmetic and copies ran while one was open for 0% -> 0% of each run, Pallas kernels for 15% -> 17%
where the time goes in v3:
time: 33.5 us; the launch traced here: 33.3 us
  starting transfers between devices  12.8 us (38%)
  Pallas kernels  10.5 us (31%)
  waiting for transfers between devices  8.49 us (25%)
  between operations  0.79 us (2%)
  other arithmetic  0.74 us (2%)
    ppermute x7, starting transfers between devices, partner(): lax.ppermute(array, axis, [(i, i ^ flip) for i in range(lax.axis_size(axi...  12.8 us
    ppermute x7, waiting for transfers between devices, partner(): lax.ppermute(array, axis, [(i, i ^ flip) for i in range(lax.axis_size(axi...  8.49 us
    pallas_call x1, Pallas kernels, body(): pl.pallas_call(build_far, out_shape=pair_shapes + (packed_map,) * 5, in_s...  2.75 us
    pallas_call x1, Pallas kernels, body(): pl.pallas_call(build_near, out_shape=pair_shapes + panel_shapes, in_specs...  2.13 us
    pallas_call x1, Pallas kernels, body(): pl.pallas_call(stage_inputs, out_shape=(jax.ShapeDtypeStruct((chains, siz...  1.87 us
    pallas_call x1, Pallas kernels, body(): pl.pallas_call(read_out, out_shape=jax.ShapeDtypeStruct((rows, features),...  0.92 us
    pallas_call x1, Pallas kernels, body(): pl.pallas_call(functools.partial(run_steps, bits - 1), out_shape=(jax.Sha...  0.9 us
    concatenate x1, other arithmetic, body(): path = jnp.concatenate([increments, step_sizes[:, None, :]], axis=1)  0.73 us
  transfers between devices with their start and end apart: 7, of which 5 were waited for; matrix products, arithmetic and copies ran while one was open for 0% of the time, Pallas kernels for 17%

profile of v3, /device:TPU:0, one launch (start us, length us, event | category | flops | bytes accessed | tf_op | source)
XLA Modules:
  0.0 33.3 jit_solution(14295526364061245101)
XLA Ops:
  0.7 0.7 %fusion.2 = (f32[1,17,16]{2,1,0:T(8,128)S(1)}, f32[17,16]{1,0:T(8,128)S(1)}) fusion(s32[]{:T(128)S(6)} %select_n.20, f32[2,16,16]{2,1,0:T(8,128)} %param.12, f32[2,1,16]{2,1,0:T(1,128)} %bitcast.13, s32[]{:T(128)S(6)} %select_n.21), kind=kLoop, calls=%fused_computation.8 | loop fusion | flops 544 | bytes 4360 | tf_op jit(solution)/shard_map/concatenate | solution.py:559
  1.4 3.0 %collective-permute-start = (f32[17,16]{1,0:T(8,128)S(1)}, f32[17,16]{1,0:T(8,128)S(1)}, u32[]{:S(2)}, u32[]{:S(2)}) collective-permute-start(f32[17,16]{1,0:T(8,128)S(1)} %get-tuple-element.55), channel_id=1, source_target_pairs={{0,2},{2,0},{4,6},{6,4},{8,10},{10,8},{12,14},{14,12},{16,18},{18,... | collective-permute-start | bytes 3272 | tf_op jit(solution)/shard_map/ppermute | solution.py:26
  4.4 1.9 %stage_inputs.1 = (bf16[2,8,128,256]{3,2,1,0:T(8,128)(2,1)S(1)}, f32[2,1,128]{2,1,0:T(1,128)S(1)}, f32[2,16,128]{2,1,0:T(8,128)S(1)}, f32[2,1,128]{2,1,0:T(1,128)S(1)}) custom-call(f32[1,512]{1,0:T(1,128)} %bitcast.12, f32[16,512]{1,0:T(8,128)} %input_ref.1, f32[2,512]{1,0:T(2,128)} %initial_ref.1, f32[16,4,128,128]{3,2,1,0:T(8,128)} %coupling_ref.1), custom_call_target="tpu_custom_call" | custom-call | tf_op jit(solution)/shard_map/stage_inputs/pallas_call | solution.py:565
  6.2 0.0 collective-permute-done
  6.3 1.8 %collective-permute-start.1 = (f32[2,17,16]{2,1,0:T(8,128)S(1)}, f32[2,17,16]{2,1,0:T(8,128)S(1)}, u32[]{:S(2)}, u32[]{:S(2)}) collective-permute-start(f32[2,17,16]{2,1,0:T(8,128)S(1)} %pad_maximum_fusion.1.near_ref), channel_id=1, source_target_pairs={{0,4},{2,6},{4,0},{6,2},{8,12},{10,14},{12,8},{14,10},{16,20},{18,... | collective-permute-start | bytes 6536 | tf_op jit(solution)/shard_map/ppermute | solution.py:26
  8.1 2.1 %build_near.1 = (bf16[2,2,16,128,128]{4,3,2,1,0:T(8,128)(2,1)S(1)}, f32[2,2,16,128]{3,2,1,0:T(8,128)S(1)}, f32[2,2,16,128]{3,2,1,0:T(8,128)S(1)}, f32[2,2,2,144,...) custom-call(f32[2,17,16]{2,1,0:T(8,128)S(1)} %pad_maximum_fusion.1.near_ref, ...), custom_call_target="tpu_custom_call" | custom-call | tf_op jit(solution)/shard_map/build_near/pallas_call | solution.py:606
  10.2 0.0 collective-permute-done.1.far_ref
  10.2 2.7 %build_far.1 = (bf16[2,2,16,128,128]{4,3,2,1,0:T(8,128)(2,1)S(1)}, f32[2,2,16,128]{3,2,1,0:T(8,128)S(1)}, f32[2,2,16,128]{3,2,1,0:T(8,128)S(1)}, bf16[2,144,128]...) custom-call(f32[2,17,16]{2,1,0:T(8,128)S(1)} %collective-permute-don, ...), custom_call_target="tpu_custom_call" | custom-call | tf_op jit(solution)/shard_map/build_far/pallas_call | solution.py:617
  13.0 1.8 %collective-permute-start.2 = (bf16[2,144,128]{2,1,0:T(8,128)(2,1)S(1)}, bf16[2,144,128]{2,1,0:T(8,128)(2,1)S(1)}, u32[]{:S(2)}, u32[]{:S(2)}) collective-permute-start(bf16[2,144,128]{2,1,0:T(8,128)(2,1)S(1)} %get-tuple-element.37.own_ref), channel_id=1, source_target_pairs={{0,8},{2,10},{4,12},{6,14},{8,0},{10,2},{12,4},{14,6},{16,24},{18,... | collective-permute-start | bytes 221192 | tf_op jit(solution)/shard_map/ppermute | solution.py:26
  14.8 2.6 %collective-permute-done.2.other_ref.refs_0_ = bf16[2,144,128]{2,1,0:T(8,128)(2,1)S(1)} collective-permute-done((bf16[2,144,128]{2,1,0:T(8,128)(2,1)S(1)}, bf16[2,144,128]{2,1,0:T(8,128)(2,1)S(1)}, u32[]{:S(2)}, u32[]{:S(2)}) %collective-permute-start.2) | collective-permute-done | bytes 73760 | tf_op jit(solution)/shard_map/ppermute | solution.py:26
  17.4 0.3 cross_pair.1
  17.7 2.7 %collective-permute-start.3 = (f32[2,1,128]{2,1,0:T(1,128)S(1)}, f32[2,1,128]{2,1,0:T(1,128)S(1)}, u32[]{:S(2)}, u32[]{:S(2)}) collective-permute-start(f32[2,1,128]{2,1,0:T(1,128)S(1)} %cross_pair.1), channel_id=1, source_target_pairs={{0,16},{2,18},{4,20},{6,22},{8,24},{10,26},{12,28},{14,30},{16,0},... | collective-permute-start | bytes 3080 | tf_op jit(solution)/shard_map/ppermute | solution.py:26
  20.4 0.4 %lay_routes.1.routes_ref = bf16[2,7,144,128]{3,2,1,0:T(8,128)(2,1)S(1)} custom-call(bf16[2,2,16,128,128]{4,3,2,1,0:T(8,128)(2,1)S(1)} %get-tuple-element.34.near_linear.refs_0_, f32[2,2,16,128]{3,2,1,0:T(8,128)S(1)} %get-tuple-element.38.refs_1_, f32[2,2,16,128]{3,2,1,0:T(8,128)S(1)} %get-tuple-element.39.refs_2_, ...), custom_call_target="tpu_custom_call" | custom-call | tf_op jit(solution)/shard_map/lay_routes/pallas_call | solution.py:642
  20.8 0.4 %enter_routes.1.routes_ref = bf16[2,8,144,128]{3,2,1,0:T(8,128)(2,1)S(1)} custom-call(bf16[2,7,144,128]{3,2,1,0:T(8,128)(2,1)S(1)} %lay_routes.1.routes_ref, bf16[2,144,128]{2,1,0:T(8,128)(2,1)S(1)} %collective-permute-done.2.other_ref.refs_0_), custom_call_target="tpu_custom_call" | custom-call | tf_op jit(solution)/shard_map/enter_routes/pallas_call | solution.py:658
  21.3 0.0 copy-start.2
  21.3 0.0 copy-start
  21.3 0.0 copy-start.1
  21.3 0.8 %collective-permute-done.3.base_ref = f32[2,1,128]{2,1,0:T(1,128)S(1)} collective-permute-done((f32[2,1,128]{2,1,0:T(1,128)S(1)}, f32[2,1,128]{2,1,0:T(1,128)S(1)}, u32[]{:S(2)}, u32[]{:S(2)}) %collective-permute-start.3) | collective-permute-done | bytes 1056 | tf_op jit(solution)/shard_map/ppermute | solution.py:26
  22.1 0.9 %run_steps.1 = (f32[1,2,16,128]{3,2,1,0:T(8,128)S(1)}, f32[2,2,16,128]{3,2,1,0:T(8,128)S(1)}, f32[1,2,16,128]{3,2,1,0:T(8,128)S(1)}) custom-call(f32[2,1,128]{2,1,0:T(1,128)S(1)} %get-tuple-element.28.start_ref, f32[2,1,128]{2,1,0:T(1,128)S(1)} %collective-permute-done.3.base_ref, bf16[2,8,144,128]{3,2,1,0:T(8,128)(2,1)S(1)} %enter_routes.1.routes_ref, ...), custom_call_target="tpu_custom_call" | custom-call | tf_op jit(solution)/shard_map/run_steps/pallas_call | solution.py:670
  23.0 1.7 %collective-permute-start.4 = (f32[2,2,16,128]{3,2,1,0:T(8,128)S(1)}, f32[2,2,16,128]{3,2,1,0:T(8,128)S(1)}, u32[]{:S(2)}, u32[]{:S(2)}) collective-permute-start(f32[2,2,16,128]{3,2,1,0:T(8,128)S(1)} %get-tuple-element.48), channel_id=1, source_target_pairs={{0,2},{2,0},{4,6},{6,4},{8,10},{10,8},{12,14},{14,12},{16,18},{18,... | collective-permute-start | bytes 98312 | tf_op jit(solution)/shard_map/ppermute | solution.py:26
  24.8 2.3 %collective-permute-done.4.across_ref = f32[2,2,16,128]{3,2,1,0:T(8,128)S(1)} collective-permute-done((f32[2,2,16,128]{3,2,1,0:T(8,128)S(1)}, f32[2,2,16,128]{3,2,1,0:T(8,128)S(1)}, u32[]{:S(2)}, u32[]{:S(2)}) %collective-permute-start.4) | collective-permute-done | bytes 32800 | tf_op jit(solution)/shard_map/ppermute | solution.py:26
  27.0 1.7 %collective-permute-start.5 = (f32[2,2,16,128]{3,2,1,0:T(8,128)S(1)}, f32[2,2,16,128]{3,2,1,0:T(8,128)S(1)}, u32[]{:S(2)}, u32[]{:S(2)}) collective-permute-start(f32[2,2,16,128]{3,2,1,0:T(8,128)S(1)} %pad_maximum_fusion), channel_id=1, source_target_pairs={{0,4},{2,6},{4,0},{6,2},{8,12},{10,14},{12,8},{14,10},{16,20},{18,... | collective-permute-start | bytes 98312 | tf_op jit(solution)/shard_map/ppermute | solution.py:26
  28.7 2.3 %collective-permute-done.5.later_ref = f32[2,2,16,128]{3,2,1,0:T(8,128)S(1)} collective-permute-done((f32[2,2,16,128]{3,2,1,0:T(8,128)S(1)}, f32[2,2,16,128]{3,2,1,0:T(8,128)S(1)}, u32[]{:S(2)}, u32[]{:S(2)}) %collective-permute-start.5) | collective-permute-done | bytes 32800 | tf_op jit(solution)/shard_map/ppermute | solution.py:26
  30.9 0.0 copy-done.2
  30.9 0.1 scale_states.1
  31.1 0.1 collective-permute-start.6
  31.1 0.0 copy-done
  31.1 0.0 copy-done.1
  31.2 0.7 %read_own.1 = (f32[2,16,512]{2,1,0:T(8,128)}, f32[2,32,512]{2,1,0:T(8,128)S(1)}) custom-call(f32[2,16,512]{2,1,0:T(8,128)S(1)} %get-tuple-element.50.states_vmem, bf16[32,640]{1,0:T(8,128)(2,1)S(1)} %get-tuple-element.51.own_ref, bf16[1024,512]{1,0:T(8,128)(2,1)S(1)} %copy-done, bf16[1024,512]{1,0:T(8,128)(2,1)S(1)} %copy-done.1), custom_call_target="tpu_custom_call" | custom-call | tf_op jit(solution)/shard_map/read_own/pallas_call | solution.py:707
  31.8 0.5 %collective-permute-done.6.other_ref = bf16[32,640]{1,0:T(8,128)(2,1)S(1)} collective-permute-done((bf16[32,640]{1,0:T(8,128)(2,1)S(1)}, bf16[32,640]{1,0:T(8,128)(2,1)S(1)}, u32[]{:S(2)}, u32[]{:S(2)}) %collective-permute-start.6) | collective-permute-done | bytes 40992 | tf_op jit(solution)/shard_map/ppermute | solution.py:26
  32.3 0.9 %read_out.1 = bf16[32,512]{1,0:T(8,128)(2,1)} custom-call(bf16[32,640]{1,0:T(8,128)(2,1)S(1)} %get-tuple-element.51.own_ref, bf16[32,640]{1,0:T(8,128)(2,1)S(1)} %collective-permute-done.6.other_ref, f32[2,32,512]{2,1,0:T(8,128)S(1)} %get-tuple-element.53.sums_ref, bf16[1024,512]{1,0:T(8,128)(2,1)S(1)} %copy-done, bf16[1024,512]{1,0:T(8,128)(2,1)S(1)} %copy-done.1), custom_call_target="tpu_custom_call" | custom-call | tf_op jit(solution)/shard_map/read_out/pallas_call | solution.py:719
  (3 shorter events, 0.0 us)
Async XLA Ops:
  1.4 4.8 %collective-permute-start = (f32[17,16]{1,0:T(8,128)S(1)}, f32[17,16]{1,0:T(8,128)S(1)}, u32[]{:S(2)}, u32[]{:S(2)}) collective-permute-start(f32[17,16]{1,0:T(8,128)S(1)} %get-tuple-element.55), channel_id=1, source_target_pairs={{0,2},{2,0},{4,6},{6,4},{8,10},{10,8},{12,14},{14,12},{16,18},{18,... | collective-permute-start | bytes 3272 | tf_op jit(solution)/shard_map/ppermute | solution.py:26
  6.3 4.0 %collective-permute-start.1 = (f32[2,17,16]{2,1,0:T(8,128)S(1)}, f32[2,17,16]{2,1,0:T(8,128)S(1)}, u32[]{:S(2)}, u32[]{:S(2)}) collective-permute-start(f32[2,17,16]{2,1,0:T(8,128)S(1)} %pad_maximum_fusion.1.near_ref), channel_id=1, source_target_pairs={{0,4},{2,6},{4,0},{6,2},{8,12},{10,14},{12,8},{14,10},{16,20},{18,... | collective-permute-start | bytes 6536 | tf_op jit(solution)/shard_map/ppermute | solution.py:26
  13.0 4.4 %collective-permute-start.2 = (bf16[2,144,128]{2,1,0:T(8,128)(2,1)S(1)}, bf16[2,144,128]{2,1,0:T(8,128)(2,1)S(1)}, u32[]{:S(2)}, u32[]{:S(2)}) collective-permute-start(bf16[2,144,128]{2,1,0:T(8,128)(2,1)S(1)} %get-tuple-element.37.own_ref), channel_id=1, source_target_pairs={{0,8},{2,10},{4,12},{6,14},{8,0},{10,2},{12,4},{14,6},{16,24},{18,... | collective-permute-start | bytes 221192 | tf_op jit(solution)/shard_map/ppermute | solution.py:26
  17.7 4.5 %collective-permute-start.3 = (f32[2,1,128]{2,1,0:T(1,128)S(1)}, f32[2,1,128]{2,1,0:T(1,128)S(1)}, u32[]{:S(2)}, u32[]{:S(2)}) collective-permute-start(f32[2,1,128]{2,1,0:T(1,128)S(1)} %cross_pair.1), channel_id=1, source_target_pairs={{0,16},{2,18},{4,20},{6,22},{8,24},{10,26},{12,28},{14,30},{16,0},... | collective-permute-start | bytes 3080 | tf_op jit(solution)/shard_map/ppermute | solution.py:26
  21.3 9.7 %copy-start.2 = (f32[512]{0:T(512)S(1)}, f32[512]{0:T(512)}, u32[]{:S(2)}) copy-start(f32[512]{0:T(512)} %param.15) | copy-start | bytes 6148
  21.3 9.9 %copy-start = (bf16[1024,512]{1,0:T(8,128)(2,1)S(1)}, bf16[1024,512]{1,0:T(8,128)(2,1)}, u32[]{:S(2)}) copy-start(bf16[1024,512]{1,0:T(8,128)(2,1)} %value_ref.3) | copy-start | bytes 3145732
  21.3 9.8 %copy-start.1 = (bf16[1024,512]{1,0:T(8,128)(2,1)S(1)}, bf16[1024,512]{1,0:T(8,128)(2,1)}, u32[]{:S(2)}) copy-start(bf16[1024,512]{1,0:T(8,128)(2,1)} %gate_ref.3) | copy-start | bytes 3145732
  23.0 4.0 %collective-permute-start.4 = (f32[2,2,16,128]{3,2,1,0:T(8,128)S(1)}, f32[2,2,16,128]{3,2,1,0:T(8,128)S(1)}, u32[]{:S(2)}, u32[]{:S(2)}) collective-permute-start(f32[2,2,16,128]{3,2,1,0:T(8,128)S(1)} %get-tuple-element.48), channel_id=1, source_target_pairs={{0,2},{2,0},{4,6},{6,4},{8,10},{10,8},{12,14},{14,12},{16,18},{18,... | collective-permute-start | bytes 98312 | tf_op jit(solution)/shard_map/ppermute | solution.py:26
  27.0 3.9 %collective-permute-start.5 = (f32[2,2,16,128]{3,2,1,0:T(8,128)S(1)}, f32[2,2,16,128]{3,2,1,0:T(8,128)S(1)}, u32[]{:S(2)}, u32[]{:S(2)}) collective-permute-start(f32[2,2,16,128]{3,2,1,0:T(8,128)S(1)} %pad_maximum_fusion), channel_id=1, source_target_pairs={{0,4},{2,6},{4,0},{6,2},{8,12},{10,14},{12,8},{14,10},{16,20},{18,... | collective-permute-start | bytes 98312 | tf_op jit(solution)/shard_map/ppermute | solution.py:26
  31.1 1.3 %collective-permute-start.6 = (bf16[32,640]{1,0:T(8,128)(2,1)S(1)}, bf16[32,640]{1,0:T(8,128)(2,1)S(1)}, u32[]{:S(2)}, u32[]{:S(2)}) collective-permute-start(bf16[32,640]{1,0:T(8,128)(2,1)S(1)} %get-tuple-element.51.own_ref), channel_id=1, source_target_pairs={{0,1},{1,0},{2,3},{3,2},{4,5},{5,4},{6,7},{7,6},{8,9},{9,8},{10,11... | collective-permute-start | bytes 122888 | tf_op jit(solution)/shard_map/ppermute | solution.py:26

commit v4 on v3

--- a/solution.py
+++ b/solution.py
@@ -165,6 +165,19 @@
         ],
         axis=1,
     )
+    corner = row_of((steps, steps)) == lax.broadcasted_iota(jnp.int32, (steps, steps), 1)
+    gaps = jnp.concatenate(
+        [
+            jnp.sum(jnp.where(corner, slot[steps : steps + 1, 0:steps], 0.0), axis=1, keepdims=True)
+            for slot in slots
+        ],
+        axis=0,
+    )
+    for chain in range(chains):
+        fades_ref[chain] = jnp.exp(-gaps * decay_ref[chain])
+        drives_ref[chain] = jnp.dot(
+            moves, input_ref[chain], precision=lax.Precision.HIGHEST, preferred_element_type=f32
+        )
     for chain in range(chains):
         for tile in range(tile_count):
             right = tiles_ref[chain, tile]
@@ -175,20 +188,6 @@
                 made[:, size:].reshape(total, 8, size),
             ]
             maps_ref[chain, :, tile * PAD : tile * PAD + PAD, :] = jnp.concatenate(halves, axis=1).astype(bf16)
-
-    corner = row_of((steps, steps)) == lax.broadcasted_iota(jnp.int32, (steps, steps), 1)
-    gaps = jnp.concatenate(
-        [
-            jnp.sum(jnp.where(corner, slot[steps : steps + 1, 0:steps], 0.0), axis=1, keepdims=True)
-            for slot in slots
-        ],
-        axis=0,
-    )
-    for chain in range(chains):
-        fades_ref[chain] = jnp.exp(-gaps * decay_ref[chain])
-        drives_ref[chain] = jnp.dot(
-            moves, input_ref[chain], precision=lax.Precision.HIGHEST, preferred_element_type=f32
-        )
 
 
 def build_pair(
@@ -435,44 +434,39 @@
             store_map(out_ref.at[chain], part, size, *joined)
 
 
-def run_steps(top, start_ref, base_ref, routes_ref, *refs):
-    near, far = refs[0:3], refs[3:6]
-    keep_ref, across_ref, later_ref, entries = refs[6:]
-    chains, _, steps, size, _ = near[0].shape
+def run_steps(top, slot, start_ref, base_ref, routes_ref, *refs):
+    pairs, out_ref = (refs[0:3], refs[3:6]), refs[6]
+    _, chains, steps, size = out_ref.shape
     part_steps = steps // PARTS
-    early = corner_of_quad() & 1
+    row = row_of((part_steps, size))
+    turn = slot ^ (corner_of_quad() & 1)
+    entries = {}
     for chain in range(chains):
         state = jnp.where(bit_of(top) == 0, start_ref[chain], base_ref[chain])
         stacked = split_state(state)
-        for part in range(4 * PARTS):
-            decay, offset = unpack_map(routes_ref.at[chain], part, size)
-            out = jnp.dot(stacked, routes_ref[chain, part, 0:size, :], preferred_element_type=f32)
-            side = part // (2 * PARTS) ^ bit_of(1)
-            slot = part // PARTS % 2 ^ early
-            entries[chain, side, slot, part % PARTS] = state * decay + out[0:1] + out[1:2] + offset
-
-    targets = {(0, 0): (keep_ref, 0), (0, 1): (across_ref, 0), (1, 0): (later_ref, 0), (1, 1): (across_ref, 1)}
-    row = row_of((part_steps, size))
-    for (side, slot), (target, place) in targets.items():
-        linear_ref, offset_ref, fade_ref = (near, far)[side]
-        for chain in range(chains):
+        for side in range(2):
             for part in range(PARTS):
-                entry = entries[chain, side, slot, part]
-                same = jnp.broadcast_to(entry, (PAD, size)).astype(bf16)
-                at = part * part_steps
-                gathered = (
-                    entry * fade_ref[chain, slot, at : at + part_steps, :]
-                    + offset_ref[chain, slot, at : at + part_steps, :]
-                )
-                for step in range(0, part_steps, 2):
-                    pair = jnp.concatenate(
-                        [linear_ref[chain, slot, at + step + half] for half in range(2)], axis=1
-                    )
-                    out = jnp.dot(same, pair, preferred_element_type=f32)
-                    for half in range(2):
-                        spread = out[0:part_steps, half * size : (half + 1) * size]
-                        gathered = gathered + jnp.where(row == step + half, spread, 0.0)
-                target[place, chain, at : at + part_steps, :] = gathered
+                at = ((side ^ bit_of(1)) * 2 + turn) * PARTS + part
+                decay, offset = unpack_map(routes_ref.at[chain], at, size)
+                out = jnp.dot(stacked, routes_ref[chain, at, 0:size, :], preferred_element_type=f32)
+                entries[chain, side, part] = state * decay + out[0:1] + out[1:2] + offset
+    for (chain, side, part), entry in entries.items():
+        linear_ref, offset_ref, fade_ref = pairs[side]
+        same = jnp.broadcast_to(entry, (PAD, size)).astype(bf16)
+        at = part * part_steps
+        gathered = (
+            entry * fade_ref[chain, slot, at : at + part_steps, :]
+            + offset_ref[chain, slot, at : at + part_steps, :]
+        )
+        for step in range(0, part_steps, 2):
+            pair = jnp.concatenate(
+                [linear_ref[chain, slot, at + step + half] for half in range(2)], axis=1
+            )
+            out = jnp.dot(same, pair, preferred_element_type=f32)
+            for half in range(2):
+                spread = out[0:part_steps, half * size : (half + 1) * size]
+                gathered = gathered + jnp.where(row == step + half, spread, 0.0)
+        out_ref[side, chain, at : at + part_steps, :] = gathered
 
 
 def scale_states(keep_ref, across_ref, later_ref, gain_ref, states_ref, packed_ref, table):
@@ -666,28 +660,19 @@
     )(routes, *earlier)
     base = partner(crossed, "tm", 1 << (bits - 1))
 
-    piece = (chains, steps, size)
-    keep, across, later = pl.pallas_call(
-        functools.partial(run_steps, bits - 1),
-        out_shape=(
-            jax.ShapeDtypeStruct((1,) + piece, f32),
-            jax.ShapeDtypeStruct((2,) + piece, f32),
-            jax.ShapeDtypeStruct((1,) + piece, f32),
-        ),
-        in_specs=[VMEM_SPEC] * 9,
-        out_specs=(VMEM_SPEC,) * 3,
-        scratch_shapes=[pltpu.VMEM((chains, 2, 2, PARTS, 1, size), f32)],
-        compiler_params=params(16),
-        name="run_steps",
-    )(
-        start,
-        base,
-        routes,
-        *near_maps[0:3],
-        *far_maps[0:3],
-    )
-    across = partner(across, "tm", 1)
-    later = partner(jnp.concatenate([later, across[1:2]], axis=0), "tm", 2)
+    def run(slot):
+        return pl.pallas_call(
+            functools.partial(run_steps, bits - 1, slot),
+            out_shape=jax.ShapeDtypeStruct((2, chains, steps, size), f32),
+            in_specs=[VMEM_SPEC] * 9,
+            out_specs=VMEM_SPEC,
+            compiler_params=params(16),
+            name="run_steps",
+        )(start, base, routes, *near_maps[0:3], *far_maps[0:3])
+
+    sent, kept = run(1), run(0)
+    across = partner(sent, "tm", 1)
+    later = partner(jnp.stack([kept[1], across[1]]), "tm", 2)
 
     rows = records * steps
     states, packed = pl.pallas_call(
@@ -701,7 +686,7 @@
         scratch_shapes=[pltpu.VMEM((records, local_blocks, steps, size), f32)],
         compiler_params=params(16),
         name="scale_states",
-    )(keep, across, later, gain.reshape(1, local_units))
+    )(kept, across, later, gain.reshape(1, local_units))
     packed_other = partner(packed, "blk", 1)
     features = value_weight.shape[1]
     states, sums = pl.pallas_call(

time: 33.5 us -> 32.9 us (0.982)
  waiting for transfers between devices: 8.49 us -> 7.69 us
  starting transfers between devices: 12.8 us -> 13.2 us
    ppermute x7, waiting for transfers between devices: 8.49 us -> 7.69 us  [partner(): lax.ppermute(array, axis, [(i, i ^ flip) for i in range(lax.axis_size(axi...]
    ppermute x7, starting transfers between devices: 12.8 us -> 13.2 us  [partner(): lax.ppermute(array, axis, [(i, i ^ flip) for i in range(lax.axis_size(axi...]
    pallas_call x1 -> x2, Pallas kernels: 0.9 us -> 1.01 us  [run(): pl.pallas_call(functools.partial(run_steps, bits - 1, slot), out_shape=ja...]
  transfers between devices with their start and end apart: 7 -> 7, of which waited for: 5 -> 6; matrix products, arithmetic and copies ran while one was open for 0% -> 0% of each run, Pallas kernels for 17% -> 18%
where the time goes in v4:
time: 32.9 us; the launch traced here: 32.6 us
  starting transfers between devices  13.2 us (40%)
  Pallas kernels  10.2 us (31%)
  waiting for transfers between devices  7.69 us (23%)
  between operations  0.78 us (2%)
  other arithmetic  0.74 us (2%)
    ppermute x7, starting transfers between devices, partner(): lax.ppermute(array, axis, [(i, i ^ flip) for i in range(lax.axis_size(axi...  13.2 us
    ppermute x7, waiting for transfers between devices, partner(): lax.ppermute(array, axis, [(i, i ^ flip) for i in range(lax.axis_size(axi...  7.69 us
    pallas_call x1, Pallas kernels, body(): pl.pallas_call(build_far, out_shape=pair_shapes + (packed_map,) * 5, in_s...  2.55 us
    pallas_call x1, Pallas kernels, body(): pl.pallas_call(build_near, out_shape=pair_shapes + panel_shapes, in_specs...  1.99 us
    pallas_call x1, Pallas kernels, body(): pl.pallas_call(stage_inputs, out_shape=(jax.ShapeDtypeStruct((chains, siz...  1.87 us
    pallas_call x2, Pallas kernels, run(): pl.pallas_call(functools.partial(run_steps, bits - 1, slot), out_shape=ja...  1.01 us
    pallas_call x1, Pallas kernels, body(): pl.pallas_call(read_out, out_shape=jax.ShapeDtypeStruct((rows, features),...  0.92 us
    concatenate x1, other arithmetic, body(): path = jnp.concatenate([increments, step_sizes[:, None, :]], axis=1)  0.73 us
  transfers between devices with their start and end apart: 7, of which 6 were waited for; matrix products, arithmetic and copies ran while one was open for 0% of the time, Pallas kernels for 18%

profile of v4, /device:TPU:0, one launch (start us, length us, event | category | flops | bytes accessed | tf_op | source)
XLA Modules:
  0.0 32.6 jit_solution(10294508829766656047)
XLA Ops:
  0.7 0.7 %fusion.2 = (f32[1,17,16]{2,1,0:T(8,128)S(1)}, f32[17,16]{1,0:T(8,128)S(1)}) fusion(s32[]{:T(128)S(6)} %select_n.20, f32[2,16,16]{2,1,0:T(8,128)} %param.12, f32[2,1,16]{2,1,0:T(1,128)} %bitcast.13, s32[]{:T(128)S(6)} %select_n.21), kind=kLoop, calls=%fused_computation.8 | loop fusion | flops 544 | bytes 4360 | tf_op jit(solution)/shard_map/concatenate | solution.py:553
  1.4 3.0 %collective-permute-start = (f32[17,16]{1,0:T(8,128)S(1)}, f32[17,16]{1,0:T(8,128)S(1)}, u32[]{:S(2)}, u32[]{:S(2)}) collective-permute-start(f32[17,16]{1,0:T(8,128)S(1)} %get-tuple-element.49), channel_id=1, source_target_pairs={{0,2},{2,0},{4,6},{6,4},{8,10},{10,8},{12,14},{14,12},{16,18},{18,... | collective-permute-start | bytes 3272 | tf_op jit(solution)/shard_map/ppermute | solution.py:26
  4.4 1.9 %stage_inputs.1 = (bf16[2,8,128,256]{3,2,1,0:T(8,128)(2,1)S(1)}, f32[2,1,128]{2,1,0:T(1,128)S(1)}, f32[2,16,128]{2,1,0:T(8,128)S(1)}, f32[2,1,128]{2,1,0:T(1,128)S(1)}) custom-call(f32[1,512]{1,0:T(1,128)} %bitcast.12, f32[16,512]{1,0:T(8,128)} %input_ref.1, f32[2,512]{1,0:T(2,128)} %initial_ref.1, f32[16,4,128,128]{3,2,1,0:T(8,128)} %coupling_ref.1), custom_call_target="tpu_custom_call" | custom-call | tf_op jit(solution)/shard_map/stage_inputs/pallas_call | solution.py:559
  6.2 0.0 collective-permute-done
  6.3 1.8 %collective-permute-start.1 = (f32[2,17,16]{2,1,0:T(8,128)S(1)}, f32[2,17,16]{2,1,0:T(8,128)S(1)}, u32[]{:S(2)}, u32[]{:S(2)}) collective-permute-start(f32[2,17,16]{2,1,0:T(8,128)S(1)} %pad_maximum_fusion.1.near_ref), channel_id=1, source_target_pairs={{0,4},{2,6},{4,0},{6,2},{8,12},{10,14},{12,8},{14,10},{16,20},{18,... | collective-permute-start | bytes 6536 | tf_op jit(solution)/shard_map/ppermute | solution.py:26
  8.1 2.0 %build_near.1 = (bf16[2,2,16,128,128]{4,3,2,1,0:T(8,128)(2,1)S(1)}, f32[2,2,16,128]{3,2,1,0:T(8,128)S(1)}, f32[2,2,16,128]{3,2,1,0:T(8,128)S(1)}, f32[2,2,2,144,...) custom-call(f32[2,17,16]{2,1,0:T(8,128)S(1)} %pad_maximum_fusion.1.near_ref, ...), custom_call_target="tpu_custom_call" | custom-call | tf_op jit(solution)/shard_map/build_near/pallas_call | solution.py:600
  10.1 0.1 collective-permute-done.1.far_ref
  10.2 2.6 %build_far.1 = (bf16[2,2,16,128,128]{4,3,2,1,0:T(8,128)(2,1)S(1)}, f32[2,2,16,128]{3,2,1,0:T(8,128)S(1)}, f32[2,2,16,128]{3,2,1,0:T(8,128)S(1)}, bf16[2,144,128]...) custom-call(f32[2,17,16]{2,1,0:T(8,128)S(1)} %collective-permute-don, ...), custom_call_target="tpu_custom_call" | custom-call | tf_op jit(solution)/shard_map/build_far/pallas_call | solution.py:611
  12.7 1.9 %collective-permute-start.2 = (bf16[2,144,128]{2,1,0:T(8,128)(2,1)S(1)}, bf16[2,144,128]{2,1,0:T(8,128)(2,1)S(1)}, u32[]{:S(2)}, u32[]{:S(2)}) collective-permute-start(bf16[2,144,128]{2,1,0:T(8,128)(2,1)S(1)} %get-tuple-element.34.own_ref), channel_id=1, source_target_pairs={{0,8},{2,10},{4,12},{6,14},{8,0},{10,2},{12,4},{14,6},{16,24},{18,... | collective-permute-start | bytes 221192 | tf_op jit(solution)/shard_map/ppermute | solution.py:26
  14.6 2.5 %collective-permute-done.2.other_ref.refs_0_ = bf16[2,144,128]{2,1,0:T(8,128)(2,1)S(1)} collective-permute-done((bf16[2,144,128]{2,1,0:T(8,128)(2,1)S(1)}, bf16[2,144,128]{2,1,0:T(8,128)(2,1)S(1)}, u32[]{:S(2)}, u32[]{:S(2)}) %collective-permute-start.2) | collective-permute-done | bytes 73760 | tf_op jit(solution)/shard_map/ppermute | solution.py:26
  17.1 0.3 cross_pair.1
  17.4 2.8 %collective-permute-start.3 = (f32[2,1,128]{2,1,0:T(1,128)S(1)}, f32[2,1,128]{2,1,0:T(1,128)S(1)}, u32[]{:S(2)}, u32[]{:S(2)}) collective-permute-start(f32[2,1,128]{2,1,0:T(1,128)S(1)} %cross_pair.1), channel_id=1, source_target_pairs={{0,16},{2,18},{4,20},{6,22},{8,24},{10,26},{12,28},{14,30},{16,0},... | collective-permute-start | bytes 3080 | tf_op jit(solution)/shard_map/ppermute | solution.py:26
  20.2 0.4 %lay_routes.1.routes_ref = bf16[2,7,144,128]{3,2,1,0:T(8,128)(2,1)S(1)} custom-call(bf16[2,2,16,128,128]{4,3,2,1,0:T(8,128)(2,1)S(1)} %get-tuple-element.31.near_linear.refs_0_, f32[2,2,16,128]{3,2,1,0:T(8,128)S(1)} %get-tuple-element.35.refs_1_, f32[2,2,16,128]{3,2,1,0:T(8,128)S(1)} %get-tuple-element.36.refs_2_, ...), custom_call_target="tpu_custom_call" | custom-call | tf_op jit(solution)/shard_map/lay_routes/pallas_call | solution.py:636
  20.7 0.4 %enter_routes.1.routes_ref = bf16[2,8,144,128]{3,2,1,0:T(8,128)(2,1)S(1)} custom-call(bf16[2,7,144,128]{3,2,1,0:T(8,128)(2,1)S(1)} %lay_routes.1.routes_ref, bf16[2,144,128]{2,1,0:T(8,128)(2,1)S(1)} %collective-permute-done.2.other_ref.refs_0_), custom_call_target="tpu_custom_call" | custom-call | tf_op jit(solution)/shard_map/enter_routes/pallas_call | solution.py:652
  21.1 0.8 %collective-permute-done.3.base_ref = f32[2,1,128]{2,1,0:T(1,128)S(1)} collective-permute-done((f32[2,1,128]{2,1,0:T(1,128)S(1)}, f32[2,1,128]{2,1,0:T(1,128)S(1)}, u32[]{:S(2)}, u32[]{:S(2)}) %collective-permute-start.3) | collective-permute-done | bytes 1056 | tf_op jit(solution)/shard_map/ppermute | solution.py:26
  21.9 0.5 %run_steps.3 = f32[2,2,16,128]{3,2,1,0:T(8,128)S(1)} custom-call(f32[2,1,128]{2,1,0:T(1,128)S(1)} %get-tuple-element.25.start_ref, f32[2,1,128]{2,1,0:T(1,128)S(1)} %collective-permute-done.3.base_ref, bf16[2,8,144,128]{3,2,1,0:T(8,128)(2,1)S(1)} %enter_routes.1.routes_ref, bf16[2,2,16,128,128]{4,3,2,1,0:T(8,128)(2,1)S(1)} %get-tuple-element.31.near_linear.refs_0_, ...), custom_call_target="tpu_custom_call" | custom-call | tf_op jit(solution)/shard_map/run_steps/pallas_call | solution.py:664
  22.4 0.0 copy-start.2
  22.4 0.0 copy-start
  22.4 0.0 copy-start.1
  22.4 1.8 %collective-permute-start.4 = (f32[2,2,16,128]{3,2,1,0:T(8,128)S(1)}, f32[2,2,16,128]{3,2,1,0:T(8,128)S(1)}, u32[]{:S(2)}, u32[]{:S(2)}) collective-permute-start(f32[2,2,16,128]{3,2,1,0:T(8,128)S(1)} %run_steps.3), channel_id=1, source_target_pairs={{0,2},{2,0},{4,6},{6,4},{8,10},{10,8},{12,14},{14,12},{16,18},{18,... | collective-permute-start | bytes 98312 | tf_op jit(solution)/shard_map/ppermute | solution.py:26
  24.2 0.5 %run_steps.2.keep_ref = f32[2,2,16,128]{3,2,1,0:T(8,128)S(1)} custom-call(f32[2,1,128]{2,1,0:T(1,128)S(1)} %get-tuple-element.25.start_ref, f32[2,1,128]{2,1,0:T(1,128)S(1)} %collective-permute-done.3.base_ref, bf16[2,8,144,128]{3,2,1,0:T(8,128)(2,1)S(1)} %enter_routes.1.routes_ref, bf16[2,2,16,128,128]{4,3,2,1,0:T(8,128)(2,1)S(1)} %get-tuple-element.31.near_linear.refs_0_, ...), custom_call_target="tpu_custom_call" | custom-call | tf_op jit(solution)/shard_map/run_steps/pallas_call | solution.py:664
  24.7 1.6 %collective-permute-done.4.across_ref = f32[2,2,16,128]{3,2,1,0:T(8,128)S(1)} collective-permute-done((f32[2,2,16,128]{3,2,1,0:T(8,128)S(1)}, f32[2,2,16,128]{3,2,1,0:T(8,128)S(1)}, u32[]{:S(2)}, u32[]{:S(2)}) %collective-permute-start.4) | collective-permute-done | bytes 32800 | tf_op jit(solution)/shard_map/ppermute | solution.py:26
  26.4 1.8 %collective-permute-start.5 = (f32[2,2,16,128]{3,2,1,0:T(8,128)S(1)}, f32[2,2,16,128]{3,2,1,0:T(8,128)S(1)}, u32[]{:S(2)}, u32[]{:S(2)}) collective-permute-start(f32[2,2,16,128]{3,2,1,0:T(8,128)S(1)} %pad_maximum_fusion), channel_id=1, source_target_pairs={{0,4},{2,6},{4,0},{6,2},{8,12},{10,14},{12,8},{14,10},{16,20},{18,... | collective-permute-start | bytes 98312 | tf_op jit(solution)/shard_map/ppermute | solution.py:26
  28.1 2.2 %collective-permute-done.5.later_ref = f32[2,2,16,128]{3,2,1,0:T(8,128)S(1)} collective-permute-done((f32[2,2,16,128]{3,2,1,0:T(8,128)S(1)}, f32[2,2,16,128]{3,2,1,0:T(8,128)S(1)}, u32[]{:S(2)}, u32[]{:S(2)}) %collective-permute-start.5) | collective-permute-done | bytes 32800 | tf_op jit(solution)/shard_map/ppermute | solution.py:26
  30.3 0.0 copy-done.2
  30.3 0.1 scale_states.1
  30.4 0.1 collective-permute-start.6
  30.5 0.0 copy-done
  30.5 0.0 copy-done.1
  30.5 0.7 %read_own.1 = (f32[2,16,512]{2,1,0:T(8,128)}, f32[2,32,512]{2,1,0:T(8,128)S(1)}) custom-call(f32[2,16,512]{2,1,0:T(8,128)S(1)} %get-tuple-element.44.states_vmem, bf16[32,640]{1,0:T(8,128)(2,1)S(1)} %get-tuple-element.45.own_ref, bf16[1024,512]{1,0:T(8,128)(2,1)S(1)} %copy-done, bf16[1024,512]{1,0:T(8,128)(2,1)S(1)} %copy-done.1), custom_call_target="tpu_custom_call" | custom-call | tf_op jit(solution)/shard_map/read_own/pallas_call | solution.py:692
  31.2 0.5 %collective-permute-done.6.other_ref = bf16[32,640]{1,0:T(8,128)(2,1)S(1)} collective-permute-done((bf16[32,640]{1,0:T(8,128)(2,1)S(1)}, bf16[32,640]{1,0:T(8,128)(2,1)S(1)}, u32[]{:S(2)}, u32[]{:S(2)}) %collective-permute-start.6) | collective-permute-done | bytes 40992 | tf_op jit(solution)/shard_map/ppermute | solution.py:26
  31.7 0.9 %read_out.1 = bf16[32,512]{1,0:T(8,128)(2,1)} custom-call(bf16[32,640]{1,0:T(8,128)(2,1)S(1)} %get-tuple-element.45.own_ref, bf16[32,640]{1,0:T(8,128)(2,1)S(1)} %collective-permute-done.6.other_ref, f32[2,32,512]{2,1,0:T(8,128)S(1)} %get-tuple-element.47.sums_ref, bf16[1024,512]{1,0:T(8,128)(2,1)S(1)} %copy-done, bf16[1024,512]{1,0:T(8,128)(2,1)S(1)} %copy-done.1), custom_call_target="tpu_custom_call" | custom-call | tf_op jit(solution)/shard_map/read_out/pallas_call | solution.py:704
  (4 shorter events, 0.0 us)
Async XLA Ops:
  1.4 4.8 %collective-permute-start = (f32[17,16]{1,0:T(8,128)S(1)}, f32[17,16]{1,0:T(8,128)S(1)}, u32[]{:S(2)}, u32[]{:S(2)}) collective-permute-start(f32[17,16]{1,0:T(8,128)S(1)} %get-tuple-element.49), channel_id=1, source_target_pairs={{0,2},{2,0},{4,6},{6,4},{8,10},{10,8},{12,14},{14,12},{16,18},{18,... | collective-permute-start | bytes 3272 | tf_op jit(solution)/shard_map/ppermute | solution.py:26
  6.3 3.9 %collective-permute-start.1 = (f32[2,17,16]{2,1,0:T(8,128)S(1)}, f32[2,17,16]{2,1,0:T(8,128)S(1)}, u32[]{:S(2)}, u32[]{:S(2)}) collective-permute-start(f32[2,17,16]{2,1,0:T(8,128)S(1)} %pad_maximum_fusion.1.near_ref), channel_id=1, source_target_pairs={{0,4},{2,6},{4,0},{6,2},{8,12},{10,14},{12,8},{14,10},{16,20},{18,... | collective-permute-start | bytes 6536 | tf_op jit(solution)/shard_map/ppermute | solution.py:26
  12.7 4.4 %collective-permute-start.2 = (bf16[2,144,128]{2,1,0:T(8,128)(2,1)S(1)}, bf16[2,144,128]{2,1,0:T(8,128)(2,1)S(1)}, u32[]{:S(2)}, u32[]{:S(2)}) collective-permute-start(bf16[2,144,128]{2,1,0:T(8,128)(2,1)S(1)} %get-tuple-element.34.own_ref), channel_id=1, source_target_pairs={{0,8},{2,10},{4,12},{6,14},{8,0},{10,2},{12,4},{14,6},{16,24},{18,... | collective-permute-start | bytes 221192 | tf_op jit(solution)/shard_map/ppermute | solution.py:26
  17.4 4.5 %collective-permute-start.3 = (f32[2,1,128]{2,1,0:T(1,128)S(1)}, f32[2,1,128]{2,1,0:T(1,128)S(1)}, u32[]{:S(2)}, u32[]{:S(2)}) collective-permute-start(f32[2,1,128]{2,1,0:T(1,128)S(1)} %cross_pair.1), channel_id=1, source_target_pairs={{0,16},{2,18},{4,20},{6,22},{8,24},{10,26},{12,28},{14,30},{16,0},... | collective-permute-start | bytes 3080 | tf_op jit(solution)/shard_map/ppermute | solution.py:26
  22.4 7.9 %copy-start.2 = (f32[512]{0:T(512)S(1)}, f32[512]{0:T(512)}, u32[]{:S(2)}) copy-start(f32[512]{0:T(512)} %param.15) | copy-start | bytes 6148
  22.4 8.1 %copy-start = (bf16[1024,512]{1,0:T(8,128)(2,1)S(1)}, bf16[1024,512]{1,0:T(8,128)(2,1)}, u32[]{:S(2)}) copy-start(bf16[1024,512]{1,0:T(8,128)(2,1)} %value_ref.3) | copy-start | bytes 3145732
  22.4 8.1 %copy-start.1 = (bf16[1024,512]{1,0:T(8,128)(2,1)S(1)}, bf16[1024,512]{1,0:T(8,128)(2,1)}, u32[]{:S(2)}) copy-start(bf16[1024,512]{1,0:T(8,128)(2,1)} %gate_ref.3) | copy-start | bytes 3145732
  22.4 4.0 %collective-permute-start.4 = (f32[2,2,16,128]{3,2,1,0:T(8,128)S(1)}, f32[2,2,16,128]{3,2,1,0:T(8,128)S(1)}, u32[]{:S(2)}, u32[]{:S(2)}) collective-permute-start(f32[2,2,16,128]{3,2,1,0:T(8,128)S(1)} %run_steps.3), channel_id=1, source_target_pairs={{0,2},{2,0},{4,6},{6,4},{8,10},{10,8},{12,14},{14,12},{16,18},{18,... | collective-permute-start | bytes 98312 | tf_op jit(solution)/shard_map/ppermute | solution.py:26
  26.4 3.9 %collective-permute-start.5 = (f32[2,2,16,128]{3,2,1,0:T(8,128)S(1)}, f32[2,2,16,128]{3,2,1,0:T(8,128)S(1)}, u32[]{:S(2)}, u32[]{:S(2)}) collective-permute-start(f32[2,2,16,128]{3,2,1,0:T(8,128)S(1)} %pad_maximum_fusion), channel_id=1, source_target_pairs={{0,4},{2,6},{4,0},{6,2},{8,12},{10,14},{12,8},{14,10},{16,20},{18,... | collective-permute-start | bytes 98312 | tf_op jit(solution)/shard_map/ppermute | solution.py:26
  30.4 1.3 %collective-permute-start.6 = (bf16[32,640]{1,0:T(8,128)(2,1)S(1)}, bf16[32,640]{1,0:T(8,128)(2,1)S(1)}, u32[]{:S(2)}, u32[]{:S(2)}) collective-permute-start(bf16[32,640]{1,0:T(8,128)(2,1)S(1)} %get-tuple-element.45.own_ref), channel_id=1, source_target_pairs={{0,1},{1,0},{2,3},{3,2},{4,5},{5,4},{6,7},{7,6},{8,9},{9,8},{10,11... | collective-permute-start | bytes 122888 | tf_op jit(solution)/shard_map/ppermute | solution.py:26

commit v5 on v4

--- a/solution.py
+++ b/solution.py
@@ -121,14 +121,6 @@
     copies.append(pltpu.make_async_copy(initial_ref, initial_vmem, sems.at[chains + 2]))
     for copy in copies:
         copy.start()
-    for copy in copies[chains:]:
-        copy.wait()
-    for chain in range(chains):
-        lanes = pl.ds(pl.multiple_of((first_block + chain) * size, size), size)
-        decays_ref[chain] = decay_vmem[:, lanes]
-        inputs_ref[chain] = input_vmem[:, lanes]
-        initial = initial_vmem[:, lanes]
-        starts_ref[chain] = jnp.where(record == 0, initial[0:1], initial[1:2])
     for chain in range(chains):
         copies[chain].wait()
         for channel in range(0, channels, 2):
@@ -139,6 +131,14 @@
                 tiles_ref[chain, tile // 2, channel * 8 : channel * 8 + PAD, at : at + size] = rows.astype(
                     bf16
                 )
+    for copy in copies[chains:]:
+        copy.wait()
+    for chain in range(chains):
+        lanes = pl.ds(pl.multiple_of((first_block + chain) * size, size), size)
+        decays_ref[chain] = decay_vmem[:, lanes]
+        inputs_ref[chain] = input_vmem[:, lanes]
+        initial = initial_vmem[:, lanes]
+        starts_ref[chain] = jnp.where(record == 0, initial[0:1], initial[1:2])
 
 
 def form_steps(slots, decay_ref, input_ref, tiles_ref, maps_ref, fades_ref, drives_ref):

time: 32.9 us -> 32.8 us (level)
  transfers between devices with their start and end apart: 7 -> 7, of which waited for: 6 -> 5; matrix products, arithmetic and copies ran while one was open for 0% -> 0% of each run, Pallas kernels for 18% -> 18%
where the time goes in v5:
time: 32.8 us; the launch traced here: 32.6 us
  starting transfers between devices  13.4 us (41%)
  Pallas kernels  10.2 us (31%)
  waiting for transfers between devices  7.42 us (23%)
  between operations  0.78 us (2%)
  other arithmetic  0.74 us (2%)
    ppermute x7, starting transfers between devices, partner(): lax.ppermute(array, axis, [(i, i ^ flip) for i in range(lax.axis_size(axi...  13.4 us
    ppermute x7, waiting for transfers between devices, partner(): lax.ppermute(array, axis, [(i, i ^ flip) for i in range(lax.axis_size(axi...  7.42 us
    pallas_call x1, Pallas kernels, body(): pl.pallas_call(build_far, out_shape=pair_shapes + (packed_map,) * 5, in_s...  2.56 us
    pallas_call x1, Pallas kernels, body(): pl.pallas_call(build_near, out_shape=pair_shapes + panel_shapes, in_specs...  1.99 us
    pallas_call x1, Pallas kernels, body(): pl.pallas_call(stage_inputs, out_shape=(jax.ShapeDtypeStruct((chains, siz...  1.8 us
    pallas_call x2, Pallas kernels, run(): pl.pallas_call(functools.partial(run_steps, bits - 1, slot), out_shape=ja...  1.01 us
    pallas_call x1, Pallas kernels, body(): pl.pallas_call(read_out, out_shape=jax.ShapeDtypeStruct((rows, features),...  0.92 us
    concatenate x1, other arithmetic, body(): path = jnp.concatenate([increments, step_sizes[:, None, :]], axis=1)  0.73 us
  transfers between devices with their start and end apart: 7, of which 5 were waited for; matrix products, arithmetic and copies ran while one was open for 0% of the time, Pallas kernels for 18%

profile of v5, /device:TPU:0, one launch (start us, length us, event | category | flops | bytes accessed | tf_op | source)
XLA Modules:
  0.0 32.6 jit_solution(8339275133117741946)
XLA Ops:
  0.7 0.7 %fusion.2 = (f32[1,17,16]{2,1,0:T(8,128)S(1)}, f32[17,16]{1,0:T(8,128)S(1)}) fusion(s32[]{:T(128)S(6)} %select_n.20, f32[2,16,16]{2,1,0:T(8,128)} %param.12, f32[2,1,16]{2,1,0:T(1,128)} %bitcast.13, s32[]{:T(128)S(6)} %select_n.21), kind=kLoop, calls=%fused_computation.8 | loop fusion | flops 544 | bytes 4360 | tf_op jit(solution)/shard_map/concatenate | solution.py:553
  1.4 3.0 %collective-permute-start = (f32[17,16]{1,0:T(8,128)S(1)}, f32[17,16]{1,0:T(8,128)S(1)}, u32[]{:S(2)}, u32[]{:S(2)}) collective-permute-start(f32[17,16]{1,0:T(8,128)S(1)} %get-tuple-element.49), channel_id=1, source_target_pairs={{0,2},{2,0},{4,6},{6,4},{8,10},{10,8},{12,14},{14,12},{16,18},{18,... | collective-permute-start | bytes 3272 | tf_op jit(solution)/shard_map/ppermute | solution.py:26
  4.4 1.8 %stage_inputs.1 = (bf16[2,8,128,256]{3,2,1,0:T(8,128)(2,1)S(1)}, f32[2,1,128]{2,1,0:T(1,128)S(1)}, f32[2,16,128]{2,1,0:T(8,128)S(1)}, f32[2,1,128]{2,1,0:T(1,128)S(1)}) custom-call(f32[1,512]{1,0:T(1,128)} %bitcast.12, f32[16,512]{1,0:T(8,128)} %input_ref.1, f32[2,512]{1,0:T(2,128)} %initial_ref.1, f32[16,4,128,128]{3,2,1,0:T(8,128)} %coupling_ref.1), custom_call_target="tpu_custom_call" | custom-call | tf_op jit(solution)/shard_map/stage_inputs/pallas_call | solution.py:559
  6.2 0.0 collective-permute-done
  6.2 1.9 %collective-permute-start.1 = (f32[2,17,16]{2,1,0:T(8,128)S(1)}, f32[2,17,16]{2,1,0:T(8,128)S(1)}, u32[]{:S(2)}, u32[]{:S(2)}) collective-permute-start(f32[2,17,16]{2,1,0:T(8,128)S(1)} %pad_maximum_fusion.1.near_ref), channel_id=1, source_target_pairs={{0,4},{2,6},{4,0},{6,2},{8,12},{10,14},{12,8},{14,10},{16,20},{18,... | collective-permute-start | bytes 6536 | tf_op jit(solution)/shard_map/ppermute | solution.py:26
  8.1 2.0 %build_near.1 = (bf16[2,2,16,128,128]{4,3,2,1,0:T(8,128)(2,1)S(1)}, f32[2,2,16,128]{3,2,1,0:T(8,128)S(1)}, f32[2,2,16,128]{3,2,1,0:T(8,128)S(1)}, f32[2,2,2,144,...) custom-call(f32[2,17,16]{2,1,0:T(8,128)S(1)} %pad_maximum_fusion.1.near_ref, ...), custom_call_target="tpu_custom_call" | custom-call | tf_op jit(solution)/shard_map/build_near/pallas_call | solution.py:600
  10.1 0.0 collective-permute-done.1.far_ref
  10.1 2.6 %build_far.1 = (bf16[2,2,16,128,128]{4,3,2,1,0:T(8,128)(2,1)S(1)}, f32[2,2,16,128]{3,2,1,0:T(8,128)S(1)}, f32[2,2,16,128]{3,2,1,0:T(8,128)S(1)}, bf16[2,144,128]...) custom-call(f32[2,17,16]{2,1,0:T(8,128)S(1)} %collective-permute-don, ...), custom_call_target="tpu_custom_call" | custom-call | tf_op jit(solution)/shard_map/build_far/pallas_call | solution.py:611
  12.7 1.9 %collective-permute-start.2 = (bf16[2,144,128]{2,1,0:T(8,128)(2,1)S(1)}, bf16[2,144,128]{2,1,0:T(8,128)(2,1)S(1)}, u32[]{:S(2)}, u32[]{:S(2)}) collective-permute-start(bf16[2,144,128]{2,1,0:T(8,128)(2,1)S(1)} %get-tuple-element.34.own_ref), channel_id=1, source_target_pairs={{0,8},{2,10},{4,12},{6,14},{8,0},{10,2},{12,4},{14,6},{16,24},{18,... | collective-permute-start | bytes 221192 | tf_op jit(solution)/shard_map/ppermute | solution.py:26
  14.6 2.5 %collective-permute-done.2.other_ref.refs_0_ = bf16[2,144,128]{2,1,0:T(8,128)(2,1)S(1)} collective-permute-done((bf16[2,144,128]{2,1,0:T(8,128)(2,1)S(1)}, bf16[2,144,128]{2,1,0:T(8,128)(2,1)S(1)}, u32[]{:S(2)}, u32[]{:S(2)}) %collective-permute-start.2) | collective-permute-done | bytes 73760 | tf_op jit(solution)/shard_map/ppermute | solution.py:26
  17.1 0.3 cross_pair.1
  17.3 2.9 %collective-permute-start.3 = (f32[2,1,128]{2,1,0:T(1,128)S(1)}, f32[2,1,128]{2,1,0:T(1,128)S(1)}, u32[]{:S(2)}, u32[]{:S(2)}) collective-permute-start(f32[2,1,128]{2,1,0:T(1,128)S(1)} %cross_pair.1), channel_id=1, source_target_pairs={{0,16},{2,18},{4,20},{6,22},{8,24},{10,26},{12,28},{14,30},{16,0},... | collective-permute-start | bytes 3080 | tf_op jit(solution)/shard_map/ppermute | solution.py:26
  20.2 0.4 %lay_routes.1.routes_ref = bf16[2,7,144,128]{3,2,1,0:T(8,128)(2,1)S(1)} custom-call(bf16[2,2,16,128,128]{4,3,2,1,0:T(8,128)(2,1)S(1)} %get-tuple-element.31.near_linear.refs_0_, f32[2,2,16,128]{3,2,1,0:T(8,128)S(1)} %get-tuple-element.35.refs_1_, f32[2,2,16,128]{3,2,1,0:T(8,128)S(1)} %get-tuple-element.36.refs_2_, ...), custom_call_target="tpu_custom_call" | custom-call | tf_op jit(solution)/shard_map/lay_routes/pallas_call | solution.py:636
  20.7 0.4 %enter_routes.1.routes_ref = bf16[2,8,144,128]{3,2,1,0:T(8,128)(2,1)S(1)} custom-call(bf16[2,7,144,128]{3,2,1,0:T(8,128)(2,1)S(1)} %lay_routes.1.routes_ref, bf16[2,144,128]{2,1,0:T(8,128)(2,1)S(1)} %collective-permute-done.2.other_ref.refs_0_), custom_call_target="tpu_custom_call" | custom-call | tf_op jit(solution)/shard_map/enter_routes/pallas_call | solution.py:652
  21.1 0.7 %collective-permute-done.3.base_ref = f32[2,1,128]{2,1,0:T(1,128)S(1)} collective-permute-done((f32[2,1,128]{2,1,0:T(1,128)S(1)}, f32[2,1,128]{2,1,0:T(1,128)S(1)}, u32[]{:S(2)}, u32[]{:S(2)}) %collective-permute-start.3) | collective-permute-done | bytes 1056 | tf_op jit(solution)/shard_map/ppermute | solution.py:26
  21.8 0.5 %run_steps.3 = f32[2,2,16,128]{3,2,1,0:T(8,128)S(1)} custom-call(f32[2,1,128]{2,1,0:T(1,128)S(1)} %get-tuple-element.25.start_ref, f32[2,1,128]{2,1,0:T(1,128)S(1)} %collective-permute-done.3.base_ref, bf16[2,8,144,128]{3,2,1,0:T(8,128)(2,1)S(1)} %enter_routes.1.routes_ref, bf16[2,2,16,128,128]{4,3,2,1,0:T(8,128)(2,1)S(1)} %get-tuple-element.31.near_linear.refs_0_, ...), custom_call_target="tpu_custom_call" | custom-call | tf_op jit(solution)/shard_map/run_steps/pallas_call | solution.py:664
  22.3 0.0 copy-start.2
  22.3 0.0 copy-start
  22.3 0.0 copy-start.1
  22.4 1.9 %collective-permute-start.4 = (f32[2,2,16,128]{3,2,1,0:T(8,128)S(1)}, f32[2,2,16,128]{3,2,1,0:T(8,128)S(1)}, u32[]{:S(2)}, u32[]{:S(2)}) collective-permute-start(f32[2,2,16,128]{3,2,1,0:T(8,128)S(1)} %run_steps.3), channel_id=1, source_target_pairs={{0,2},{2,0},{4,6},{6,4},{8,10},{10,8},{12,14},{14,12},{16,18},{18,... | collective-permute-start | bytes 98312 | tf_op jit(solution)/shard_map/ppermute | solution.py:26
  24.2 0.5 %run_steps.2.keep_ref = f32[2,2,16,128]{3,2,1,0:T(8,128)S(1)} custom-call(f32[2,1,128]{2,1,0:T(1,128)S(1)} %get-tuple-element.25.start_ref, f32[2,1,128]{2,1,0:T(1,128)S(1)} %collective-permute-done.3.base_ref, bf16[2,8,144,128]{3,2,1,0:T(8,128)(2,1)S(1)} %enter_routes.1.routes_ref, bf16[2,2,16,128,128]{4,3,2,1,0:T(8,128)(2,1)S(1)} %get-tuple-element.31.near_linear.refs_0_, ...), custom_call_target="tpu_custom_call" | custom-call | tf_op jit(solution)/shard_map/run_steps/pallas_call | solution.py:664
  24.7 1.6 %collective-permute-done.4.across_ref = f32[2,2,16,128]{3,2,1,0:T(8,128)S(1)} collective-permute-done((f32[2,2,16,128]{3,2,1,0:T(8,128)S(1)}, f32[2,2,16,128]{3,2,1,0:T(8,128)S(1)}, u32[]{:S(2)}, u32[]{:S(2)}) %collective-permute-start.4) | collective-permute-done | bytes 32800 | tf_op jit(solution)/shard_map/ppermute | solution.py:26
  26.3 1.8 %collective-permute-start.5 = (f32[2,2,16,128]{3,2,1,0:T(8,128)S(1)}, f32[2,2,16,128]{3,2,1,0:T(8,128)S(1)}, u32[]{:S(2)}, u32[]{:S(2)}) collective-permute-start(f32[2,2,16,128]{3,2,1,0:T(8,128)S(1)} %pad_maximum_fusion), channel_id=1, source_target_pairs={{0,4},{2,6},{4,0},{6,2},{8,12},{10,14},{12,8},{14,10},{16,20},{18,... | collective-permute-start | bytes 98312 | tf_op jit(solution)/shard_map/ppermute | solution.py:26
  28.1 2.1 %collective-permute-done.5.later_ref = f32[2,2,16,128]{3,2,1,0:T(8,128)S(1)} collective-permute-done((f32[2,2,16,128]{3,2,1,0:T(8,128)S(1)}, f32[2,2,16,128]{3,2,1,0:T(8,128)S(1)}, u32[]{:S(2)}, u32[]{:S(2)}) %collective-permute-start.5) | collective-permute-done | bytes 32800 | tf_op jit(solution)/shard_map/ppermute | solution.py:26
  30.3 0.0 copy-done.2
  30.3 0.1 scale_states.1
  30.4 0.1 collective-permute-start.6
  30.5 0.0 copy-done
  30.5 0.0 copy-done.1
  30.5 0.7 %read_own.1 = (f32[2,16,512]{2,1,0:T(8,128)}, f32[2,32,512]{2,1,0:T(8,128)S(1)}) custom-call(f32[2,16,512]{2,1,0:T(8,128)S(1)} %get-tuple-element.44.states_vmem, bf16[32,640]{1,0:T(8,128)(2,1)S(1)} %get-tuple-element.45.own_ref, bf16[1024,512]{1,0:T(8,128)(2,1)S(1)} %copy-done, bf16[1024,512]{1,0:T(8,128)(2,1)S(1)} %copy-done.1), custom_call_target="tpu_custom_call" | custom-call | tf_op jit(solution)/shard_map/read_own/pallas_call | solution.py:692
  31.1 0.5 %collective-permute-done.6.other_ref = bf16[32,640]{1,0:T(8,128)(2,1)S(1)} collective-permute-done((bf16[32,640]{1,0:T(8,128)(2,1)S(1)}, bf16[32,640]{1,0:T(8,128)(2,1)S(1)}, u32[]{:S(2)}, u32[]{:S(2)}) %collective-permute-start.6) | collective-permute-done | bytes 40992 | tf_op jit(solution)/shard_map/ppermute | solution.py:26
  31.7 0.9 %read_out.1 = bf16[32,512]{1,0:T(8,128)(2,1)} custom-call(bf16[32,640]{1,0:T(8,128)(2,1)S(1)} %get-tuple-element.45.own_ref, bf16[32,640]{1,0:T(8,128)(2,1)S(1)} %collective-permute-done.6.other_ref, f32[2,32,512]{2,1,0:T(8,128)S(1)} %get-tuple-element.47.sums_ref, bf16[1024,512]{1,0:T(8,128)(2,1)S(1)} %copy-done, bf16[1024,512]{1,0:T(8,128)(2,1)S(1)} %copy-done.1), custom_call_target="tpu_custom_call" | custom-call | tf_op jit(solution)/shard_map/read_out/pallas_call | solution.py:704
  (4 shorter events, 0.0 us)
Async XLA Ops:
  1.4 4.8 %collective-permute-start = (f32[17,16]{1,0:T(8,128)S(1)}, f32[17,16]{1,0:T(8,128)S(1)}, u32[]{:S(2)}, u32[]{:S(2)}) collective-permute-start(f32[17,16]{1,0:T(8,128)S(1)} %get-tuple-element.49), channel_id=1, source_target_pairs={{0,2},{2,0},{4,6},{6,4},{8,10},{10,8},{12,14},{14,12},{16,18},{18,... | collective-permute-start | bytes 3272 | tf_op jit(solution)/shard_map/ppermute | solution.py:26
  6.2 3.9 %collective-permute-start.1 = (f32[2,17,16]{2,1,0:T(8,128)S(1)}, f32[2,17,16]{2,1,0:T(8,128)S(1)}, u32[]{:S(2)}, u32[]{:S(2)}) collective-permute-start(f32[2,17,16]{2,1,0:T(8,128)S(1)} %pad_maximum_fusion.1.near_ref), channel_id=1, source_target_pairs={{0,4},{2,6},{4,0},{6,2},{8,12},{10,14},{12,8},{14,10},{16,20},{18,... | collective-permute-start | bytes 6536 | tf_op jit(solution)/shard_map/ppermute | solution.py:26
  12.7 4.4 %collective-permute-start.2 = (bf16[2,144,128]{2,1,0:T(8,128)(2,1)S(1)}, bf16[2,144,128]{2,1,0:T(8,128)(2,1)S(1)}, u32[]{:S(2)}, u32[]{:S(2)}) collective-permute-start(bf16[2,144,128]{2,1,0:T(8,128)(2,1)S(1)} %get-tuple-element.34.own_ref), channel_id=1, source_target_pairs={{0,8},{2,10},{4,12},{6,14},{8,0},{10,2},{12,4},{14,6},{16,24},{18,... | collective-permute-start | bytes 221192 | tf_op jit(solution)/shard_map/ppermute | solution.py:26
  17.3 4.5 %collective-permute-start.3 = (f32[2,1,128]{2,1,0:T(1,128)S(1)}, f32[2,1,128]{2,1,0:T(1,128)S(1)}, u32[]{:S(2)}, u32[]{:S(2)}) collective-permute-start(f32[2,1,128]{2,1,0:T(1,128)S(1)} %cross_pair.1), channel_id=1, source_target_pairs={{0,16},{2,18},{4,20},{6,22},{8,24},{10,26},{12,28},{14,30},{16,0},... | collective-permute-start | bytes 3080 | tf_op jit(solution)/shard_map/ppermute | solution.py:26
  22.3 7.9 %copy-start.2 = (f32[512]{0:T(512)S(1)}, f32[512]{0:T(512)}, u32[]{:S(2)}) copy-start(f32[512]{0:T(512)} %param.15) | copy-start | bytes 6148
  22.3 8.1 %copy-start = (bf16[1024,512]{1,0:T(8,128)(2,1)S(1)}, bf16[1024,512]{1,0:T(8,128)(2,1)}, u32[]{:S(2)}) copy-start(bf16[1024,512]{1,0:T(8,128)(2,1)} %value_ref.3) | copy-start | bytes 3145732
  22.3 8.1 %copy-start.1 = (bf16[1024,512]{1,0:T(8,128)(2,1)S(1)}, bf16[1024,512]{1,0:T(8,128)(2,1)}, u32[]{:S(2)}) copy-start(bf16[1024,512]{1,0:T(8,128)(2,1)} %gate_ref.3) | copy-start | bytes 3145732
  22.4 4.0 %collective-permute-start.4 = (f32[2,2,16,128]{3,2,1,0:T(8,128)S(1)}, f32[2,2,16,128]{3,2,1,0:T(8,128)S(1)}, u32[]{:S(2)}, u32[]{:S(2)}) collective-permute-start(f32[2,2,16,128]{3,2,1,0:T(8,128)S(1)} %run_steps.3), channel_id=1, source_target_pairs={{0,2},{2,0},{4,6},{6,4},{8,10},{10,8},{12,14},{14,12},{16,18},{18,... | collective-permute-start | bytes 98312 | tf_op jit(solution)/shard_map/ppermute | solution.py:26
  26.3 3.9 %collective-permute-start.5 = (f32[2,2,16,128]{3,2,1,0:T(8,128)S(1)}, f32[2,2,16,128]{3,2,1,0:T(8,128)S(1)}, u32[]{:S(2)}, u32[]{:S(2)}) collective-permute-start(f32[2,2,16,128]{3,2,1,0:T(8,128)S(1)} %pad_maximum_fusion), channel_id=1, source_target_pairs={{0,4},{2,6},{4,0},{6,2},{8,12},{10,14},{12,8},{14,10},{16,20},{18,... | collective-permute-start | bytes 98312 | tf_op jit(solution)/shard_map/ppermute | solution.py:26
  30.4 1.3 %collective-permute-start.6 = (bf16[32,640]{1,0:T(8,128)(2,1)S(1)}, bf16[32,640]{1,0:T(8,128)(2,1)S(1)}, u32[]{:S(2)}, u32[]{:S(2)}) collective-permute-start(bf16[32,640]{1,0:T(8,128)(2,1)S(1)} %get-tuple-element.45.own_ref), channel_id=1, source_target_pairs={{0,1},{1,0},{2,3},{3,2},{4,5},{5,4},{6,7},{7,6},{8,9},{9,8},{10,11... | collective-permute-start | bytes 122888 | tf_op jit(solution)/shard_map/ppermute | solution.py:26
